TPU v7x, 32 devices: a whole 2x2x4 slice. The times are simulated.
32 devices in a mesh: row: 8 (over y, x, core), col: 4 (over z).
Axes of the slice: x: 2, y: 2, z: 4, core: 2. Of those that a mesh axis runs over, the one named last changes fastest.
Arguments:
- grid_obs: float32 [32, 2048, 512], P(None, 'row', 'col'), may hold values from -6 to 6
- grid_noise: float32 [2048, 512], P('row', 'col'), may hold values from 0.25 to 2
- station_obs: float32 [32, 8, 4, 1024], P(None, 'row', 'col'), may hold values from -6 to 6
- station_noise: float32 [8, 4, 1024], P('row', 'col'), may hold values from 0.25 to 2
- station_offset: float32 [2, 8, 4, 1024], P(None, 'row', 'col'), may hold values from 0 to 1
- station_cell: int32 [8, 4, 1024], P('row', 'col'), may hold values from 0 to 32638, as said below
- station_count: int32 [8, 4], P('row', 'col'), may hold values from 128 to 1024, as said below
- time_cov: float32 [32, 32], replicated, as said below
Outputs:
- solution_grid: float32 [32, 2048, 512], P(None, 'row', 'col')
- solution_stations: float32 [32, 8, 4, 1024], P(None, 'row', 'col')
- residual_grid: float32 [32, 2048, 512], P(None, 'row', 'col')
Inputs may be any that keep to these rules, and one draw needn't show every extreme that they name: `station_cell`: cell r * 128 + c with r < 255 and c < 127, so the footprint lies in the station's tile. `station_count`: each tile holds 1024, 512, 256 or 128 stations. `time_cov`: symmetric; each diagonal entry exceeds the sum of the magnitudes of the other entries of its row.
All inputs are finite; a program needn't handle non-finite values.
Results may differ from a plain program's by a relative error of at most 0.00019.
Values sent between devices are 32-bit elements; how exact they have to be, the bound alone decides.
No kernel may reach another device: no remote copies, remote signals or barrier semaphores. Data moves between devices by JAX's collectives and lax.ppermute only.
A program may use at most 128 MiB of HBM per device.

v0:
```python
import jax
import jax.numpy as jnp
from jax import lax
from jax.sharding import PartitionSpec as P

REACH = 8
ITERS = 2


highest_precision = lax.Precision.HIGHEST


def extended(block, sides, width):
    for axis, dim in sides:
        count = lax.axis_size(axis)
        forward = [(i, i + 1) for i in range(count - 1)]
        backward = [(target, source) for source, target in forward]
        low = lax.ppermute(
            lax.slice_in_dim(block, block.shape[dim] - width, None, axis=dim), axis, forward
        )
        high = lax.ppermute(lax.slice_in_dim(block, 0, width, axis=dim), axis, backward)
        block = jnp.concatenate([low, block, high], axis=dim)
    return block


def banded(count, reach):
    shape = (count + 2 * reach, count)
    offset = (
        lax.broadcasted_iota(jnp.int32, shape, 0)
        - reach
        - lax.broadcasted_iota(jnp.int32, shape, 1)
    )
    spread = jnp.abs(offset).astype(jnp.float32)
    value = (1.0 - spread / (reach + 1)) * jnp.exp(-spread / 3.0)
    return jnp.where(jnp.abs(offset) <= reach, value, 0.0)


def inner(first, second):
    return jnp.sum(first[0] * second[0]) + jnp.sum(first[1] * second[1])


def combine(scale, first, second):
    return (first[0] + scale * second[0], first[1] + scale * second[1])


def squares(residual_vector):
    return lax.psum(inner(residual_vector, residual_vector), ("row", "col"))


def body(
    grid_obs,
    grid_noise,
    station_obs,
    station_noise,
    station_offset,
    station_cell,
    station_count,
    time_cov,
):
    steps, rows, cols = grid_obs.shape
    slots = station_obs.shape[3]
    taper_band_rows = banded(rows, REACH)
    band_cols = banded(cols, REACH)
    base = station_cell.reshape(slots)
    shifts = jnp.array([0, cols, 1, cols + 1], jnp.int32)
    station_indices = (shifts[:, None] + base[None, :]).reshape(4 * slots)
    offsets = station_offset.reshape(2, slots)
    along_row = offsets[0]
    along_col = offsets[1]
    footprint = jnp.stack(
        [
            (1.0 - along_row) * (1.0 - along_col),
            along_row * (1.0 - along_col),
            (1.0 - along_row) * along_col,
            along_row * along_col,
        ]
    )
    live = (jnp.arange(slots, dtype=jnp.int32) < station_count.reshape(())).astype(jnp.float32)[
        None, :
    ]
    noise_grid = grid_noise[None]
    noise_site = station_noise.reshape(1, slots)
    residual_vector = (grid_obs, live * station_obs.reshape(steps, slots))
    solution = (jnp.zeros_like(grid_obs), jnp.zeros((steps, slots), jnp.float32))
    direction = residual_vector
    norm_now = squares(residual_vector)
    for iteration in range(ITERS):
        grid_part, site_part = direction
        scattered = (footprint[None] * (live * site_part)[:, None]).reshape(steps, 4 * slots)
        merged = (
            grid_part.reshape(steps, rows * cols)
            .at[:, station_indices]
            .add(scattered)
            .reshape(steps, rows, cols)
        )
        operate_temporal_shift = jnp.einsum(
            "st,tij->sij", time_cov, merged, precision=highest_precision
        )
        widened_tiles = extended(operate_temporal_shift, (("row", 1),), REACH)
        row_sweep = jnp.einsum(
            "fbm,bv->fvm", widened_tiles, taper_band_rows, precision=highest_precision
        )
        broader = extended(row_sweep, (("col", 2),), REACH)
        smooth = jnp.einsum("tia,aj->tij", broader, band_cols, precision=highest_precision)
        picked = smooth.reshape(steps, rows * cols)[:, station_indices].reshape(steps, 4, slots)
        sampled = jnp.sum(footprint[None] * picked, axis=1)
        grid_out = 0.25 * smooth + noise_grid * grid_part
        site_out = live * (0.25 * sampled + noise_site * site_part) + (1.0 - live) * site_part
        image = (grid_out, site_out)
        alpha = norm_now / lax.psum(inner(direction, image), ("row", "col"))
        solution = combine(alpha, solution, direction)
        residual_vector = combine(-alpha, residual_vector, image)
        if iteration + 1 < ITERS:
            norm_next = squares(residual_vector)
            direction = combine(norm_next / norm_now, residual_vector, direction)
            norm_now = norm_next
    return (solution[0], solution[1].reshape(steps, 1, 1, slots), residual_vector[0])


def solution(mesh):
    placed = (
        P(None, "row", "col"),
        P("row", "col"),
        P(None, "row", "col", None),
        P("row", "col", None),
        P(None, "row", "col", None),
        P("row", "col", None),
        P("row", "col"),
        P(),
    )
    return jax.shard_map(
        body,
        mesh=mesh,
        in_specs=placed,
        out_specs=(P(None, "row", "col"), P(None, "row", "col", None), P(None, "row", "col")),
        check_vma=False,
    )
```

profile of v0, /device:TPU:0, one launch (start us, length us, event | category | flops | bytes accessed | tf_op | source)
XLA Modules:
  0.0 445.8 jit_solution(3582918658931796456)
XLA Ops:
  1.3 0.8 add_bitcast_fusion
  2.1 0.7 fusion.67
  2.9 0.9 fusion.51
  3.8 0.2 copy.34
  4.0 10.6 %copy.33 = f32[32,256,128]{0,2,1:T(8,128)} copy(f32[32,256,128]{2,1,0:T(8,128)} %param.9) | data formatting | bytes 8388608 | tf_op args[0]
  14.6 0.6 bitcast_multiply_fusion.1
  15.2 31.6 %scatter_custom_fusion = f32[32,32768]{0,1:T(8,128)} fusion(f32[32,32768]{0,1:T(8,128)} %bitcast.117, s32[4096]{0:T(1024)S(1)} %bitcast.132, f32[32,4096]{0,1:T(8,128)S(1)} %bitcast_multiply_fusion.1), kind=kCustom, calls=%fused_computation.39 | custom fusion | flops 131072 | bytes 6291456 | tf_op jit(solution)/shard_map/scatter-add | solution.py:93
  46.9 21.0 %convolution_bitcast_fusion.1 = f32[32,256,128]{2,0,1:T(8,128)S(1)} fusion(f32[32,256,128]{0,2,1:T(8,128)} %bitcast.118, f32[32,32]{1,0:T(8,128)S(1)} %copy-done), kind=kOutput, calls=%fused_computation.35 | convolution fusion | flops 402653184 | bytes 8392704 | tf_op jit(solution)/shard_map/st,tij->sij/dot_general | solution.py:96
  67.9 2.4 collective-permute-start
  70.3 1.5 collective-permute-start.1
  71.9 3.8 collective-permute-done.1
  75.7 0.5 pad_maximum_fusion
  76.2 12.2 %fusion.16 = f32[32,256,128]{1,2,0:T(8,128)S(1)} fusion(f32[32,272,128]{2,0,1:T(8,128)S(1)} %pad_maximum_fusion, s32[272]{0:T(512)S(1)} %iota_add_fusion), kind=kOutput, calls=%fused_computation.32 | convolution fusion | flops 3423248384 | bytes 8651840 | tf_op jit(solution)/shard_map/fbm,bv->fvm/dot_general | solution.py:100
  88.4 3.5 collective-permute-start.2
  91.9 1.3 collective-permute-start.3
  93.2 2.8 collective-permute-done.2
  96.0 4.7 %collective-permute-done.3 = f32[32,256,8]{1,2,0:T(8,128)S(1)} collective-permute-done((f32[32,256,8]{1,2,0:T(8,128)S(1)}, f32[32,256,8]{1,2,0:T(8,128)S(1)}, u32[]{:S(2)}, u32[]{:S(2)}) %collective-permute-start.3) | collective-permute-done | bytes 262176 | tf_op jit(solution)/shard_map/ppermute | solution.py:21
  100.7 16.0 %multiply_reduce_fusion.2 = (f32[]{:T(128)}, f32[]{:T(128)}, f32[32,256,128]{2,1,0:T(8,128)}) fusion(f32[32,256,128]{2,1,0:T(8,128)S(1)} %copy-done.1, f32[256,128]{1,0:T(8,128)S(1)} %copy-done.4, s32[144]{0:T(256)S(1)} %iota_add_fusion.1, f32[32,256,8]{1,2,0:T(8,128)S(1)} %collective-permute-done.3, f32[32,256,128]{1,2,0:T(8,128)S(1)} %fusion.16, ...), kind=kOutput, calls=%fused_computation.29 | convolution fusion | flops 1821822976 | bytes 13238856 | tf_op jit(solution)/shard_map/tia,aj->tij/dot_general | solution.py:104
  116.7 10.6 %copy.49 = f32[32,256,128]{0,2,1:T(8,128)} copy(f32[32,256,128]{2,1,0:T(8,128)} %get-tuple-element.31) | data formatting | bytes 8388608 | tf_op jit(solution)/shard_map/reshape | solution.py:105
  127.3 16.6 %gather_fusion = f32[4096,32]{1,0:T(8,128)S(1)} fusion(f32[32,32768]{0,1:T(8,128)} %bitcast.122, s32[4096]{0:T(1024)S(1)} %broadcast_clamp_fusion), kind=kCustom, calls=%fused_computation | custom fusion | bytes 1064960 | tf_op jit(solution)/shard_map/gather | solution.py:105
  143.9 0.7 multiply_reduce_fusion.5
  144.8 0.7 multiply_reduce_fusion.8
  148.1 43.6 %all-reduce = (f32[]{:T(128)}, f32[]{:T(128)}) all-reduce(f32[]{:T(128)S(6)} %add.135, f32[]{:T(128)S(6)} %add.145), channel_id=1, replica_groups=mesh['row'=8,'col'=4] {'row','col'}, use_global_device_ids=true, to_apply=%region_2.3 | all-reduce | flops 2 | bytes 16 | tf_op jit(solution)/shard_map/psum | solution.py:47
  193.1 0.7 multiply_reduce_fusion.7
  193.8 5.2 %multiply_reduce_fusion.1 = f32[]{:T(128)} fusion(f32[32,256,128]{2,1,0:T(8,128)} %param.9, f32[256,128]{1,0:T(8,128)S(1)} %copy-done.4, f32[32,256,128]{2,1,0:T(8,128)} %get-tuple-element.31, f32[]{:T(128)S(6)} %neg.18), kind=kLoop, calls=%fused_computation.27 | loop fusion | flops 7340031 | bytes 8519688 | tf_op jit(solution)/shard_map/reduce_sum | solution.py:39
  200.3 40.5 %psum.30 = f32[]{:T(128)} all-reduce(f32[]{:T(128)S(6)} %add.148), channel_id=1, replica_groups=mesh['row'=8,'col'=4] {'row','col'}, use_global_device_ids=true, to_apply=%region_10.11 | all-reduce | flops 1 | bytes 8 | tf_op jit(solution)/shard_map/psum | solution.py:47
  242.2 6.7 %multiply_add_fusion.3 = f32[32,256,128]{2,1,0:T(8,128)} fusion(f32[32,256,128]{2,1,0:T(8,128)} %param.9, f32[]{:T(128)S(6)} %div.50, f32[256,128]{1,0:T(8,128)S(1)} %copy-done.4, f32[32,256,128]{2,1,0:T(8,128)} %get-tuple-element.31, f32[]{:T(128)S(6)} %neg.18), kind=kLoop, calls=%fused_computation.26 | loop fusion | flops 7340032 | bytes 12713992 | tf_op jit(solution)/shard_map/add | solution.py:43
  249.1 0.6 bitcast_multiply_fusion
  249.7 10.6 %copy.50 = f32[32,256,128]{0,2,1:T(8,128)} copy(f32[32,256,128]{2,1,0:T(8,128)} %multiply_add_fusion.3) | data formatting | bytes 8388608 | tf_op jit(solution)/shard_map/reshape | solution.py:91
  260.3 31.6 %scatter_custom_fusion.1 = f32[32,32768]{0,1:T(8,128)} fusion(f32[32,32768]{0,1:T(8,128)} %bitcast.119, s32[4096]{0:T(1024)S(1)} %bitcast.134, f32[32,4096]{0,1:T(8,128)S(1)} %bitcast_multiply_fusion), kind=kCustom, calls=%fused_computation.36 | custom fusion | flops 131072 | bytes 6291456 | tf_op jit(solution)/shard_map/scatter-add | solution.py:93
  291.9 21.0 %convolution_bitcast_fusion = f32[32,256,128]{2,0,1:T(8,128)S(1)} fusion(f32[32,256,128]{0,2,1:T(8,128)} %bitcast.120, f32[32,32]{1,0:T(8,128)S(1)} %copy-done), kind=kOutput, calls=%fused_computation.34 | convolution fusion | flops 402653184 | bytes 8392704 | tf_op jit(solution)/shard_map/st,tij->sij/dot_general | solution.py:96
  313.0 1.3 collective-permute-start.4
  314.3 1.5 collective-permute-start.5
  315.8 4.2 collective-permute-done.5
  320.0 0.5 pad_maximum_fusion.1
  320.5 12.0 %fusion.19 = f32[32,256,128]{1,2,0:T(8,128)S(1)} fusion(f32[32,272,128]{2,0,1:T(8,128)S(1)} %pad_maximum_fusion.1, s32[272]{0:T(512)S(1)} %iota_add_fusion), kind=kOutput, calls=%fused_computation.33 | convolution fusion | flops 3423248384 | bytes 8651840 | tf_op jit(solution)/shard_map/fbm,bv->fvm/dot_general | solution.py:100
  332.6 3.7 collective-permute-start.6
  336.3 1.3 collective-permute-start.7
  337.6 2.8 collective-permute-done.6
  340.4 4.7 %collective-permute-done.7 = f32[32,256,8]{1,2,0:T(8,128)S(1)} collective-permute-done((f32[32,256,8]{1,2,0:T(8,128)S(1)}, f32[32,256,8]{1,2,0:T(8,128)S(1)}, u32[]{:S(2)}, u32[]{:S(2)}) %collective-permute-start.7) | collective-permute-done | bytes 262176 | tf_op jit(solution)/shard_map/ppermute | solution.py:21
  345.1 16.1 %multiply_reduce_fusion = (f32[]{:T(128)}, f32[32,256,128]{2,1,0:T(8,128)}) fusion(f32[32,256,128]{2,1,0:T(8,128)S(1)} %copy-done.2, f32[256,128]{1,0:T(8,128)S(1)} %copy-done.4, s32[144]{0:T(256)S(1)} %iota_add_fusion.1, f32[32,256,8]{1,2,0:T(8,128)S(1)} %collective-permute-done.7, f32[32,256,128]{1,2,0:T(8,128)S(1)} %fusion.19, ...), kind=kOutput, calls=%fused_computation.24 | convolution fusion | flops 1819725824 | bytes 13238852 | tf_op jit(solution)/shard_map/tia,aj->tij/dot_general | solution.py:104
  361.2 10.6 %copy.51 = f32[32,256,128]{0,2,1:T(8,128)} copy(f32[32,256,128]{2,1,0:T(8,128)} %get-tuple-element.33) | data formatting | bytes 8388608 | tf_op jit(solution)/shard_map/reshape | solution.py:105
  371.8 16.5 %gather_fusion.1 = f32[4096,32]{1,0:T(8,128)S(1)} fusion(f32[32,32768]{0,1:T(8,128)} %bitcast.121, s32[4096]{0:T(1024)S(1)} %broadcast_clamp_fusion), kind=kCustom, calls=%fused_computation.1 | custom fusion | bytes 1064960 | tf_op jit(solution)/shard_map/gather | solution.py:105
  388.3 0.7 multiply_reduce_fusion.4
  389.2 0.8 multiply_reduce_fusion.6
  391.3 42.5 %psum.31 = f32[]{:T(128)} all-reduce(f32[]{:T(128)S(6)} %add.154), channel_id=1, replica_groups=mesh['row'=8,'col'=4] {'row','col'}, use_global_device_ids=true, to_apply=%region_15.16 | all-reduce | flops 1 | bytes 8 | tf_op jit(solution)/shard_map/psum | solution.py:110
  435.2 9.3 %multiply_add_fusion = (f32[32,256,128]{2,1,0:T(8,128)}, f32[32,256,128]{2,1,0:T(8,128)}) fusion(f32[32,256,128]{2,1,0:T(8,128)} %multiply_add_fusion.3, f32[32,256,128]{2,1,0:T(8,128)} %get-tuple-element.33, f32[]{:T(128)S(6)} %neg.19, f32[256,128]{1,0:T(8,128)S(1)} %copy-done.4, f32[32,256,128]{2,1,0:T(8,128)} %param.9, ...), kind=kLoop, calls=%fused_computation.22 | loop fusion | flops 13631488 | bytes 25296912 | tf_op jit(solution)/shard_map/add | solution.py:43
  444.5 0.8 copy.46
  (32 shorter events, 0.9 us)
Async XLA Ops:
  0.6 46.2 %copy-start = (f32[32,32]{1,0:T(8,128)S(1)}, f32[32,32]{1,0:T(8,128)}, u32[]{:S(2)}) copy-start(f32[32,32]{1,0:T(8,128)} %param.16) | copy-start | bytes 12292
  67.9 4.0 collective-permute-start
  70.3 5.3 %collective-permute-start.1 = (f32[32,8,128]{2,0,1:T(8,128)S(1)}, f32[32,8,128]{2,0,1:T(8,128)S(1)}, u32[]{:S(2)}, u32[]{:S(2)}) collective-permute-start(f32[32,8,128]{2,0,1:T(8,128)S(1)} %get-tuple-element.24), channel_id=1, source_target_pairs={{4,0},{8,4},{12,8},{16,12},{20,16},{24,20},{28,24},{5,1},{9,5},{13... | collective-permute-start | bytes 393224 | tf_op jit(solution)/shard_map/ppermute | solution.py:21
  76.2 24.6 %copy-start.1 = (f32[32,256,128]{2,1,0:T(8,128)S(1)}, f32[32,256,128]{2,1,0:T(8,128)}, u32[]{:S(2)}) copy-start(f32[32,256,128]{2,1,0:T(8,128)} %param.9) | copy-start | bytes 12582916
  76.2 24.5 %copy-start.4 = (f32[256,128]{1,0:T(8,128)S(1)}, f32[256,128]{1,0:T(8,128)}, u32[]{:S(2)}) copy-start(f32[256,128]{1,0:T(8,128)} %param.10) | copy-start | bytes 393220
  88.4 7.6 %collective-permute-start.2 = (f32[32,256,8]{1,2,0:T(8,128)S(1)}, f32[32,256,8]{1,2,0:T(8,128)S(1)}, u32[]{:S(2)}, u32[]{:S(2)}) collective-permute-start(f32[32,256,8]{1,2,0:T(8,128)S(1)} %get-tuple-element.21), channel_id=1, source_target_pairs={{0,1},{1,2},{2,3},{4,5},{5,6},{6,7},{8,9},{9,10},{10,11},{12,13},{... | collective-permute-start | bytes 786440 | tf_op jit(solution)/shard_map/ppermute | solution.py:18
  91.9 8.8 %collective-permute-start.3 = (f32[32,256,8]{1,2,0:T(8,128)S(1)}, f32[32,256,8]{1,2,0:T(8,128)S(1)}, u32[]{:S(2)}, u32[]{:S(2)}) collective-permute-start(f32[32,256,8]{1,2,0:T(8,128)S(1)} %get-tuple-element.22), channel_id=1, source_target_pairs={{1,0},{2,1},{3,2},{5,4},{6,5},{7,6},{9,8},{10,9},{11,10},{13,12},{... | collective-permute-start | bytes 786440 | tf_op jit(solution)/shard_map/ppermute | solution.py:21
  127.3 17.5 %copy-start.3 = (f32[32,1,1,1024]{3,2,1,0:T(1,128)S(1)}, f32[32,1,1,1024]{3,2,1,0:T(1,128)}, u32[]{:S(2)}) copy-start(f32[32,1,1,1024]{3,2,1,0:T(1,128)} %param.11) | copy-start | bytes 393220
  127.3 17.5 %copy-start.5 = (f32[1,1,1024]{2,1,0:T(1,128)S(1)}, f32[1,1,1024]{2,1,0:T(1,128)}, u32[]{:S(2)}) copy-start(f32[1,1,1024]{2,1,0:T(1,128)} %param.12) | copy-start | bytes 12292
  313.0 2.8 collective-permute-start.4
  314.3 5.8 %collective-permute-start.5 = (f32[32,8,128]{2,0,1:T(8,128)S(1)}, f32[32,8,128]{2,0,1:T(8,128)S(1)}, u32[]{:S(2)}, u32[]{:S(2)}) collective-permute-start(f32[32,8,128]{2,0,1:T(8,128)S(1)} %get-tuple-element.20), channel_id=1, source_target_pairs={{4,0},{8,4},{12,8},{16,12},{20,16},{24,20},{28,24},{5,1},{9,5},{13... | collective-permute-start | bytes 393224 | tf_op jit(solution)/shard_map/ppermute | solution.py:21
  320.5 24.6 %copy-start.2 = (f32[32,256,128]{2,1,0:T(8,128)S(1)}, f32[32,256,128]{2,1,0:T(8,128)}, u32[]{:S(2)}) copy-start(f32[32,256,128]{2,1,0:T(8,128)} %multiply_add_fusion.3) | copy-start | bytes 12582916
  332.6 7.8 %collective-permute-start.6 = (f32[32,256,8]{1,2,0:T(8,128)S(1)}, f32[32,256,8]{1,2,0:T(8,128)S(1)}, u32[]{:S(2)}, u32[]{:S(2)}) collective-permute-start(f32[32,256,8]{1,2,0:T(8,128)S(1)} %get-tuple-element.17), channel_id=1, source_target_pairs={{0,1},{1,2},{2,3},{4,5},{5,6},{6,7},{8,9},{9,10},{10,11},{12,13},{... | collective-permute-start | bytes 786440 | tf_op jit(solution)/shard_map/ppermute | solution.py:18
  336.3 8.8 %collective-permute-start.7 = (f32[32,256,8]{1,2,0:T(8,128)S(1)}, f32[32,256,8]{1,2,0:T(8,128)S(1)}, u32[]{:S(2)}, u32[]{:S(2)}) collective-permute-start(f32[32,256,8]{1,2,0:T(8,128)S(1)} %get-tuple-element.18), channel_id=1, source_target_pairs={{1,0},{2,1},{3,2},{5,4},{6,5},{7,6},{9,8},{10,9},{11,10},{13,12},{... | collective-permute-start | bytes 786440 | tf_op jit(solution)/shard_map/ppermute | solution.py:21
where the time goes:
time: 453 us; the launch traced here: 446 us
  blocking collectives  127 us (28%)
  matrix products  98.4 us (22%)
  other arithmetic  92.9 us (21%)
  local copies, waits for them, and re-layouts  77.2 us (17%)
  waiting for transfers between devices  23 us (5%)
  starting transfers between devices  16.5 us (4%)
  between operations  11.3 us (2%)
    psum x2, blocking collectives, squares(): return lax.psum(inner(residual_vector, residual_vector), ('row', 'col'))  84.1 us
    scatter-add x2, other arithmetic, body(): merged = grid_part.reshape(steps, rows * cols).at[:, station_indices].add...  63.2 us
    psum x1, blocking collectives, body(): alpha = norm_now / lax.psum(inner(direction, image), ('row', 'col'))  42.5 us
    dot_general x2, matrix products, body(): jnp.einsum('st,tij->sij', time_cov, merged, precision=highest_precision)  42.1 us
    gather x2, local copies, waits for them, and re-layouts, body(): smooth.reshape(steps, rows * cols)[:, station_indices]  33.1 us
    dot_general x2, matrix products, body(): jnp.einsum('tia,aj->tij', broader, band_cols, precision=highest_precision)  32.1 us
    dot_general x2, matrix products, body(): jnp.einsum('fbm,bv->fvm', widened_tiles, taper_band_rows, precision=highe...  24.2 us
    reshape x2, local copies, waits for them, and re-layouts, body(): smooth.reshape(steps, rows * cols)[:, station_indices]  21.2 us
  transfers between devices with their start and end apart: 8, of which 6 were waited for; matrix products, arithmetic and copies ran while one was open for 0% of the time, Pallas kernels for 0%

commit v1 on v0

v1 whole, which is shorter than its diff:
```python
import functools

import jax
import jax.numpy as jnp
from jax import lax
from jax.experimental import pallas as pl
from jax.experimental.pallas import tpu as pltpu
from jax.sharding import PartitionSpec as P

REACH = 8
LANES = 128
GROUP = 8
F32 = jnp.float32
BF16 = jnp.bfloat16
HIGHEST = lax.Precision.HIGHEST


def iota(shape, dim):
    return lax.broadcasted_iota(jnp.int32, shape, dim)


def taper(distance):
    spread = jnp.abs(distance).astype(F32)
    value = (1.0 - spread / (REACH + 1)) * jnp.exp(-spread / 3.0)
    return jnp.where(jnp.abs(distance) <= REACH, value, 0.0)


def split(x):
    high = x.astype(BF16)
    return high, (x - high.astype(F32)).astype(BF16)


def pair(x):
    high, low = split(x)
    return jnp.concatenate([high, low], axis=1)


def dot(a, b):
    return jnp.dot(a, b, preferred_element_type=F32)


def dot_nt(a, b):
    return lax.dot_general(a, b, (((1,), (1,)), ((), ())), preferred_element_type=F32)


def halves(x):
    width = x.shape[1] // 2
    return x[:, :width] + x[:, width:]


def three(x):
    high = x.astype(BF16)
    rest = x - high.astype(F32)
    middle = rest.astype(BF16)
    low = (rest - middle.astype(F32)).astype(BF16)
    return jnp.concatenate([high, middle, low], axis=0)


def cut(x, axis):
    return [
        lax.slice_in_dim(x, start, start + LANES, axis=axis)
        for start in range(0, x.shape[axis], LANES)
    ]


def rows_of(g):
    return pl.ds(pl.multiple_of(g * GROUP, GROUP), GROUP)


def prepare_kernel(
    count, cell, offset, noise, obs, cov,
    sb, info, rank_out, sv, gv, ut, bounds, mix, mat, band_rows, band_cols, edge,
    table, sorted_rows,
):
    steps, slots = obs.shape
    tiles = slots // LANES
    rows = band_rows.shape[1]
    groups = rows // GROUP
    wide = steps * GROUP
    slot = iota((1, slots), 1)
    live = slot < count[0, 0]
    where_row = cell[...] // LANES
    where_col = cell[...] - where_row * LANES
    key = jnp.where(live, where_row, rows) * slots + slot
    key = key.astype(F32)
    total = jnp.zeros((1, slots), F32)
    for block in range(tiles):
        piece = key[:, block * LANES : (block + 1) * LANES]
        column = jnp.transpose(jnp.broadcast_to(piece, (LANES, LANES)))
        column = jnp.concatenate([column] * tiles, axis=1)
        less = jnp.where(column < key, 1.0, 0.0)
        total = total + jnp.sum(less, axis=0, keepdims=True)
    rank = total.astype(jnp.int32)
    rank_out[...] = rank
    lived = jnp.where(live, 1.0, 0.0)
    table[pl.ds(0, steps), :] = obs[...] * lived
    table[pl.ds(steps, 1), :] = where_row.astype(F32)
    table[pl.ds(steps + 1, 1), :] = where_col.astype(F32)
    table[pl.ds(steps + 2, 1), :] = offset[0:1, :]
    table[pl.ds(steps + 3, 1), :] = offset[1:2, :]
    table[pl.ds(steps + 4, 1), :] = noise[...]
    table[pl.ds(steps + 5, 1), :] = lived
    table[pl.ds(steps + 6, 2), :] = jnp.zeros((2, slots), F32)
    pieces = three(table[...])
    height = table.shape[0]

    def sort_block(block, carry):
        start = pl.multiple_of(block * LANES, LANES)
        order = (iota((LANES, slots), 0) + start == rank).astype(F32).astype(BF16)
        out = dot_nt(pieces, order)
        sorted_rows[:, pl.ds(start, LANES)] = (
            out[:height] + out[height : 2 * height] + out[2 * height :]
        )
        return carry

    lax.fori_loop(0, tiles, sort_block, 0)
    ordered_row = sorted_rows[pl.ds(steps, 1), :]
    ordered_live = sorted_rows[pl.ds(steps + 5, 1), :]
    first_row = (iota((groups, slots), 0) * GROUP).astype(F32)
    before = jnp.where(ordered_row < first_row - 1.0, ordered_live, 0.0)
    until = jnp.where(ordered_row < first_row + GROUP, ordered_live, 0.0)
    low = jnp.sum(before, axis=1, keepdims=True)
    high = jnp.sum(until, axis=1, keepdims=True)
    start_tile = jnp.where(high > low, jnp.floor(low * (1.0 / LANES)), float(tiles))
    stop_tile = jnp.where(high > low, jnp.floor((high - 1.0) * (1.0 / LANES)) + 1.0, 0.0)
    lane = iota((groups, LANES), 1)
    bounds[...] = jnp.where(lane == 0, start_tile, stop_tile).astype(jnp.int32)
    for block in range(tiles + 2):
        if block >= tiles:
            sb[block] = jnp.zeros((steps, GROUP, LANES), F32)
            info[:, block] = jnp.zeros((2, GROUP, LANES), F32)
            sv[block] = jnp.zeros((2 * LANES, 2 * LANES), BF16)
            gv[block] = jnp.zeros((2 * LANES, 2 * LANES), BF16)
            ut[block] = jnp.zeros((rows, LANES), F32)
            continue
        lanes = pl.ds(block * LANES, LANES)
        at_row = sorted_rows[pl.ds(steps, 1), lanes].astype(jnp.int32)
        at_col = sorted_rows[pl.ds(steps + 1, 1), lanes].astype(jnp.int32)
        along_row = sorted_rows[pl.ds(steps + 2, 1), lanes]
        along_col = sorted_rows[pl.ds(steps + 3, 1), lanes]
        row = iota((rows, LANES), 0)
        ut[block] = jnp.where(row == at_row, 1.0 - along_row, 0.0) + jnp.where(
            row == at_row + 1, along_row, 0.0
        )
        col = iota((LANES, LANES), 0)
        across = jnp.where(col == at_col, 1.0 - along_col, 0.0) + jnp.where(
            col == at_col + 1, along_col, 0.0
        )
        for target, weight in ((gv, across), (sv, jnp.transpose(across))):
            high_part, low_part = split(weight)
            target[block] = jnp.concatenate(
                [
                    jnp.concatenate([high_part, low_part], axis=1),
                    jnp.concatenate([high_part, jnp.zeros_like(low_part)], axis=1),
                ],
                axis=0,
            )
        info[0, block] = jnp.broadcast_to(
            sorted_rows[pl.ds(steps + 4, 1), lanes], (GROUP, LANES)
        )
        info[1, block] = jnp.broadcast_to(
            sorted_rows[pl.ds(steps + 5, 1), lanes], (GROUP, LANES)
        )
        for step in range(steps):
            sb[block, step] = jnp.broadcast_to(
                sorted_rows[pl.ds(step, 1), lanes], (GROUP, LANES)
            )
    spread = (iota((wide, steps), 0) // GROUP == iota((wide, steps), 1)).astype(F32)
    spread_t = (iota((steps, wide), 1) // GROUP == iota((steps, wide), 0)).astype(F32)
    expanded = jnp.dot(
        jnp.dot(spread, cov[...], precision=HIGHEST, preferred_element_type=F32),
        spread_t,
        precision=HIGHEST,
        preferred_element_type=F32,
    )
    a = iota((wide, wide), 0)
    b = iota((wide, wide), 1)
    same = (a % GROUP) == (b % GROUP)
    mix[0], mix[1] = split(jnp.where(same, expanded, 0.0))
    near = taper((b % GROUP) + REACH - (a % GROUP)) * expanded
    near = jnp.concatenate(
        [jnp.concatenate([x[GROUP:], x[:GROUP]], axis=0) for x in cut(near, 0)], axis=0
    )
    mat[0], mat[1] = split(near)
    far = taper(REACH + (a % GROUP) - (b % GROUP)) * expanded
    far = jnp.concatenate(
        [pltpu.roll(x, LANES - GROUP, 1) for x in cut(far, 1)], axis=1
    )
    mat[2], mat[3] = split(far)
    ra = iota((rows, rows), 0)
    rb = iota((rows, rows), 1)
    band_rows[0], band_rows[1] = split(0.25 * taper(ra - rb))
    ca = iota((LANES, LANES), 0)
    cb = iota((LANES, LANES), 1)
    high_part, low_part = split(taper(ca - cb))
    band_cols[...] = jnp.concatenate(
        [
            jnp.concatenate([high_part, low_part], axis=1),
            jnp.concatenate([high_part, jnp.zeros_like(low_part)], axis=1),
        ],
        axis=0,
    )
    block_same = (a // GROUP) == (b // GROUP)
    above = 0.25 * taper((a % GROUP) + REACH - (b % GROUP))
    below = 0.25 * taper(REACH + (b % GROUP) - (a % GROUP))
    edge[0], edge[1] = split(jnp.where(block_same, above, 0.0))
    edge[2], edge[3] = split(jnp.where(block_same, below, 0.0))


def scatter_group(g, base, z, sb, ut, sv, bounds):
    steps = base.shape[0]
    flat = (steps * GROUP, LANES)
    first = bounds[g, 0]

    def tile(index):
        scaled = (sb[index] * ut[index, rows_of(g), :][None]).reshape(flat)
        return dot(pair(scaled), sv[index])

    out = halves(tile(first) + tile(first + 1))
    z[:, rows_of(g), :] = base[:, rows_of(g), :] + out.reshape(steps, GROUP, LANES)

    @pl.when(bounds[g, 1] > first + 2)
    def _():
        def more(index, carry):
            z[:, rows_of(g), :] += halves(tile(index)).reshape(steps, GROUP, LANES)
            return carry

        lax.fori_loop(first + 2, bounds[g, 1], more, 0)


def pack_group(g, z, strips):
    steps = z.shape[0]
    per = LANES // GROUP
    slot = iota((GROUP, LANES), 1) // GROUP
    for half in range(steps // per):
        left = jnp.zeros((GROUP, LANES), F32)
        right = jnp.zeros((GROUP, LANES), F32)
        for local in range(per):
            value = z[half * per + local, rows_of(g), :]
            if local:
                value = pltpu.roll(value, local * GROUP, 1)
            left = jnp.where(slot == local, value, left)
            right = jnp.where(slot == (local - 1) % per, value, right)
        lanes = pl.ds(half * LANES, LANES)
        strips[0, rows_of(g), lanes] = left
        strips[1, rows_of(g), lanes] = right


def unpack(left, right, step):
    per = LANES // GROUP
    half, local = step // per, step % per
    lane = iota((GROUP, LANES), 1)
    slot = lane // GROUP
    lanes = slice(half * LANES, (half + 1) * LANES)
    both = jnp.where(slot == local, left[:, lanes], right[:, lanes])
    if local:
        both = pltpu.roll(both, LANES - local * GROUP, 1)
    return jnp.where((lane < GROUP) | (lane >= LANES - GROUP), both, 0.0)


def scatter_all(base, z, strips, sb, ut, sv, bounds):
    groups = base.shape[1] // GROUP

    def run(g, carry):
        scatter_group(g, base, z, sb, ut, sv, bounds)
        pack_group(g, z, strips)
        return carry

    lax.fori_loop(0, groups, run, 0)


def scatter_kernel(bounds, base, sb, ut, sv, z, strips):
    scatter_all(base, z, strips, sb, ut, sv, bounds)


def filter_kernel(z, mix, band_rows, band_cols, w, u_edges, u):
    steps, rows, cols = z.shape
    groups = rows // GROUP
    flat = (steps * GROUP, LANES)

    def first(g, carry):
        value = z[:, rows_of(g), :].reshape(flat)
        across = halves(dot(pair(value), band_cols[...]))
        both = pair(across)
        mixed = halves(dot(mix[0], both)) + dot(mix[1], both[:, :LANES])
        u[:, rows_of(g), :] = mixed.reshape(steps, GROUP, LANES)
        return carry

    lax.fori_loop(0, groups, first, 0, unroll=2)
    u_edges[0] = u[:, pl.ds(0, GROUP), :]
    u_edges[1] = u[:, pl.ds(rows - GROUP, GROUP), :]

    def second(pairs, carry):
        one = pair(u[2 * pairs])
        two = pair(u[2 * pairs + 1])
        low = dot(band_rows[1], jnp.concatenate([one[:, :LANES], two[:, :LANES]], axis=1))
        w[2 * pairs] = halves(dot(band_rows[0], one)) + low[:, :LANES]
        w[2 * pairs + 1] = halves(dot(band_rows[0], two)) + low[:, LANES:]
        return carry

    lax.fori_loop(0, steps // 2, second, 0)


def edge_kernel(from_left, from_right, u_edges, mat, band_rows, sides, full_edges):
    steps = u_edges.shape[1]
    rows = from_left.shape[0]
    for side, source in ((0, from_left), (1, from_right)):
        high, low = split(source[...])
        value = dot(high, mat[2 * side]) + dot(low, mat[2 * side])
        value = value + dot(high, mat[2 * side + 1])
        sides[side] = value
    for which, start in ((0, 0), (1, rows - GROUP)):
        left = sides[0, pl.ds(start, GROUP), :]
        right = sides[1, pl.ds(start, GROUP), :]
        for step in range(steps):
            full_edges[which, step] = u_edges[which, step] + unpack(left, right, step)
    for side in range(2):
        high, low = split(sides[side])
        sides[side] = (
            dot(band_rows[0], high) + dot(band_rows[0], low) + dot(band_rows[1], high)
        )


def add_sides_kernel(w_in, sides, w):
    steps, rows, _ = w.shape

    def run(g, carry):
        left = sides[0, rows_of(g), :]
        right = sides[1, rows_of(g), :]
        for step in range(steps):
            w[step, rows_of(g), :] = w_in[step, rows_of(g), :] + unpack(left, right, step)
        return carry

    lax.fori_loop(0, rows // GROUP, run, 0)


def fill_extra(extra, above, below, edge):
    steps = above.shape[0]
    flat = (steps * GROUP, LANES)
    for which, source in ((0, above), (1, below)):
        both = pair(source[...].reshape(flat))
        value = halves(dot(edge[2 * which], both)) + dot(edge[2 * which + 1], both[:, :LANES])
        extra[which] = value.reshape(steps, GROUP, LANES)
    extra[2] = jnp.zeros((steps, GROUP, LANES), F32)


def gather_group(g, value, acc, ut, gv, bounds):
    steps = value.shape[0]
    both = pair(value.reshape(steps * GROUP, LANES))
    first = bounds[g, 0]

    def add(index):
        out = halves(dot(both, gv[index])).reshape(steps, GROUP, LANES)
        acc[index] += out * ut[index, rows_of(g), :][None]

    add(first)
    add(first + 1)

    @pl.when(bounds[g, 1] > first + 2)
    def _():
        def more(index, carry):
            add(index)
            return carry

        lax.fori_loop(first + 2, bounds[g, 1], more, 0)


def whole(x):
    return jnp.sum(jnp.sum(x, axis=1, keepdims=True), axis=0, keepdims=True)


def image_pass(w, extra, noise, field, out, acc, ut, gv, bounds, terms, sums):
    steps, rows, _ = w.shape
    groups = rows // GROUP
    acc[...] = jnp.zeros_like(acc)

    def run(g, carry):
        which = jnp.where(g == 0, 0, jnp.where(g == groups - 1, 1, 2))
        value = w[:, rows_of(g), :] + extra[which]
        mine = field[:, rows_of(g), :]
        image = value + noise[rows_of(g), :][None] * mine
        out[:, rows_of(g), :] = image
        gather_group(g, value, acc, ut, gv, bounds)
        return tuple(c + t for c, t in zip(carry, terms(g, mine, image)))

    return lax.fori_loop(0, groups, run, sums)


def image_stations(index, acc, info, field):
    sampled = jnp.sum(acc[index], axis=1, keepdims=True)
    mine = field[index]
    live = info[1, index][None]
    return live * (sampled + info[0, index][None] * mine) + (1.0 - live) * mine


def image_one_kernel(
    bounds, w, above, below, edge, noise, b, sb, info, ut, gv, sv, rank,
    p, ps, z, strips, sums, unsorted, acc, extra, flat_rows,
):
    steps, rows, _ = w.shape
    tiles = sb.shape[0] - 2
    slots = tiles * LANES
    fill_extra(extra, above, below, edge)

    def fold(x, y):
        return jnp.sum(x * y, axis=0)

    def terms(g, mine, image):
        return fold(mine, mine), fold(mine, image), fold(image, image)

    zero = jnp.zeros((GROUP, LANES), F32)
    grid_sums = image_pass(w, extra, noise, b, p, acc, ut, gv, bounds, terms, (zero,) * 3)

    def stations(index, carry):
        image = image_stations(index, acc, info, sb)
        ps[index] = image
        for step in range(steps):
            flat_rows[pl.ds(step, 1), pl.ds(pl.multiple_of(index * LANES, LANES), LANES)] = image[step, 0:1]
        mine = sb[index]
        return tuple(c + (1.0 / GROUP) * t for c, t in zip(carry, terms(0, mine, image)))

    both = lax.fori_loop(0, tiles, stations, grid_sums)
    ps[tiles] = jnp.zeros((steps, GROUP, LANES), F32)
    ps[tiles + 1] = jnp.zeros((steps, GROUP, LANES), F32)
    bb, bp, pp = (whole(x) for x in both)
    lane = iota((GROUP, LANES), 1)
    value = jnp.where(lane == 0, bb / bp, 0.0)
    value = jnp.where(lane == 1, bb, value)
    value = jnp.where(lane == 2, bp, value)
    value = jnp.where(lane == 3, pp, value)
    sums[...] = value
    scatter_all(p, z, strips, ps, ut, sv, bounds)
    pieces = three(flat_rows[...])

    def unsort_block(block, carry):
        start = pl.multiple_of(block * LANES, LANES)
        order = (iota((slots, LANES), 0) == rank[:, pl.ds(start, LANES)]).astype(F32).astype(BF16)
        out = dot(pieces, order)
        unsorted[:, pl.ds(start, LANES)] = (
            out[:steps] + out[steps : 2 * steps] + out[2 * steps :]
        )
        return carry

    lax.fori_loop(0, tiles, unsort_block, 0)


def image_two_kernel(
    bounds, w, above, below, edge, noise, b, p, sb, ps, info, ut, gv, sums,
    q, message, acc, extra,
):
    steps, rows, _ = w.shape
    tiles = sb.shape[0] - 2
    fill_extra(extra, above, below, edge)
    shift = sums[0:1, 0:1]

    def fold(x, y):
        return jnp.sum(x * y, axis=0)

    def products(first, mine, image):
        residual = first - shift[None] * mine
        moved = mine - shift[None] * image
        return fold(residual, residual), fold(residual, moved), fold(mine, image), fold(residual, image)

    def terms(g, mine, image):
        return products(b[:, rows_of(g), :], mine, image)

    zero = jnp.zeros((GROUP, LANES), F32)
    grid_sums = image_pass(w, extra, noise, p, q, acc, ut, gv, bounds, terms, (zero,) * 4)

    def stations(index, carry):
        image = image_stations(index, acc, info, ps)
        new = products(sb[index], ps[index], image)
        return tuple(c + (1.0 / GROUP) * t for c, t in zip(carry, new))

    both = lax.fori_loop(0, tiles, stations, grid_sums)
    lane = iota((1, LANES), 1)
    value = jnp.where(lane < 4, sums[0:1, :], 0.0)
    for place, x in enumerate(both):
        value = jnp.where(lane == 4 + place, whole(x), value)
    message[...] = jnp.broadcast_to(value, message.shape)


def final_kernel(received, b, p, q, obs, unsorted, count, solution_out, residual_out, station_out):
    everything = received[...]

    def column(index):
        return everything[:, index : index + 1]

    def total(x):
        return jnp.sum(x, axis=0, keepdims=True)

    shift, bb, bp, pp = (column(i) for i in range(4))
    rr, ru, pq, rq = (column(i) for i in range(4, 8))
    norm = total(bb)
    alpha = norm / total(bp)
    delta = shift - alpha
    rp = bp - shift * pp
    pu = pp - shift * pq
    norm_next = total(rr + 2.0 * delta * rp + delta * delta * pp)
    energy = total(ru + delta * (rq + pu) + delta * delta * pq)
    beta = norm_next / norm
    alpha_next = norm_next / (energy - beta * norm_next / alpha)
    along = alpha + alpha_next * (1.0 + beta)
    twice = alpha_next * alpha
    first = b[...]
    second = p[...]
    solution_out[...] = along[None] * first - twice[None] * second
    residual_out[...] = first - along[None] * second + twice[None] * q[...]

    @pl.when(pl.program_id(0) == 0)
    def _():
        steps, slots = obs.shape
        live = iota((steps, slots), 1) < count[0, 0]
        own = jnp.where(live, obs[...], 0.0)
        station_out[...] = along * own - twice * unsorted[...]


VMEM = pl.BlockSpec(memory_space=pltpu.VMEM)
SMEM = pl.BlockSpec(memory_space=pltpu.SMEM)


def call(kernel, outs, ins, operands, scratch=(), flops=10**9, moved=10**7, limit=40, **extra):
    return pl.pallas_call(
        kernel,
        out_shape=outs,
        in_specs=ins,
        out_specs=[VMEM] * len(outs),
        scratch_shapes=list(scratch),
        compiler_params=pltpu.CompilerParams(vmem_limit_bytes=limit * 2**20),
        cost_estimate=pl.CostEstimate(flops=flops, bytes_accessed=moved, transcendentals=0),
        **extra,
    )(*operands)


def exchange(first, second, axis):
    count = lax.axis_size(axis)
    forward = [(i, i + 1) for i in range(count - 1)]
    backward = [(target, source) for source, target in forward]
    return lax.ppermute(first, axis, forward), lax.ppermute(second, axis, backward)


def body(
    grid_obs, grid_noise, station_obs, station_noise, station_offset, station_cell,
    station_count, time_cov,
):
    steps, rows, cols = grid_obs.shape
    slots = station_obs.shape[3]
    tiles = slots // LANES
    wide = steps * GROUP
    groups = rows // GROUP
    devices = lax.axis_size("row") * lax.axis_size("col")
    obs = station_obs.reshape(steps, slots)
    shape = jax.ShapeDtypeStruct
    field = shape((steps, rows, cols), F32)
    rim = shape((2, steps, GROUP, cols), F32)
    strips_shape = shape((2, rows, wide), F32)
    sb, info, rank, sv, gv, ut, bounds, mix, mat, band_rows, band_cols, edge = call(
        prepare_kernel,
        [
            shape((tiles + 2, steps, GROUP, LANES), F32),
            shape((2, tiles + 2, GROUP, LANES), F32),
            shape((1, slots), jnp.int32),
            shape((tiles + 2, 2 * LANES, 2 * LANES), BF16),
            shape((tiles + 2, 2 * LANES, 2 * LANES), BF16),
            shape((tiles + 2, rows, LANES), F32),
            shape((groups, LANES), jnp.int32),
            shape((2, wide, wide), BF16),
            shape((4, wide, wide), BF16),
            shape((2, rows, rows), BF16),
            shape((2 * LANES, 2 * LANES), BF16),
            shape((4, wide, wide), BF16),
        ],
        [SMEM] + [VMEM] * 5,
        (
            station_count,
            station_cell.reshape(1, slots),
            station_offset.reshape(2, slots),
            station_noise.reshape(1, slots),
            obs,
            time_cov,
        ),
        [pltpu.VMEM((steps + 8, slots), F32), pltpu.VMEM((steps + 8, slots), F32)],
    )
    z, strips = call(
        scatter_kernel,
        [field, strips_shape],
        [SMEM] + [VMEM] * 4,
        (bounds, grid_obs, sb, ut, sv),
    )

    def smooth(z, strips):
        from_left, from_right = exchange(strips[1], strips[0], "col")
        w, u_edges = call(
            filter_kernel,
            [field, rim],
            [VMEM] * 4,
            (z, mix, band_rows, band_cols),
            [pltpu.VMEM((steps, rows, cols), F32)],
        )
        sides, full_edges = call(
            edge_kernel,
            [strips_shape, rim],
            [VMEM] * 5,
            (from_left, from_right, u_edges, mat, band_rows),
        )
        above, below = exchange(full_edges[1], full_edges[0], "row")
        (w,) = call(add_sides_kernel, [field], [VMEM] * 2, (w, sides), input_output_aliases={0: 0})
        return w, above, below

    w, above, below = smooth(z, strips)
    station_field = shape((tiles + 2, steps, GROUP, LANES), F32)
    p, ps, z, strips, sums, unsorted = call(
        image_one_kernel,
        [field, station_field, field, strips_shape, shape((GROUP, LANES), F32), shape((steps, slots), F32)],
        [SMEM] + [VMEM] * 12,
        (bounds, w, above, below, edge, grid_noise, grid_obs, sb, info, ut, gv, sv, rank),
        [
            pltpu.VMEM((tiles + 2, steps, GROUP, LANES), F32),
            pltpu.VMEM((3, steps, GROUP, LANES), F32),
            pltpu.VMEM((steps, slots), F32),
        ],
    )
    w, above, below = smooth(z, strips)
    q, message = call(
        image_two_kernel,
        [field, shape((devices, LANES), F32)],
        [SMEM] + [VMEM] * 13,
        (bounds, w, above, below, edge, grid_noise, grid_obs, p, sb, ps, info, ut, gv, sums),
        [
            pltpu.VMEM((tiles + 2, steps, GROUP, LANES), F32),
            pltpu.VMEM((3, steps, GROUP, LANES), F32),
        ],
    )
    received = lax.all_to_all(message, ("row", "col"), 0, 0, tiled=True)
    parts = 8
    block = pl.BlockSpec((steps // parts, rows, cols), lambda i: (i, 0, 0))
    fixed = lambda dims: pl.BlockSpec(dims, lambda i: (0,) * len(dims))
    solution_grid, residual_grid, solution_stations = pl.pallas_call(
        final_kernel,
        grid=(parts,),
        out_shape=[field, field, shape((steps, slots), F32)],
        in_specs=[
            fixed((devices, LANES)), block, block, block, fixed((steps, slots)), fixed((steps, slots)), SMEM,
        ],
        out_specs=[block, block, fixed((steps, slots))],
        compiler_params=pltpu.CompilerParams(vmem_limit_bytes=20 * 2**20),
    )(received, grid_obs, p, q, obs, unsorted, station_count)
    return solution_grid, solution_stations.reshape(steps, 1, 1, slots), residual_grid


def solution(mesh):
    placed = (
        P(None, "row", "col"),
        P("row", "col"),
        P(None, "row", "col", None),
        P("row", "col", None),
        P(None, "row", "col", None),
        P("row", "col", None),
        P("row", "col"),
        P(),
    )
    return jax.shard_map(
        body,
        mesh=mesh,
        in_specs=placed,
        out_specs=(P(None, "row", "col"), P(None, "row", "col", None), P(None, "row", "col")),
        check_vma=False,
    )
```

time: 453 us -> 171 us (0.38); the launches traced: 446 us -> 170 us
  blocking collectives: 127 us -> 13.4 us
  Pallas kernels: 0 us -> 111 us
  matrix products: 98.4 us -> 0 us
  other arithmetic: 92.9 us -> 0 us
  local copies, waits for them, and re-layouts: 77.2 us -> 21.8 us
  waiting for transfers between devices: 23 us -> 0.02 us
  between operations: 11.3 us -> 1.76 us
  starting transfers between devices: 16.5 us -> 22 us
    psum x3 -> x0, blocking collectives: 127 us -> none  [the longest x2 84.1 us: squares(): return lax.psum(inner(residual_vector, residual_vector), ('row', 'col'))]
    pallas_call x0 -> x11, Pallas kernels: none -> 111 us  [the longest x10 103 us: call(): pl.pallas_call(kernel, out_shape=outs, in_specs=ins, out_specs=[VMEM] * l...]
    dot_general x6 -> x0, matrix products: 98.4 us -> none  [the longest x2 42.1 us: body(): jnp.einsum('st,tij->sij', time_cov, merged, precision=highest_precision)]
    scatter-add x2 -> x0, other arithmetic: 63.2 us -> none  [body(): merged = grid_part.reshape(steps, rows * cols).at[:, station_indices].add...]
    gather x2 -> x0, local copies, waits for them, and re-layouts: 33.1 us -> none  [body(): smooth.reshape(steps, rows * cols)[:, station_indices]]
    reshape x3 -> x0, local copies, waits for them, and re-layouts: 31.8 us -> none  [the longest x2 21.2 us: body(): smooth.reshape(steps, rows * cols)[:, station_indices]]
    ppermute x8, waiting for transfers between devices: 23 us -> 0.02 us  [the longest x4 0.01 us: exchange(): lax.ppermute(first, axis, forward)]
    add x3 -> x0, other arithmetic: 16.1 us -> none  [combine(): return (first[0] + scale * second[0], first[1] + scale * second[1])]
  transfers between devices with their start and end apart: 8 -> 8, of which waited for: 6 -> 0; matrix products, arithmetic and copies ran while one was open for 0% -> 0% of each run, Pallas kernels for 0% -> 24%
where the time goes in v1:
time: 171 us; the launch traced here: 170 us
  Pallas kernels  111 us (65%)
  starting transfers between devices  22 us (13%)
  local copies, waits for them, and re-layouts  21.8 us (13%)
  blocking collectives  13.4 us (8%)
  between operations  1.76 us (1%)
    pallas_call x10, Pallas kernels, call(): pl.pallas_call(kernel, out_shape=outs, in_specs=ins, out_specs=[VMEM] * l...  103 us
    unnamed x61, local copies, waits for them, and re-layouts  21.6 us
    ppermute x4, starting transfers between devices, exchange(): lax.ppermute(first, axis, forward)  16.7 us
    all_to_all x1, blocking collectives, body(): received = lax.all_to_all(message, ('row', 'col'), 0, 0, tiled=True)  13.4 us
    pallas_call x1, Pallas kernels, body(): pl.pallas_call(final_kernel, grid=(parts,), out_shape=[field, field, shap...  8.41 us
    ppermute x4, starting transfers between devices, exchange(): lax.ppermute(second, axis, backward)  5.3 us
  transfers between devices with their start and end apart: 8, of which 0 were waited for; matrix products, arithmetic and copies ran while one was open for 0% of the time, Pallas kernels for 24%

profile of v1, /device:TPU:0, one launch (start us, length us, event | category | flops | bytes accessed | tf_op | source)
XLA Modules:
  0.0 170.2 jit_solution(9599502368716819010)
XLA Ops:
  1.3 0.7 copy.21
  2.0 0.9 copy.20
  2.9 0.0 copy-start.24
  2.9 0.7 copy-done.24
  3.6 0.7 copy-done.25
  4.3 0.7 copy-done.26
  5.0 4.2 %shard_map.103 = (f32[10,32,8,128]{3,2,1,0:T(8,128)S(1)}, f32[2,10,8,128]{3,2,1,0:T(8,128)S(1)}, s32[1,1024]{1,0:T(1,128)S(1)}, bf16[10,256,256]{2,1,0:T(8,128)(...) custom-call(s32[1,1]{1,0:T(1,128)S(6)} %copy.24.count, ...), custom_call_target="tpu_custom_call" | custom-call | flops 1000000000 | bytes 10000000 | tf_op jit(solution)/shard_map/pallas_call | solution.py:523
  9.3 0.0 copy-start
  9.3 3.5 %copy-done = f32[32,256,128]{2,1,0:T(8,128)S(1)} copy-done((f32[32,256,128]{2,1,0:T(8,128)S(1)}, f32[32,256,128]{2,1,0:T(8,128)}, u32[]{:S(2)}) %copy-start) | copy-done | bytes 4194328
  12.8 11.6 %shard_map.104 = (f32[32,256,128]{2,1,0:T(8,128)S(1)}, f32[2,256,256]{2,1,0:T(8,128)S(1)}) custom-call(s32[32,128]{1,0:T(8,128)S(1)} %get-tuple-element.36.bounds, f32[32,256,128]{2,1,0:T(8,128)S(1)} %copy-done, f32[10,32,8,128]{3,2,1,0:T(8,128)S(1)} %get-tuple-element.37.sb, f32[10,256,128]{2,1,0:T(8,128)S(1)} %get-tuple-element.38.ut, ...), custom_call_target="tpu_custom_call" | custom-call | flops 1000000000 | bytes 10000000 | tf_op jit(solution)/shard_map/pallas_call | solution.py:523
  24.4 0.0 copy-start.11
  24.4 2.0 %copy-done.11 = f32[32,256,128]{2,1,0:T(8,128)} copy-done((f32[32,256,128]{2,1,0:T(8,128)}, f32[32,256,128]{2,1,0:T(8,128)S(1)}, u32[]{:S(2)}) %copy-start.11) | copy-done | bytes 4194328
  26.5 1.3 collective-permute-start.1
  27.8 5.6 %collective-permute-start = (f32[256,256]{1,0:T(8,128)S(1)}, f32[256,256]{1,0:T(8,128)S(1)}, u32[]{:S(2)}, u32[]{:S(2)}) collective-permute-start(f32[256,256]{1,0:T(8,128)S(1)} %get-tuple-element.78), channel_id=1, source_target_pairs={{0,1},{1,2},{2,3},{4,5},{5,6},{6,7},{8,9},{9,10},{10,11},{12,13},{... | collective-permute-start | bytes 786440 | tf_op jit(solution)/shard_map/ppermute | solution.py:539
  33.4 0.0 copy-start.12
  33.4 2.2 %copy-done.12 = f32[32,256,128]{2,1,0:T(8,128)S(1)} copy-done((f32[32,256,128]{2,1,0:T(8,128)S(1)}, f32[32,256,128]{2,1,0:T(8,128)}, u32[]{:S(2)}) %copy-start.12) | copy-done | bytes 4194328
  35.6 15.6 %shard_map.105 = (f32[32,256,128]{2,1,0:T(8,128)S(1)}, f32[2,32,8,128]{3,2,1,0:T(8,128)S(1)}) custom-call(f32[32,256,128]{2,1,0:T(8,128)S(1)} %copy-done.12, bf16[2,256,256]{2,1,0:T(8,128)(2,1)S(1)} %get-tuple-element.41.mix, bf16[2,256,256]{2,1,0:T(8,128)(2,1)S(1)} %get-tuple-element.42.band_rows, bf16[256,256]{1,0:T(8,128)(2,1)S(1)} %get-tuple-element.43.band_cols), custom_call_target="tpu_custom_call" | custom-call | flops 1000000000 | bytes 10000000 | tf_op jit(solution)/shard_map/pallas_call | solution.py:523
  51.2 0.0 collective-permute-done.1.from_right
  51.3 0.0 collective-permute-done.from_left
  51.3 0.7 shard_map.106
  52.1 1.3 collective-permute-start.3
  53.4 3.0 %collective-permute-start.2 = (f32[32,8,128]{2,1,0:T(8,128)S(1)}, f32[32,8,128]{2,1,0:T(8,128)S(1)}, u32[]{:S(2)}, u32[]{:S(2)}) collective-permute-start(f32[32,8,128]{2,1,0:T(8,128)S(1)} %get-tuple-element.82), channel_id=1, source_target_pairs={{0,4},{4,8},{8,12},{12,16},{16,20},{20,24},{24,28},{1,5},{5,9},{9,... | collective-permute-start | bytes 393224 | tf_op jit(solution)/shard_map/ppermute | solution.py:539
  56.4 0.0 copy-start.19
  56.4 4.8 %shard_map.107.w = f32[32,256,128]{2,1,0:T(8,128)S(1)} custom-call(f32[32,256,128]{2,1,0:T(8,128)S(1)} %get-tuple-element.44.w_in, f32[2,256,256]{2,1,0:T(8,128)S(1)} %get-tuple-element.48.sides), custom_call_target="tpu_custom_call", output_to_operand_aliasing={{}: (0, {})} | custom-call | flops 1000000000 | bytes 10000000 | tf_op jit(solution)/shard_map/pallas_call | solution.py:523
  61.2 0.0 copy-start.5
  61.2 2.0 %copy-done.5 = f32[32,256,128]{2,1,0:T(8,128)} copy-done((f32[32,256,128]{2,1,0:T(8,128)}, f32[32,256,128]{2,1,0:T(8,128)S(1)}, u32[]{:S(2)}) %copy-start.5) | copy-done | bytes 4194328
  63.3 0.0 copy-start.21
  63.3 28.0 %shard_map.108 = (f32[32,256,128]{2,1,0:T(8,128)S(1)}, f32[10,32,8,128]{3,2,1,0:T(8,128)S(1)}, f32[32,256,128]{2,1,0:T(8,128)}, f32[2,256,256]{2,1,0:T(8,128)S(1...) custom-call(s32[32,128]{1,0:T(8,128)S(1)} %get-tuple-element.36.bounds, f32[32,256,128]{2,1,0:T(8,128)} %copy-done.5, ...), custom_call_target="tpu_custom_call" | custom-call | flops 1000000000 | bytes 10000000 | tf_op jit(solution)/shard_map/pallas_call | solution.py:523
  91.3 2.0 %copy-done.2 = f32[32,256,128]{2,1,0:T(8,128)} copy-done((f32[32,256,128]{2,1,0:T(8,128)}, f32[32,256,128]{2,1,0:T(8,128)S(1)}, u32[]{:S(2)}) %copy-start.2) | copy-done | bytes 4194328
  93.2 1.2 copy-done.13
  94.4 1.4 collective-permute-start.5
  95.9 4.6 %collective-permute-start.4 = (f32[256,256]{1,0:T(8,128)S(1)}, f32[256,256]{1,0:T(8,128)S(1)}, u32[]{:S(2)}, u32[]{:S(2)}) collective-permute-start(f32[256,256]{1,0:T(8,128)S(1)} %get-tuple-element.76), channel_id=1, source_target_pairs={{0,1},{1,2},{2,3},{4,5},{5,6},{6,7},{8,9},{9,10},{10,11},{12,13},{... | collective-permute-start | bytes 786440 | tf_op jit(solution)/shard_map/ppermute | solution.py:539
  100.5 0.0 copy-start.10
  100.5 2.2 %copy-done.10 = f32[32,256,128]{2,1,0:T(8,128)S(1)} copy-done((f32[32,256,128]{2,1,0:T(8,128)S(1)}, f32[32,256,128]{2,1,0:T(8,128)}, u32[]{:S(2)}) %copy-start.10) | copy-done | bytes 4194328
  102.7 15.4 %shard_map.109 = (f32[32,256,128]{2,1,0:T(8,128)S(1)}, f32[2,32,8,128]{3,2,1,0:T(8,128)S(1)}) custom-call(f32[32,256,128]{2,1,0:T(8,128)S(1)} %copy-done.10, bf16[2,256,256]{2,1,0:T(8,128)(2,1)S(1)} %copy-done.18, bf16[2,256,256]{2,1,0:T(8,128)(2,1)S(1)} %copy-done.16, bf16[256,256]{1,0:T(8,128)(2,1)S(1)} %copy-done.21), custom_call_target="tpu_custom_call" | custom-call | flops 1000000000 | bytes 10000000 | tf_op jit(solution)/shard_map/pallas_call | solution.py:523
  118.1 0.0 collective-permute-done.5.from_right
  118.1 0.0 collective-permute-done.4.from_left
  118.1 0.7 shard_map.110
  118.9 1.3 collective-permute-start.7
  120.2 3.5 %collective-permute-start.6 = (f32[32,8,128]{2,1,0:T(8,128)S(1)}, f32[32,8,128]{2,1,0:T(8,128)S(1)}, u32[]{:S(2)}, u32[]{:S(2)}) collective-permute-start(f32[32,8,128]{2,1,0:T(8,128)S(1)} %get-tuple-element.80), channel_id=1, source_target_pairs={{0,4},{4,8},{8,12},{12,16},{16,20},{20,24},{24,28},{1,5},{5,9},{9,... | collective-permute-start | bytes 393224 | tf_op jit(solution)/shard_map/ppermute | solution.py:539
  123.8 4.8 %shard_map.111.w = f32[32,256,128]{2,1,0:T(8,128)S(1)} custom-call(f32[32,256,128]{2,1,0:T(8,128)S(1)} %get-tuple-element.55.w_in, f32[2,256,256]{2,1,0:T(8,128)S(1)} %get-tuple-element.58.sides), custom_call_target="tpu_custom_call", output_to_operand_aliasing={{}: (0, {})} | custom-call | flops 1000000000 | bytes 10000000 | tf_op jit(solution)/shard_map/pallas_call | solution.py:523
  128.6 0.0 copy-start.4
  128.6 2.0 %copy-done.4 = f32[32,256,128]{2,1,0:T(8,128)} copy-done((f32[32,256,128]{2,1,0:T(8,128)}, f32[32,256,128]{2,1,0:T(8,128)S(1)}, u32[]{:S(2)}) %copy-start.4) | copy-done | bytes 4194328
  130.6 0.0 copy-start.1
  130.6 16.9 %shard_map.112 = (f32[32,256,128]{2,1,0:T(8,128)S(1)}, f32[32,128]{1,0:T(8,128)S(1)}) custom-call(s32[32,128]{1,0:T(8,128)S(1)} %get-tuple-element.36.bounds, f32[32,256,128]{2,1,0:T(8,128)} %copy-done.4, f32[32,8,128]{2,1,0:T(8,128)S(1)} %collective-permute-done.6.above, f32[32,8,128]{2,1,0:T(8,128)S(1)} %collective-permute-done.7.below, ...), custom_call_target="tpu_custom_call" | custom-call | flops 1000000000 | bytes 10000000 | tf_op jit(solution)/shard_map/pallas_call | solution.py:523
  147.5 13.4 %all_to_all.11 = f32[32,1,128]{2,1,0:T(1,128)S(1)} all-to-all(f32[32,1,128]{2,1,0:T(1,128)S(1)} %bitcast.33), channel_id=1, replica_groups=mesh['row'=8,'col'=4] {'row','col'}, dimensions={0} | all-to-all | bytes 32768 | tf_op jit(solution)/shard_map/all_to_all | solution.py:634
  161.0 8.4 %shard_map.113 = (f32[32,256,128]{2,1,0:T(8,128)}, f32[32,256,128]{2,1,0:T(8,128)}, f32[32,1024]{1,0:T(8,128)S(1)}) custom-call(f32[32,128]{1,0:T(8,128)S(1)} %bitcast.32, f32[32,256,128]{2,1,0:T(8,128)S(1)} %copy-done.1, f32[32,256,128]{2,1,0:T(8,128)S(1)} %copy-done.3, f32[32,256,128]{2,1,0:T(8,128)S(1)} %get-tuple-element.64.q, f32[32,1024]{1,0:T(8,128)S(1)} %bitcast.30, ...), custom_call_target="tpu_custom_call" | custom-call | tf_op jit(solution)/shard_map/pallas_call | solution.py:638
  169.4 0.8 copy.15
  (45 shorter events, 0.2 us)
Async XLA Ops:
  2.9 0.7 copy-start.24
  3.6 0.7 copy-start.25
  4.3 0.7 copy-start.26
  9.2 24.2 %copy-start.17 = (bf16[2,256,256]{2,1,0:T(8,128)(2,1)}, bf16[2,256,256]{2,1,0:T(8,128)(2,1)S(1)}, u32[]{:S(2)}) copy-start(bf16[2,256,256]{2,1,0:T(8,128)(2,1)S(1)} %get-tuple-element.41.mix) | copy-start | bytes 786436
  9.2 24.2 %copy-start.20 = (bf16[256,256]{1,0:T(8,128)(2,1)}, bf16[256,256]{1,0:T(8,128)(2,1)S(1)}, u32[]{:S(2)}) copy-start(bf16[256,256]{1,0:T(8,128)(2,1)S(1)} %get-tuple-element.43.band_cols) | copy-start | bytes 393220
  9.2 42.1 %copy-start.15 = (bf16[2,256,256]{2,1,0:T(8,128)(2,1)}, bf16[2,256,256]{2,1,0:T(8,128)(2,1)S(1)}, u32[]{:S(2)}) copy-start(bf16[2,256,256]{2,1,0:T(8,128)(2,1)S(1)} %get-tuple-element.42.band_rows) | copy-start | bytes 786436
  9.2 42.1 %copy-start.27 = (bf16[4,256,256]{2,1,0:T(8,128)(2,1)}, bf16[4,256,256]{2,1,0:T(8,128)(2,1)S(1)}, u32[]{:S(2)}) copy-start(bf16[4,256,256]{2,1,0:T(8,128)(2,1)S(1)} %get-tuple-element.47.mat) | copy-start | bytes 1572868
  9.2 54.0 %copy-start.6 = (f32[10,256,128]{2,1,0:T(8,128)}, f32[10,256,128]{2,1,0:T(8,128)S(1)}, u32[]{:S(2)}) copy-start(f32[10,256,128]{2,1,0:T(8,128)S(1)} %get-tuple-element.38.ut) | copy-start | bytes 3932164
  9.2 54.0 %copy-start.8 = (bf16[10,256,256]{2,1,0:T(8,128)(2,1)}, bf16[10,256,256]{2,1,0:T(8,128)(2,1)S(1)}, u32[]{:S(2)}) copy-start(bf16[10,256,256]{2,1,0:T(8,128)(2,1)S(1)} %get-tuple-element.52.gv) | copy-start | bytes 3932164
  9.3 54.0 %copy-start.22 = (f32[2,10,8,128]{3,2,1,0:T(8,128)}, f32[2,10,8,128]{3,2,1,0:T(8,128)S(1)}, u32[]{:S(2)}) copy-start(f32[2,10,8,128]{3,2,1,0:T(8,128)S(1)} %get-tuple-element.51.info) | copy-start | bytes 245764
  9.3 3.6 %copy-start = (f32[32,256,128]{2,1,0:T(8,128)S(1)}, f32[32,256,128]{2,1,0:T(8,128)}, u32[]{:S(2)}) copy-start(f32[32,256,128]{2,1,0:T(8,128)} %b.5) | copy-start | bytes 12582916
  24.4 2.0 %copy-start.11 = (f32[32,256,128]{2,1,0:T(8,128)}, f32[32,256,128]{2,1,0:T(8,128)S(1)}, u32[]{:S(2)}) copy-start(f32[32,256,128]{2,1,0:T(8,128)S(1)} %get-tuple-element.40.z) | copy-start | bytes 12582916
  26.5 24.8 %collective-permute-start.1 = (f32[256,256]{1,0:T(8,128)S(1)}, f32[256,256]{1,0:T(8,128)S(1)}, u32[]{:S(2)}, u32[]{:S(2)}) collective-permute-start(f32[256,256]{1,0:T(8,128)S(1)} %get-tuple-element.77), channel_id=1, source_target_pairs={{1,0},{2,1},{3,2},{5,4},{6,5},{7,6},{9,8},{10,9},{11,10},{13,12},{... | collective-permute-start | bytes 786440 | tf_op jit(solution)/shard_map/ppermute | solution.py:539
  27.8 23.5 %collective-permute-start = (f32[256,256]{1,0:T(8,128)S(1)}, f32[256,256]{1,0:T(8,128)S(1)}, u32[]{:S(2)}, u32[]{:S(2)}) collective-permute-start(f32[256,256]{1,0:T(8,128)S(1)} %get-tuple-element.78), channel_id=1, source_target_pairs={{0,1},{1,2},{2,3},{4,5},{5,6},{6,7},{8,9},{9,10},{10,11},{12,13},{... | collective-permute-start | bytes 786440 | tf_op jit(solution)/shard_map/ppermute | solution.py:539
  33.4 2.2 %copy-start.12 = (f32[32,256,128]{2,1,0:T(8,128)S(1)}, f32[32,256,128]{2,1,0:T(8,128)}, u32[]{:S(2)}) copy-start(f32[32,256,128]{2,1,0:T(8,128)} %copy-done.11) | copy-start | bytes 12582916
  52.1 11.2 %collective-permute-start.3 = (f32[32,8,128]{2,1,0:T(8,128)S(1)}, f32[32,8,128]{2,1,0:T(8,128)S(1)}, u32[]{:S(2)}, u32[]{:S(2)}) collective-permute-start(f32[32,8,128]{2,1,0:T(8,128)S(1)} %get-tuple-element.81), channel_id=1, source_target_pairs={{4,0},{8,4},{12,8},{16,12},{20,16},{24,20},{28,24},{5,1},{9,5},{13... | collective-permute-start | bytes 393224 | tf_op jit(solution)/shard_map/ppermute | solution.py:539
  53.4 9.9 %collective-permute-start.2 = (f32[32,8,128]{2,1,0:T(8,128)S(1)}, f32[32,8,128]{2,1,0:T(8,128)S(1)}, u32[]{:S(2)}, u32[]{:S(2)}) collective-permute-start(f32[32,8,128]{2,1,0:T(8,128)S(1)} %get-tuple-element.82), channel_id=1, source_target_pairs={{0,4},{4,8},{8,12},{12,16},{16,20},{20,24},{24,28},{1,5},{5,9},{9,... | collective-permute-start | bytes 393224 | tf_op jit(solution)/shard_map/ppermute | solution.py:539
  56.4 6.9 %copy-start.19 = (f32[256,128]{1,0:T(8,128)S(1)}, f32[256,128]{1,0:T(8,128)}, u32[]{:S(2)}) copy-start(f32[256,128]{1,0:T(8,128)} %noise.3) | copy-start | bytes 393220
  61.2 2.0 %copy-start.5 = (f32[32,256,128]{2,1,0:T(8,128)}, f32[32,256,128]{2,1,0:T(8,128)S(1)}, u32[]{:S(2)}) copy-start(f32[32,256,128]{2,1,0:T(8,128)S(1)} %shard_map.107.w) | copy-start | bytes 12582916
  63.3 37.2 %copy-start.16 = (bf16[2,256,256]{2,1,0:T(8,128)(2,1)S(1)}, bf16[2,256,256]{2,1,0:T(8,128)(2,1)}, u32[]{:S(2)}) copy-start(bf16[2,256,256]{2,1,0:T(8,128)(2,1)} %copy-done.15) | copy-start | bytes 786436
  63.3 37.2 %copy-start.18 = (bf16[2,256,256]{2,1,0:T(8,128)(2,1)S(1)}, bf16[2,256,256]{2,1,0:T(8,128)(2,1)}, u32[]{:S(2)}) copy-start(bf16[2,256,256]{2,1,0:T(8,128)(2,1)} %copy-done.17) | copy-start | bytes 786436
  63.3 37.2 %copy-start.21 = (bf16[256,256]{1,0:T(8,128)(2,1)S(1)}, bf16[256,256]{1,0:T(8,128)(2,1)}, u32[]{:S(2)}) copy-start(bf16[256,256]{1,0:T(8,128)(2,1)} %copy-done.20) | copy-start | bytes 393220
  91.3 2.0 %copy-start.2 = (f32[32,256,128]{2,1,0:T(8,128)}, f32[32,256,128]{2,1,0:T(8,128)S(1)}, u32[]{:S(2)}) copy-start(f32[32,256,128]{2,1,0:T(8,128)S(1)} %get-tuple-element.60.p) | copy-start | bytes 12582916
  93.2 1.2 copy-start.13
  94.4 23.7 %copy-start.28 = (bf16[4,256,256]{2,1,0:T(8,128)(2,1)S(1)}, bf16[4,256,256]{2,1,0:T(8,128)(2,1)}, u32[]{:S(2)}) copy-start(bf16[4,256,256]{2,1,0:T(8,128)(2,1)} %copy-done.27) | copy-start | bytes 1572868
  94.4 23.7 %collective-permute-start.5 = (f32[256,256]{1,0:T(8,128)S(1)}, f32[256,256]{1,0:T(8,128)S(1)}, u32[]{:S(2)}, u32[]{:S(2)}) collective-permute-start(f32[256,256]{1,0:T(8,128)S(1)} %get-tuple-element.75), channel_id=1, source_target_pairs={{1,0},{2,1},{3,2},{5,4},{6,5},{7,6},{9,8},{10,9},{11,10},{13,12},{... | collective-permute-start | bytes 786440 | tf_op jit(solution)/shard_map/ppermute | solution.py:539
  95.9 22.2 %collective-permute-start.4 = (f32[256,256]{1,0:T(8,128)S(1)}, f32[256,256]{1,0:T(8,128)S(1)}, u32[]{:S(2)}, u32[]{:S(2)}) collective-permute-start(f32[256,256]{1,0:T(8,128)S(1)} %get-tuple-element.76), channel_id=1, source_target_pairs={{0,1},{1,2},{2,3},{4,5},{5,6},{6,7},{8,9},{9,10},{10,11},{12,13},{... | collective-permute-start | bytes 786440 | tf_op jit(solution)/shard_map/ppermute | solution.py:539
  100.5 2.2 %copy-start.10 = (f32[32,256,128]{2,1,0:T(8,128)S(1)}, f32[32,256,128]{2,1,0:T(8,128)}, u32[]{:S(2)}) copy-start(f32[32,256,128]{2,1,0:T(8,128)} %get-tuple-element.54.z) | copy-start | bytes 12582916
  118.9 11.7 %collective-permute-start.7 = (f32[32,8,128]{2,1,0:T(8,128)S(1)}, f32[32,8,128]{2,1,0:T(8,128)S(1)}, u32[]{:S(2)}, u32[]{:S(2)}) collective-permute-start(f32[32,8,128]{2,1,0:T(8,128)S(1)} %get-tuple-element.79), channel_id=1, source_target_pairs={{4,0},{8,4},{12,8},{16,12},{20,16},{24,20},{28,24},{5,1},{9,5},{13... | collective-permute-start | bytes 393224 | tf_op jit(solution)/shard_map/ppermute | solution.py:539
  120.2 10.4 %collective-permute-start.6 = (f32[32,8,128]{2,1,0:T(8,128)S(1)}, f32[32,8,128]{2,1,0:T(8,128)S(1)}, u32[]{:S(2)}, u32[]{:S(2)}) collective-permute-start(f32[32,8,128]{2,1,0:T(8,128)S(1)} %get-tuple-element.80), channel_id=1, source_target_pairs={{0,4},{4,8},{8,12},{12,16},{16,20},{20,24},{24,28},{1,5},{5,9},{9,... | collective-permute-start | bytes 393224 | tf_op jit(solution)/shard_map/ppermute | solution.py:539
  123.7 6.9 %copy-start.7 = (f32[10,256,128]{2,1,0:T(8,128)S(1)}, f32[10,256,128]{2,1,0:T(8,128)}, u32[]{:S(2)}) copy-start(f32[10,256,128]{2,1,0:T(8,128)} %copy-done.6) | copy-start | bytes 3932164
  123.7 6.9 %copy-start.9 = (bf16[10,256,256]{2,1,0:T(8,128)(2,1)S(1)}, bf16[10,256,256]{2,1,0:T(8,128)(2,1)}, u32[]{:S(2)}) copy-start(bf16[10,256,256]{2,1,0:T(8,128)(2,1)} %copy-done.8) | copy-start | bytes 3932164
  123.7 6.9 %copy-start.14 = (f32[10,32,8,128]{3,2,1,0:T(8,128)S(1)}, f32[10,32,8,128]{3,2,1,0:T(8,128)}, u32[]{:S(2)}) copy-start(f32[10,32,8,128]{3,2,1,0:T(8,128)} %copy-done.13) | copy-start | bytes 3932164
  123.8 6.9 %copy-start.23 = (f32[2,10,8,128]{3,2,1,0:T(8,128)S(1)}, f32[2,10,8,128]{3,2,1,0:T(8,128)}, u32[]{:S(2)}) copy-start(f32[2,10,8,128]{3,2,1,0:T(8,128)} %copy-done.22) | copy-start | bytes 245764
  128.6 2.0 %copy-start.4 = (f32[32,256,128]{2,1,0:T(8,128)}, f32[32,256,128]{2,1,0:T(8,128)S(1)}, u32[]{:S(2)}) copy-start(f32[32,256,128]{2,1,0:T(8,128)S(1)} %shard_map.111.w) | copy-start | bytes 12582916
  130.6 30.3 %copy-start.1 = (f32[32,256,128]{2,1,0:T(8,128)S(1)}, f32[32,256,128]{2,1,0:T(8,128)}, u32[]{:S(2)}) copy-start(f32[32,256,128]{2,1,0:T(8,128)} %b.5) | copy-start | bytes 12582916
  130.6 30.3 %copy-start.3 = (f32[32,256,128]{2,1,0:T(8,128)S(1)}, f32[32,256,128]{2,1,0:T(8,128)}, u32[]{:S(2)}) copy-start(f32[32,256,128]{2,1,0:T(8,128)} %copy-done.2) | copy-start | bytes 12582916

commit v2 on v1

v2 whole, which is shorter than its diff:
```python
import functools

import jax
import jax.numpy as jnp
from jax import lax
from jax.experimental import pallas as pl
from jax.experimental.pallas import tpu as pltpu
from jax.sharding import PartitionSpec as P

REACH = 8
LANES = 128
GROUP = 8
F32 = jnp.float32
BF16 = jnp.bfloat16
HIGHEST = lax.Precision.HIGHEST


def iota(shape, dim):
    return lax.broadcasted_iota(jnp.int32, shape, dim)


def taper(distance):
    spread = jnp.abs(distance).astype(F32)
    value = (1.0 - spread / (REACH + 1)) * jnp.exp(-spread / 3.0)
    return jnp.where(jnp.abs(distance) <= REACH, value, 0.0)


def split(x):
    high = x.astype(BF16)
    return high, (x - high.astype(F32)).astype(BF16)


def pair(x):
    high, low = split(x)
    return jnp.concatenate([high, low], axis=1)


def dot(a, b):
    return jnp.dot(a, b, preferred_element_type=F32)


def dot_nt(a, b):
    return lax.dot_general(a, b, (((1,), (1,)), ((), ())), preferred_element_type=F32)


def halves(x):
    width = x.shape[1] // 2
    return x[:, :width] + x[:, width:]


def three(x):
    high = x.astype(BF16)
    rest = x - high.astype(F32)
    middle = rest.astype(BF16)
    low = (rest - middle.astype(F32)).astype(BF16)
    return jnp.concatenate([high, middle, low], axis=0)


def cut(x, axis):
    return [
        lax.slice_in_dim(x, start, start + LANES, axis=axis)
        for start in range(0, x.shape[axis], LANES)
    ]


def rows_of(g):
    return pl.ds(pl.multiple_of(g * GROUP, GROUP), GROUP)


def prepare_kernel(
    count, cell, offset, noise, obs, cov,
    sb, info, rank_out, sv, gv, ut, bounds, mix, mat, band_rows, band_cols, edge,
    table, sorted_rows,
):
    steps, slots = obs.shape
    tiles = slots // LANES
    rows = band_rows.shape[0]
    groups = rows // GROUP
    wide = steps * GROUP
    slot = iota((1, slots), 1)
    live = slot < count[0, 0]
    where_row = cell[...] // LANES
    where_col = cell[...] - where_row * LANES
    key = jnp.where(live, where_row, rows) * slots + slot
    key = key.astype(F32)
    total = jnp.zeros((1, slots), F32)
    for block in range(tiles):
        piece = key[:, block * LANES : (block + 1) * LANES]
        column = jnp.transpose(jnp.broadcast_to(piece, (LANES, LANES)))
        column = jnp.concatenate([column] * tiles, axis=1)
        less = jnp.where(column < key, 1.0, 0.0)
        total = total + jnp.sum(less, axis=0, keepdims=True)
    rank = total.astype(jnp.int32)
    rank_out[...] = rank
    lived = jnp.where(live, 1.0, 0.0)
    table[pl.ds(0, steps), :] = obs[...] * lived
    table[pl.ds(steps, 1), :] = where_row.astype(F32)
    table[pl.ds(steps + 1, 1), :] = where_col.astype(F32)
    table[pl.ds(steps + 2, 1), :] = offset[0:1, :]
    table[pl.ds(steps + 3, 1), :] = offset[1:2, :]
    table[pl.ds(steps + 4, 1), :] = noise[...]
    table[pl.ds(steps + 5, 1), :] = lived
    table[pl.ds(steps + 6, 2), :] = jnp.zeros((2, slots), F32)
    pieces = three(table[...])
    height = table.shape[0]

    def sort_block(block, carry):
        start = pl.multiple_of(block * LANES, LANES)
        order = (iota((LANES, slots), 0) + start == rank).astype(F32).astype(BF16)
        out = dot_nt(pieces, order)
        sorted_rows[:, pl.ds(start, LANES)] = (
            out[:height] + out[height : 2 * height] + out[2 * height :]
        )
        return carry

    lax.fori_loop(0, tiles, sort_block, 0)
    ordered_row = sorted_rows[pl.ds(steps, 1), :]
    ordered_live = sorted_rows[pl.ds(steps + 5, 1), :]
    first_row = (iota((groups, slots), 0) * GROUP).astype(F32)
    before = jnp.where(ordered_row < first_row - 1.0, ordered_live, 0.0)
    until = jnp.where(ordered_row < first_row + GROUP, ordered_live, 0.0)
    low = jnp.sum(before, axis=1, keepdims=True)
    high = jnp.sum(until, axis=1, keepdims=True)
    start_tile = jnp.where(high > low, jnp.floor(low * (1.0 / LANES)), float(tiles))
    stop_tile = jnp.where(high > low, jnp.floor((high - 1.0) * (1.0 / LANES)) + 1.0, 0.0)
    lane = iota((groups, LANES), 1)
    span = jnp.max(stop_tile - start_tile, axis=0, keepdims=True)
    bounds[...] = jnp.where(
        lane == 0, start_tile, jnp.where(lane == 1, stop_tile, span)
    ).astype(jnp.int32)
    extra = pl.ds(slots, 2 * LANES)
    sb[:, :, extra] = jnp.zeros((steps, GROUP, 2 * LANES), F32)
    info[:, :, extra] = jnp.zeros((2, GROUP, 2 * LANES), F32)
    sv[:, extra, :] = jnp.zeros((2, 2 * LANES, 2 * LANES), BF16)
    gv[:, extra] = jnp.zeros((3 * LANES, 2 * LANES), BF16)
    ut[:, extra] = jnp.zeros((rows, 2 * LANES), F32)
    for block in range(tiles):
        lanes = pl.ds(block * LANES, LANES)
        at_row = sorted_rows[pl.ds(steps, 1), lanes].astype(jnp.int32)
        at_col = sorted_rows[pl.ds(steps + 1, 1), lanes].astype(jnp.int32)
        along_row = sorted_rows[pl.ds(steps + 2, 1), lanes]
        along_col = sorted_rows[pl.ds(steps + 3, 1), lanes]
        row = iota((rows, LANES), 0)
        ut[:, lanes] = jnp.where(row == at_row, 1.0 - along_row, 0.0) + jnp.where(
            row == at_row + 1, along_row, 0.0
        )
        col = iota((LANES, LANES), 0)
        across = jnp.where(col == at_col, 1.0 - along_col, 0.0) + jnp.where(
            col == at_col + 1, along_col, 0.0
        )
        high_part, low_part = split(across)
        gv[:, lanes] = jnp.concatenate([high_part, high_part, low_part], axis=0)
        high_part, low_part = split(jnp.transpose(across))
        sv[0, lanes, :] = jnp.concatenate([high_part, low_part], axis=1)
        sv[1, lanes, :] = jnp.concatenate([high_part, jnp.zeros_like(low_part)], axis=1)
        for place in range(2):
            info[place, :, lanes] = jnp.broadcast_to(
                sorted_rows[pl.ds(steps + 4 + place, 1), lanes], (GROUP, LANES)
            )
        for step in range(steps):
            sb[step, :, lanes] = jnp.broadcast_to(
                sorted_rows[pl.ds(step, 1), lanes], (GROUP, LANES)
            )
    spread = (iota((wide, steps), 0) // GROUP == iota((wide, steps), 1)).astype(F32)
    spread_t = (iota((steps, wide), 1) // GROUP == iota((steps, wide), 0)).astype(F32)
    expanded = jnp.dot(
        jnp.dot(spread, cov[...], precision=HIGHEST, preferred_element_type=F32),
        spread_t,
        precision=HIGHEST,
        preferred_element_type=F32,
    )
    a = iota((wide, wide), 0)
    b = iota((wide, wide), 1)
    same = (a % GROUP) == (b % GROUP)
    high_part, low_part = split(jnp.where(same, expanded, 0.0))
    mix[...] = jnp.concatenate([high_part, high_part, low_part], axis=1)
    near = taper((b % GROUP) + REACH - (a % GROUP)) * expanded
    near = jnp.concatenate(
        [jnp.concatenate([x[GROUP:], x[:GROUP]], axis=0) for x in cut(near, 0)], axis=0
    )
    mat[0], mat[1] = split(near)
    far = taper(REACH + (a % GROUP) - (b % GROUP)) * expanded
    far = jnp.concatenate(
        [pltpu.roll(x, LANES - GROUP, 1) for x in cut(far, 1)], axis=1
    )
    mat[2], mat[3] = split(far)
    ra = iota((rows, rows), 0)
    rb = iota((rows, rows), 1)
    high_part, low_part = split(0.25 * taper(ra - rb))
    band_rows[...] = jnp.concatenate([high_part, high_part, low_part], axis=1)
    ca = iota((LANES, LANES), 0)
    cb = iota((LANES, LANES), 1)
    high_part, low_part = split(taper(ca - cb))
    band_cols[...] = jnp.concatenate(
        [
            jnp.concatenate([high_part, low_part], axis=1),
            jnp.concatenate([high_part, jnp.zeros_like(low_part)], axis=1),
        ],
        axis=0,
    )
    block_same = (a // GROUP) == (b // GROUP)
    above = 0.25 * taper((a % GROUP) + REACH - (b % GROUP))
    below = 0.25 * taper(REACH + (b % GROUP) - (a % GROUP))
    edge[0], edge[1] = split(jnp.where(block_same, above, 0.0))
    edge[2], edge[3] = split(jnp.where(block_same, below, 0.0))


def tile_lanes(index, count):
    return pl.ds(pl.multiple_of(index * LANES, LANES), count * LANES)


def spread_tiles(g, first, count, sb, ut, sv):
    steps = sb.shape[0]
    lanes = tile_lanes(first, count)
    scaled = sb[:, :, lanes] * ut[rows_of(g), lanes][None]
    left = pair(scaled.reshape(steps * GROUP, count * LANES))
    right = jnp.concatenate([sv[0, lanes, :], sv[1, lanes, :]], axis=0)
    return halves(dot(left, right)).reshape(steps, GROUP, LANES)


def scatter_all(base, z, strips, sb, ut, sv, bounds):
    groups = base.shape[1] // GROUP

    def run(g, carry):
        z[:, rows_of(g), :] = base[:, rows_of(g), :] + spread_tiles(g, bounds[g, 0], 2, sb, ut, sv)
        return carry

    lax.fori_loop(0, groups, run, 0, unroll=2)

    @pl.when(bounds[0, 2] > 2)
    def _():
        def crowded(g, carry):
            def more(index, inner):
                z[:, rows_of(g), :] += spread_tiles(g, index, 1, sb, ut, sv)
                return inner

            return lax.fori_loop(bounds[g, 0] + 2, bounds[g, 1], more, carry)

        lax.fori_loop(0, groups, crowded, 0)

    def pack(g, carry):
        pack_group(g, z, strips)
        return carry

    lax.fori_loop(0, groups, pack, 0, unroll=2)


def pack_group(g, z, strips):
    steps = z.shape[0]
    per = LANES // GROUP
    slot = iota((GROUP, LANES), 1) // GROUP
    for half in range(steps // per):
        left = jnp.zeros((GROUP, LANES), F32)
        right = jnp.zeros((GROUP, LANES), F32)
        for local in range(per):
            value = z[half * per + local, rows_of(g), :]
            if local:
                value = pltpu.roll(value, local * GROUP, 1)
            left = jnp.where(slot == local, value, left)
            right = jnp.where(slot == (local - 1) % per, value, right)
        lanes = pl.ds(half * LANES, LANES)
        strips[0, rows_of(g), lanes] = left
        strips[1, rows_of(g), lanes] = right


def unpack(sides, where_rows, count, step):
    per = LANES // GROUP
    half, local = step // per, step % per
    lane = iota((count, LANES), 1)
    lanes = pl.ds(half * LANES, LANES) if isinstance(step, int) else tile_lanes(half, 1)
    both = jnp.where(lane // GROUP == local, sides[0, where_rows, lanes], sides[1, where_rows, lanes])
    both = pltpu.roll(both, (LANES - local * GROUP) % LANES, 1)
    return jnp.where((lane < GROUP) | (lane >= LANES - GROUP), both, 0.0)


def scatter_kernel(bounds, base, sb, ut, sv, z, strips):
    scatter_all(base, z, strips, sb, ut, sv, bounds)


def first_filter_kernel(z, mix, band_cols, u, u_edges, y):
    steps, rows, cols = z.shape
    groups = rows // GROUP
    flat = (steps * GROUP, LANES)

    def across(quad, carry):
        parts = [z[:, rows_of(4 * quad + i), :].reshape(flat) for i in range(4)]
        value = halves(dot(pair(jnp.concatenate(parts, axis=0)), band_cols[...]))
        both = split(value)
        for i in range(4):
            for part in range(2):
                y[2 * quad + i // 2, part, :, pl.ds((i % 2) * LANES, LANES)] = both[part][
                    i * flat[0] : (i + 1) * flat[0]
                ]
        return carry

    lax.fori_loop(0, groups // 4, across, 0)

    def mixing(two, carry):
        right = jnp.concatenate([y[two, 0], y[two, 1], y[two, 0]], axis=0)
        out = dot(mix[...], right)
        u[:, rows_of(2 * two), :] = out[:, :LANES].reshape(steps, GROUP, LANES)
        u[:, rows_of(2 * two + 1), :] = out[:, LANES:].reshape(steps, GROUP, LANES)
        return carry

    lax.fori_loop(0, groups // 2, mixing, 0, unroll=2)
    u_edges[0] = u[:, pl.ds(0, GROUP), :]
    u_edges[1] = u[:, pl.ds(rows - GROUP, GROUP), :]


def second_filter_kernel(u, sides, band_rows, w):
    steps, rows, cols = u.shape

    def along(two, carry):
        one = split(u[2 * two])
        other = split(u[2 * two + 1])
        high = jnp.concatenate([one[0], other[0]], axis=1)
        low = jnp.concatenate([one[1], other[1]], axis=1)
        out = dot(band_rows[...], jnp.concatenate([high, low, high], axis=0))
        everything = pl.ds(0, rows)
        w[2 * two] = out[:, :LANES] + unpack(sides, everything, rows, 2 * two)
        w[2 * two + 1] = out[:, LANES:] + unpack(sides, everything, rows, 2 * two + 1)
        return carry

    lax.fori_loop(0, steps // 2, along, 0, unroll=2)


def edge_kernel(from_left, from_right, u_edges, mat, band_rows, sides, full_edges):
    steps = u_edges.shape[1]
    rows = from_left.shape[0]
    for side, source in ((0, from_left), (1, from_right)):
        high, low = split(source[...])
        value = dot(high, mat[2 * side]) + dot(low, mat[2 * side])
        value = value + dot(high, mat[2 * side + 1])
        sides[side] = value
    for which, start in ((0, 0), (1, rows - GROUP)):
        for step in range(steps):
            full_edges[which, step] = u_edges[which, step] + unpack(
                sides, pl.ds(start, GROUP), GROUP, step
            )
    for side in range(2):
        high, low = split(sides[side])
        sides[side] = dot(band_rows[...], jnp.concatenate([high, low, high], axis=0))


def fill_extra(extra, above, below, edge):
    steps = above.shape[0]
    flat = (steps * GROUP, LANES)
    for which, source in ((0, above), (1, below)):
        both = pair(source[...].reshape(flat))
        value = halves(dot(edge[2 * which], both)) + dot(edge[2 * which + 1], both[:, :LANES])
        extra[which] = value.reshape(steps, GROUP, LANES)
    extra[2] = jnp.zeros((steps, GROUP, LANES), F32)


def which_extra(g, groups):
    return jnp.where(g == 0, 0, jnp.where(g == groups - 1, 1, 2))


def gather_tiles(g, both, first, count, acc, ut, gv):
    steps = acc.shape[0]
    lanes = tile_lanes(first, count)
    out = dot(both, gv[:, lanes]).reshape(steps, GROUP, count * LANES)
    acc[:, :, lanes] += out * ut[rows_of(g), lanes][None]


def left_of(value):
    steps = value.shape[0]
    high, low = split(value.reshape(steps * GROUP, LANES))
    return jnp.concatenate([high, low, high], axis=1)


def whole(x):
    return jnp.sum(jnp.sum(x, axis=1, keepdims=True), axis=0, keepdims=True)


def fold(x):
    return jnp.sum(x, axis=0)


def image_one_kernel(
    bounds, w, above, below, edge, noise, b, sb, info, ut, gv, sv, rank,
    p, ps, z, strips, sums, unsorted, acc, extra, flat_rows,
):
    steps, rows, _ = w.shape
    groups = rows // GROUP
    slots = rank.shape[1]
    tiles = slots // LANES
    fill_extra(extra, above, below, edge)
    acc[...] = jnp.zeros_like(acc)

    def run(g, carry):
        value = w[:, rows_of(g), :] + extra[which_extra(g, groups)]
        mine = b[:, rows_of(g), :]
        image = value + noise[rows_of(g), :][None] * mine
        p[:, rows_of(g), :] = image
        gather_tiles(g, left_of(value), bounds[g, 0], 2, acc, ut, gv)
        return (
            carry[0] + fold(mine * mine),
            carry[1] + fold(mine * image),
            carry[2] + fold(image * image),
        )

    zero = jnp.zeros((GROUP, LANES), F32)
    carry = lax.fori_loop(0, groups, run, (zero,) * 3, unroll=2)

    @pl.when(bounds[0, 2] > 2)
    def _():
        def crowded(g, inner):
            value = w[:, rows_of(g), :] + extra[which_extra(g, groups)]

            def more(index, innermost):
                gather_tiles(g, left_of(value), index, 1, acc, ut, gv)
                return innermost

            return lax.fori_loop(bounds[g, 0] + 2, bounds[g, 1], more, inner)

        lax.fori_loop(0, groups, crowded, 0)

    def stations(index, carry):
        lanes = tile_lanes(index, 1)
        sampled = jnp.sum(acc[:, :, lanes], axis=1, keepdims=True)
        mine = sb[:, :, lanes]
        live = info[1, :, lanes][None]
        image = live * (sampled + info[0, :, lanes][None] * mine) + (1.0 - live) * mine
        ps[:, :, lanes] = image
        for step in range(steps):
            flat_rows[pl.ds(step, 1), lanes] = image[step, 0:1]
        part = 1.0 / GROUP
        return (
            carry[0] + part * fold(mine * mine),
            carry[1] + part * fold(mine * image),
            carry[2] + part * fold(image * image),
        )

    carry = lax.fori_loop(0, tiles, stations, carry)
    ps[:, :, pl.ds(slots, 2 * LANES)] = jnp.zeros((steps, GROUP, 2 * LANES), F32)
    bb, bp, pp = (whole(x) for x in carry)
    lane = iota((GROUP, LANES), 1)
    value = jnp.where(lane == 0, bb / bp, 0.0)
    value = jnp.where(lane == 1, bb, value)
    value = jnp.where(lane == 2, bp, value)
    value = jnp.where(lane == 3, pp, value)
    sums[...] = value
    scatter_all(p, z, strips, ps, ut, sv, bounds)
    pieces = three(flat_rows[...])

    def unsort_block(block, carry):
        lanes = tile_lanes(block, 1)
        order = (iota((slots, LANES), 0) == rank[:, lanes]).astype(F32).astype(BF16)
        out = dot(pieces, order)
        unsorted[:, lanes] = out[:steps] + out[steps : 2 * steps] + out[2 * steps :]
        return carry

    lax.fori_loop(0, tiles, unsort_block, 0)


def image_two_kernel(
    w, above, below, edge, noise, b, p, z_first, z, sb, ps, info, sums,
    q, message, extra,
):
    steps, rows, _ = w.shape
    groups = rows // GROUP
    tiles = sb.shape[2] // LANES - 2
    fill_extra(extra, above, below, edge)
    shift = jnp.broadcast_to(sums[0:1, 0:1], (GROUP, LANES))[None]

    def run(g, carry):
        here = rows_of(g)
        value = w[:, here, :] + extra[which_extra(g, groups)]
        mine = p[:, here, :]
        scaled = noise[here, :][None] * mine
        q[:, here, :] = value + scaled
        residual = b[:, here, :] - shift * mine
        second = z[:, here, :]
        moved = z_first[:, here, :] - shift * second
        return (
            carry[0] + fold(residual * residual),
            carry[1] + fold(moved * value + residual * scaled),
            carry[2] + fold(second * value + mine * scaled),
        )

    zero = jnp.zeros((GROUP, LANES), F32)
    carry = lax.fori_loop(0, groups, run, (zero,) * 3)

    def stations(index, carry):
        lanes = tile_lanes(index, 1)
        mine = ps[:, :, lanes]
        live = info[1, :, lanes]
        scaled = (live * info[0, :, lanes] + (1.0 - live))[None] * mine
        residual = sb[:, :, lanes] - shift * mine
        part = 1.0 / GROUP
        return (
            carry[0] + part * fold(residual * residual),
            carry[1] + part * fold(residual * scaled),
            carry[2] + part * fold(mine * scaled),
        )

    carry = lax.fori_loop(0, tiles, stations, carry)
    lane = iota((1, LANES), 1)
    value = jnp.where(lane < 4, sums[0:1, :], 0.0)
    for place, x in enumerate(carry):
        value = jnp.where(lane == 4 + place, whole(x), value)
    message[...] = jnp.broadcast_to(value, message.shape)


def final_kernel(received, b, p, q, obs, unsorted, count, solution_out, residual_out, station_out):
    everything = received[...]

    def column(index):
        return everything[:, index : index + 1]

    def total(x):
        return jnp.sum(x, axis=0, keepdims=True)

    shift, bb, bp, pp = (column(i) for i in range(4))
    rr, rq, pq = (column(i) for i in range(4, 7))
    norm = total(bb)
    alpha = norm / total(bp)
    delta = shift - alpha
    rp = bp - shift * pp
    ru = rp - shift * rq
    pu = pp - shift * pq
    norm_next = total(rr + 2.0 * delta * rp + delta * delta * pp)
    energy = total(ru + delta * (rq + pu) + delta * delta * pq)
    beta = norm_next / norm
    alpha_next = norm_next / (energy - beta * norm_next / alpha)
    along = alpha + alpha_next * (1.0 + beta)
    twice = alpha_next * alpha
    part = solution_out.shape[0]
    rows = solution_out.shape[1]
    start = pl.program_id(0) * part
    chunk = 64
    wide_along = jnp.broadcast_to(along, (chunk, LANES))
    wide_twice = jnp.broadcast_to(twice, (chunk, LANES))
    pieces = rows // chunk

    def run(index, carry):
        step = index // pieces
        here = pl.ds(pl.multiple_of((index % pieces) * chunk, chunk), chunk)
        first = b[start + step, here, :]
        second = p[start + step, here, :]
        solution_out[step, here, :] = wide_along * first - wide_twice * second
        residual_out[step, here, :] = (
            first - wide_along * second + wide_twice * q[start + step, here, :]
        )
        return carry

    lax.fori_loop(0, part * pieces, run, 0, unroll=2)

    @pl.when(pl.program_id(0) == 0)
    def _():
        steps, slots = obs.shape
        live = iota((steps, slots), 1) < count[0, 0]
        own = jnp.where(live, obs[...], 0.0)
        station_out[...] = along * own - twice * unsorted[...]


VMEM = pl.BlockSpec(memory_space=pltpu.VMEM)
SMEM = pl.BlockSpec(memory_space=pltpu.SMEM)


def call(kernel, outs, ins, operands, scratch=(), flops=10**9, moved=10**7, limit=8, **extra):
    return pl.pallas_call(
        kernel,
        out_shape=outs,
        in_specs=ins,
        out_specs=[VMEM] * len(outs),
        scratch_shapes=list(scratch),
        compiler_params=pltpu.CompilerParams(vmem_limit_bytes=limit * 2**20),
        cost_estimate=pl.CostEstimate(flops=flops, bytes_accessed=moved, transcendentals=0),
        **extra,
    )(*operands)


def exchange(first, second, axis):
    count = lax.axis_size(axis)
    forward = [(i, i + 1) for i in range(count - 1)]
    backward = [(target, source) for source, target in forward]
    return lax.ppermute(first, axis, forward), lax.ppermute(second, axis, backward)


def body(
    grid_obs, grid_noise, station_obs, station_noise, station_offset, station_cell,
    station_count, time_cov,
):
    steps, rows, cols = grid_obs.shape
    slots = station_obs.shape[3]
    wide = steps * GROUP
    groups = rows // GROUP
    lanes = slots + 2 * LANES
    devices = lax.axis_size("row") * lax.axis_size("col")
    obs = station_obs.reshape(steps, slots)
    shape = jax.ShapeDtypeStruct
    field = shape((steps, rows, cols), F32)
    rim = shape((2, steps, GROUP, cols), F32)
    strips_shape = shape((2, rows, wide), F32)
    station_field = shape((steps, GROUP, lanes), F32)
    extra = pltpu.VMEM((3, steps, GROUP, LANES), F32)
    sb, info, rank, sv, gv, ut, bounds, mix, mat, band_rows, band_cols, edge = call(
        prepare_kernel,
        [
            station_field,
            shape((2, GROUP, lanes), F32),
            shape((1, slots), jnp.int32),
            shape((2, lanes, 2 * LANES), BF16),
            shape((3 * LANES, lanes), BF16),
            shape((rows, lanes), F32),
            shape((groups, LANES), jnp.int32),
            shape((wide, 3 * wide), BF16),
            shape((4, wide, wide), BF16),
            shape((rows, 3 * rows), BF16),
            shape((2 * LANES, 2 * LANES), BF16),
            shape((4, wide, wide), BF16),
        ],
        [SMEM] + [VMEM] * 5,
        (
            station_count,
            station_cell.reshape(1, slots),
            station_offset.reshape(2, slots),
            station_noise.reshape(1, slots),
            obs,
            time_cov,
        ),
        [pltpu.VMEM((steps + 8, slots), F32), pltpu.VMEM((steps + 8, slots), F32)],
    )
    z_first, strips = call(
        scatter_kernel,
        [field, strips_shape],
        [SMEM] + [VMEM] * 4,
        (bounds, grid_obs, sb, ut, sv),
        limit=4,
    )

    def smooth(z, strips):
        from_left, from_right = exchange(strips[1], strips[0], "col")
        u, u_edges = call(
            first_filter_kernel,
            [field, rim],
            [VMEM] * 3,
            (z, mix, band_cols),
            [pltpu.VMEM((groups // 2, 2, wide, 2 * LANES), BF16)],
        )
        sides, full_edges = call(
            edge_kernel,
            [strips_shape, rim],
            [VMEM] * 5,
            (from_left, from_right, u_edges, mat, band_rows),
            limit=4,
        )
        above, below = exchange(full_edges[1], full_edges[0], "row")
        (w,) = call(
            second_filter_kernel, [field], [VMEM] * 3, (u, sides, band_rows), limit=4
        )
        return w, above, below

    w, above, below = smooth(z_first, strips)
    p, ps, z, strips, sums, unsorted = call(
        image_one_kernel,
        [field, station_field, field, strips_shape, shape((GROUP, LANES), F32), shape((steps, slots), F32)],
        [SMEM] + [VMEM] * 12,
        (bounds, w, above, below, edge, grid_noise, grid_obs, sb, info, ut, gv, sv, rank),
        [pltpu.VMEM((steps, GROUP, lanes), F32), extra, pltpu.VMEM((steps, slots), F32)],
    )
    w, above, below = smooth(z, strips)
    q, message = call(
        image_two_kernel,
        [field, shape((devices, LANES), F32)],
        [VMEM] * 13,
        (w, above, below, edge, grid_noise, grid_obs, p, z_first, z, sb, ps, info, sums),
        [extra],
        limit=4,
    )
    received = lax.all_to_all(message, ("row", "col"), 0, 0, tiled=True)
    parts = 8
    block = pl.BlockSpec((steps // parts, rows, cols), lambda i: (i, 0, 0))
    solution_grid, residual_grid, solution_stations = pl.pallas_call(
        final_kernel,
        grid=(parts,),
        out_shape=[field, field, shape((steps, slots), F32)],
        in_specs=[VMEM] * 6 + [SMEM],
        out_specs=[block, block, pl.BlockSpec((steps, slots), lambda i: (0, 0))],
        compiler_params=pltpu.CompilerParams(vmem_limit_bytes=6 * 2**20),
    )(received, grid_obs, p, q, obs, unsorted, station_count)
    return solution_grid, solution_stations.reshape(steps, 1, 1, slots), residual_grid


def solution(mesh):
    placed = (
        P(None, "row", "col"),
        P("row", "col"),
        P(None, "row", "col", None),
        P("row", "col", None),
        P(None, "row", "col", None),
        P("row", "col", None),
        P("row", "col"),
        P(),
    )
    return jax.shard_map(
        body,
        mesh=mesh,
        in_specs=placed,
        out_specs=(P(None, "row", "col"), P(None, "row", "col", None), P(None, "row", "col")),
        check_vma=False,
    )
```

time: 171 us -> 109 us (0.64)
  Pallas kernels: 111 us -> 62.3 us
  local copies, waits for them, and re-layouts: 21.8 us -> 6.82 us
  blocking collectives: 13.4 us -> 15.5 us
    pallas_call x10, Pallas kernels: 103 us -> 54.2 us  [call(): pl.pallas_call(kernel, out_shape=outs, in_specs=ins, out_specs=[VMEM] * l...]
    unnamed x61 -> x15, local copies, waits for them, and re-layouts: 21.6 us -> 6.71 us
    all_to_all x1, blocking collectives: 13.4 us -> 15.5 us  [body(): received = lax.all_to_all(message, ('row', 'col'), 0, 0, tiled=True)]
  transfers between devices with their start and end apart: 8 -> 8, of which waited for: 0 -> 1; matrix products, arithmetic and copies ran while one was open for 0% -> 0% of each run, Pallas kernels for 24% -> 16%
where the time goes in v2:
time: 109 us
  Pallas kernels  62.3 us (57%)
  starting transfers between devices  21.8 us (20%)
  blocking collectives  15.5 us (14%)
  local copies, waits for them, and re-layouts  6.82 us (6%)
  between operations  1.54 us (1%)
    pallas_call x10, Pallas kernels, call(): pl.pallas_call(kernel, out_shape=outs, in_specs=ins, out_specs=[VMEM] * l...  54.2 us
    ppermute x4, starting transfers between devices, exchange(): lax.ppermute(first, axis, forward)  16.7 us
    all_to_all x1, blocking collectives, body(): received = lax.all_to_all(message, ('row', 'col'), 0, 0, tiled=True)  15.5 us
    pallas_call x1, Pallas kernels, body(): pl.pallas_call(final_kernel, grid=(parts,), out_shape=[field, field, shap...  8.06 us
    unnamed x15, local copies, waits for them, and re-layouts  6.71 us
    ppermute x4, starting transfers between devices, exchange(): lax.ppermute(second, axis, backward)  5.17 us
  transfers between devices with their start and end apart: 8, of which 1 were waited for; matrix products, arithmetic and copies ran while one was open for 0% of the time, Pallas kernels for 16%

profile of v2, /device:TPU:0, one launch (start us, length us, event | category | flops | bytes accessed | tf_op | source)
XLA Modules:
  0.0 108.8 jit_solution(13633875287698372817)
XLA Ops:
  1.3 0.7 copy.19
  2.0 0.9 copy.18
  2.9 0.0 copy-start.3
  2.9 0.7 copy-done.3
  3.6 0.0 copy-start.4
  3.6 0.7 copy-done.4
  4.3 0.0 copy-start.5
  4.3 0.7 copy-done.5
  5.0 4.2 %shard_map.103 = (f32[32,8,1280]{2,1,0:T(8,128)S(1)}, f32[2,8,1280]{2,1,0:T(8,128)S(1)}, s32[1,1024]{1,0:T(1,128)S(1)}, bf16[2,1280,256]{2,1,0:T(8,128)(2,1)S(1)...) custom-call(s32[1,1]{1,0:T(1,128)S(6)} %copy.20.count, ...), custom_call_target="tpu_custom_call" | custom-call | flops 1000000000 | bytes 10000000 | tf_op jit(solution)/shard_map/pallas_call | solution.py:563
  9.2 0.0 copy-start
  9.2 2.2 %copy-done = f32[32,256,128]{2,1,0:T(8,128)S(1)} copy-done((f32[32,256,128]{2,1,0:T(8,128)S(1)}, f32[32,256,128]{2,1,0:T(8,128)}, u32[]{:S(2)}) %copy-start) | copy-done | bytes 4194328
  11.4 8.0 %shard_map.104 = (f32[32,256,128]{2,1,0:T(8,128)S(1)}, f32[2,256,256]{2,1,0:T(8,128)S(1)}) custom-call(s32[32,128]{1,0:T(8,128)S(1)} %get-tuple-element.36.bounds, f32[32,256,128]{2,1,0:T(8,128)S(1)} %copy-done, f32[32,8,1280]{2,1,0:T(8,128)S(1)} %get-tuple-element.37.sb, f32[256,1280]{1,0:T(8,128)S(1)} %get-tuple-element.38.ut, ...), custom_call_target="tpu_custom_call" | custom-call | flops 1000000000 | bytes 10000000 | tf_op jit(solution)/shard_map/pallas_call | solution.py:563
  19.5 1.3 %collective-permute-start.1 = (f32[256,256]{1,0:T(8,128)S(1)}, f32[256,256]{1,0:T(8,128)S(1)}, u32[]{:S(2)}, u32[]{:S(2)}) collective-permute-start(f32[256,256]{1,0:T(8,128)S(1)} %get-tuple-element.77), channel_id=1, source_target_pairs={{1,0},{2,1},{3,2},{5,4},{6,5},{7,6},{9,8},{10,9},{11,10},{13,12},{... | collective-permute-start | bytes 786440 | tf_op jit(solution)/shard_map/ppermute | solution.py:579
  20.8 5.6 %collective-permute-start = (f32[256,256]{1,0:T(8,128)S(1)}, f32[256,256]{1,0:T(8,128)S(1)}, u32[]{:S(2)}, u32[]{:S(2)}) collective-permute-start(f32[256,256]{1,0:T(8,128)S(1)} %get-tuple-element.78), channel_id=1, source_target_pairs={{0,1},{1,2},{2,3},{4,5},{5,6},{6,7},{8,9},{9,10},{10,11},{12,13},{... | collective-permute-start | bytes 786440 | tf_op jit(solution)/shard_map/ppermute | solution.py:579
  26.4 5.5 %shard_map.105 = (f32[32,256,128]{2,1,0:T(8,128)S(1)}, f32[2,32,8,128]{3,2,1,0:T(8,128)S(1)}) custom-call(f32[32,256,128]{2,1,0:T(8,128)S(1)} %get-tuple-element.40.z.z_first, bf16[256,768]{1,0:T(8,128)(2,1)S(1)} %get-tuple-element.41.mix, bf16[256,256]{1,0:T(8,128)(2,1)S(1)} %get-tuple-element.42.band_cols), custom_call_target="tpu_custom_call" | custom-call | flops 1000000000 | bytes 10000000 | tf_op jit(solution)/shard_map/pallas_call | solution.py:563
  31.9 0.0 collective-permute-done.1.from_right
  31.9 0.0 collective-permute-done.from_left
  31.9 0.7 shard_map.106
  32.7 1.3 %collective-permute-start.3 = (f32[32,8,128]{2,1,0:T(8,128)S(1)}, f32[32,8,128]{2,1,0:T(8,128)S(1)}, u32[]{:S(2)}, u32[]{:S(2)}) collective-permute-start(f32[32,8,128]{2,1,0:T(8,128)S(1)} %get-tuple-element.81), channel_id=1, source_target_pairs={{4,0},{8,4},{12,8},{16,12},{20,16},{24,20},{28,24},{5,1},{9,5},{13... | collective-permute-start | bytes 393224 | tf_op jit(solution)/shard_map/ppermute | solution.py:579
  34.0 3.0 %collective-permute-start.2 = (f32[32,8,128]{2,1,0:T(8,128)S(1)}, f32[32,8,128]{2,1,0:T(8,128)S(1)}, u32[]{:S(2)}, u32[]{:S(2)}) collective-permute-start(f32[32,8,128]{2,1,0:T(8,128)S(1)} %get-tuple-element.82), channel_id=1, source_target_pairs={{0,4},{4,8},{8,12},{12,16},{16,20},{20,24},{24,28},{1,5},{5,9},{9,... | collective-permute-start | bytes 393224 | tf_op jit(solution)/shard_map/ppermute | solution.py:579
  37.0 0.0 copy-start.1
  37.0 0.0 copy-start.2
  37.1 3.3 %shard_map.107.w = f32[32,256,128]{2,1,0:T(8,128)S(1)} custom-call(f32[32,256,128]{2,1,0:T(8,128)S(1)} %get-tuple-element.43.u, f32[2,256,256]{2,1,0:T(8,128)S(1)} %get-tuple-element.48.sides, bf16[256,768]{1,0:T(8,128)(2,1)S(1)} %get-tuple-element.47.band_rows), custom_call_target="tpu_custom_call" | custom-call | flops 1000000000 | bytes 10000000 | tf_op jit(solution)/shard_map/pallas_call | solution.py:563
  40.3 0.0 collective-permute-done.3.below
  40.3 0.0 collective-permute-done.2.above
  40.3 0.0 copy-done.1
  40.4 0.0 copy-done.2
  40.4 16.6 %shard_map.108 = (f32[32,256,128]{2,1,0:T(8,128)S(1)}, f32[32,8,1280]{2,1,0:T(8,128)S(1)}, f32[32,256,128]{2,1,0:T(8,128)S(1)}, f32[2,256,256]{2,1,0:T(8,128)S(1...) custom-call(s32[32,128]{1,0:T(8,128)S(1)} %get-tuple-element.36.bounds, f32[32,256,128]{2,1,0:T(8,128)S(1)} %shard_map.107.w, ...), custom_call_target="tpu_custom_call" | custom-call | flops 1000000000 | bytes 10000000 | tf_op jit(solution)/shard_map/pallas_call | solution.py:563
  57.0 1.3 %collective-permute-start.5 = (f32[256,256]{1,0:T(8,128)S(1)}, f32[256,256]{1,0:T(8,128)S(1)}, u32[]{:S(2)}, u32[]{:S(2)}) collective-permute-start(f32[256,256]{1,0:T(8,128)S(1)} %get-tuple-element.75), channel_id=1, source_target_pairs={{1,0},{2,1},{3,2},{5,4},{6,5},{7,6},{9,8},{10,9},{11,10},{13,12},{... | collective-permute-start | bytes 786440 | tf_op jit(solution)/shard_map/ppermute | solution.py:579
  58.3 5.0 %collective-permute-start.4 = (f32[256,256]{1,0:T(8,128)S(1)}, f32[256,256]{1,0:T(8,128)S(1)}, u32[]{:S(2)}, u32[]{:S(2)}) collective-permute-start(f32[256,256]{1,0:T(8,128)S(1)} %get-tuple-element.76), channel_id=1, source_target_pairs={{0,1},{1,2},{2,3},{4,5},{5,6},{6,7},{8,9},{9,10},{10,11},{12,13},{... | collective-permute-start | bytes 786440 | tf_op jit(solution)/shard_map/ppermute | solution.py:579
  63.3 5.5 %shard_map.109 = (f32[32,256,128]{2,1,0:T(8,128)S(1)}, f32[2,32,8,128]{3,2,1,0:T(8,128)S(1)}) custom-call(f32[32,256,128]{2,1,0:T(8,128)S(1)} %get-tuple-element.54.z, bf16[256,768]{1,0:T(8,128)(2,1)S(1)} %get-tuple-element.41.mix, bf16[256,256]{1,0:T(8,128)(2,1)S(1)} %get-tuple-element.42.band_cols), custom_call_target="tpu_custom_call" | custom-call | flops 1000000000 | bytes 10000000 | tf_op jit(solution)/shard_map/pallas_call | solution.py:563
  68.9 0.0 collective-permute-done.5.from_right
  68.9 0.8 collective-permute-done.4.from_left
  69.7 0.7 shard_map.110
  70.5 1.3 %collective-permute-start.7 = (f32[32,8,128]{2,1,0:T(8,128)S(1)}, f32[32,8,128]{2,1,0:T(8,128)S(1)}, u32[]{:S(2)}, u32[]{:S(2)}) collective-permute-start(f32[32,8,128]{2,1,0:T(8,128)S(1)} %get-tuple-element.79), channel_id=1, source_target_pairs={{4,0},{8,4},{12,8},{16,12},{20,16},{24,20},{28,24},{5,1},{9,5},{13... | collective-permute-start | bytes 393224 | tf_op jit(solution)/shard_map/ppermute | solution.py:579
  71.8 3.0 %collective-permute-start.6 = (f32[32,8,128]{2,1,0:T(8,128)S(1)}, f32[32,8,128]{2,1,0:T(8,128)S(1)}, u32[]{:S(2)}, u32[]{:S(2)}) collective-permute-start(f32[32,8,128]{2,1,0:T(8,128)S(1)} %get-tuple-element.80), channel_id=1, source_target_pairs={{0,4},{4,8},{8,12},{12,16},{16,20},{20,24},{24,28},{1,5},{5,9},{9,... | collective-permute-start | bytes 393224 | tf_op jit(solution)/shard_map/ppermute | solution.py:579
  74.8 3.2 %shard_map.111.w = f32[32,256,128]{2,1,0:T(8,128)S(1)} custom-call(f32[32,256,128]{2,1,0:T(8,128)S(1)} %get-tuple-element.55.u, f32[2,256,256]{2,1,0:T(8,128)S(1)} %get-tuple-element.58.sides, bf16[256,768]{1,0:T(8,128)(2,1)S(1)} %get-tuple-element.47.band_rows), custom_call_target="tpu_custom_call" | custom-call | flops 1000000000 | bytes 10000000 | tf_op jit(solution)/shard_map/pallas_call | solution.py:563
  78.0 0.0 collective-permute-done.7.below
  78.0 0.0 collective-permute-done.6.above
  78.0 6.4 %shard_map.112 = (f32[32,256,128]{2,1,0:T(8,128)S(1)}, f32[32,128]{1,0:T(8,128)S(1)}) custom-call(f32[32,256,128]{2,1,0:T(8,128)S(1)} %shard_map.111.w, f32[32,8,128]{2,1,0:T(8,128)S(1)} %collective-permute-done.6.above, f32[32,8,128]{2,1,0:T(8,128)S(1)} %collective-permute-done.7.below, bf16[4,256,256]{2,1,0:T(8,128)(2,1)S(1)} %get-tuple-element.50.edge, ...), custom_call_target="tpu_custom_call" | custom-call | flops 1000000000 | bytes 10000000 | tf_op jit(solution)/shard_map/pallas_call | solution.py:563
  84.4 15.5 %all_to_all.11 = f32[32,1,128]{2,1,0:T(1,128)S(1)} all-to-all(f32[32,1,128]{2,1,0:T(1,128)S(1)} %bitcast.33), channel_id=1, replica_groups=mesh['row'=8,'col'=4] {'row','col'}, dimensions={0} | all-to-all | bytes 32768 | tf_op jit(solution)/shard_map/all_to_all | solution.py:673
  100.0 8.1 %shard_map.113 = (f32[32,256,128]{2,1,0:T(8,128)}, f32[32,256,128]{2,1,0:T(8,128)}, f32[32,1024]{1,0:T(8,128)S(1)}) custom-call(f32[32,128]{1,0:T(8,128)S(1)} %bitcast.32, f32[32,256,128]{2,1,0:T(8,128)S(1)} %copy-done.1, f32[32,256,128]{2,1,0:T(8,128)S(1)} %get-tuple-element.60.p, f32[32,256,128]{2,1,0:T(8,128)S(1)} %get-tuple-element.64.q, ...), custom_call_target="tpu_custom_call" | custom-call | tf_op jit(solution)/shard_map/pallas_call | solution.py:676
  108.0 0.8 copy.13
  (4 shorter events, 0.1 us)
Async XLA Ops:
  2.9 0.7 copy-start.3
  3.6 0.7 copy-start.4
  4.3 0.7 copy-start.5
  9.2 2.2 %copy-start = (f32[32,256,128]{2,1,0:T(8,128)S(1)}, f32[32,256,128]{2,1,0:T(8,128)}, u32[]{:S(2)}) copy-start(f32[32,256,128]{2,1,0:T(8,128)} %b.5) | copy-start | bytes 12582916
  19.5 12.4 %collective-permute-start.1 = (f32[256,256]{1,0:T(8,128)S(1)}, f32[256,256]{1,0:T(8,128)S(1)}, u32[]{:S(2)}, u32[]{:S(2)}) collective-permute-start(f32[256,256]{1,0:T(8,128)S(1)} %get-tuple-element.77), channel_id=1, source_target_pairs={{1,0},{2,1},{3,2},{5,4},{6,5},{7,6},{9,8},{10,9},{11,10},{13,12},{... | collective-permute-start | bytes 786440 | tf_op jit(solution)/shard_map/ppermute | solution.py:579
  20.8 11.1 %collective-permute-start = (f32[256,256]{1,0:T(8,128)S(1)}, f32[256,256]{1,0:T(8,128)S(1)}, u32[]{:S(2)}, u32[]{:S(2)}) collective-permute-start(f32[256,256]{1,0:T(8,128)S(1)} %get-tuple-element.78), channel_id=1, source_target_pairs={{0,1},{1,2},{2,3},{4,5},{5,6},{6,7},{8,9},{9,10},{10,11},{12,13},{... | collective-permute-start | bytes 786440 | tf_op jit(solution)/shard_map/ppermute | solution.py:579
  32.7 7.6 %collective-permute-start.3 = (f32[32,8,128]{2,1,0:T(8,128)S(1)}, f32[32,8,128]{2,1,0:T(8,128)S(1)}, u32[]{:S(2)}, u32[]{:S(2)}) collective-permute-start(f32[32,8,128]{2,1,0:T(8,128)S(1)} %get-tuple-element.81), channel_id=1, source_target_pairs={{4,0},{8,4},{12,8},{16,12},{20,16},{24,20},{28,24},{5,1},{9,5},{13... | collective-permute-start | bytes 393224 | tf_op jit(solution)/shard_map/ppermute | solution.py:579
  34.0 6.3 %collective-permute-start.2 = (f32[32,8,128]{2,1,0:T(8,128)S(1)}, f32[32,8,128]{2,1,0:T(8,128)S(1)}, u32[]{:S(2)}, u32[]{:S(2)}) collective-permute-start(f32[32,8,128]{2,1,0:T(8,128)S(1)} %get-tuple-element.82), channel_id=1, source_target_pairs={{0,4},{4,8},{8,12},{12,16},{16,20},{20,24},{24,28},{1,5},{5,9},{9,... | collective-permute-start | bytes 393224 | tf_op jit(solution)/shard_map/ppermute | solution.py:579
  37.0 3.3 %copy-start.1 = (f32[32,256,128]{2,1,0:T(8,128)S(1)}, f32[32,256,128]{2,1,0:T(8,128)}, u32[]{:S(2)}) copy-start(f32[32,256,128]{2,1,0:T(8,128)} %b.5) | copy-start | bytes 12582916
  37.0 3.3 %copy-start.2 = (f32[256,128]{1,0:T(8,128)S(1)}, f32[256,128]{1,0:T(8,128)}, u32[]{:S(2)}) copy-start(f32[256,128]{1,0:T(8,128)} %noise.3) | copy-start | bytes 393220
  57.0 11.8 %collective-permute-start.5 = (f32[256,256]{1,0:T(8,128)S(1)}, f32[256,256]{1,0:T(8,128)S(1)}, u32[]{:S(2)}, u32[]{:S(2)}) collective-permute-start(f32[256,256]{1,0:T(8,128)S(1)} %get-tuple-element.75), channel_id=1, source_target_pairs={{1,0},{2,1},{3,2},{5,4},{6,5},{7,6},{9,8},{10,9},{11,10},{13,12},{... | collective-permute-start | bytes 786440 | tf_op jit(solution)/shard_map/ppermute | solution.py:579
  58.3 11.4 %collective-permute-start.4 = (f32[256,256]{1,0:T(8,128)S(1)}, f32[256,256]{1,0:T(8,128)S(1)}, u32[]{:S(2)}, u32[]{:S(2)}) collective-permute-start(f32[256,256]{1,0:T(8,128)S(1)} %get-tuple-element.76), channel_id=1, source_target_pairs={{0,1},{1,2},{2,3},{4,5},{5,6},{6,7},{8,9},{9,10},{10,11},{12,13},{... | collective-permute-start | bytes 786440 | tf_op jit(solution)/shard_map/ppermute | solution.py:579
  70.5 7.6 %collective-permute-start.7 = (f32[32,8,128]{2,1,0:T(8,128)S(1)}, f32[32,8,128]{2,1,0:T(8,128)S(1)}, u32[]{:S(2)}, u32[]{:S(2)}) collective-permute-start(f32[32,8,128]{2,1,0:T(8,128)S(1)} %get-tuple-element.79), channel_id=1, source_target_pairs={{4,0},{8,4},{12,8},{16,12},{20,16},{24,20},{28,24},{5,1},{9,5},{13... | collective-permute-start | bytes 393224 | tf_op jit(solution)/shard_map/ppermute | solution.py:579
  71.8 6.3 %collective-permute-start.6 = (f32[32,8,128]{2,1,0:T(8,128)S(1)}, f32[32,8,128]{2,1,0:T(8,128)S(1)}, u32[]{:S(2)}, u32[]{:S(2)}) collective-permute-start(f32[32,8,128]{2,1,0:T(8,128)S(1)} %get-tuple-element.80), channel_id=1, source_target_pairs={{0,4},{4,8},{8,12},{12,16},{16,20},{20,24},{24,28},{1,5},{5,9},{9,... | collective-permute-start | bytes 393224 | tf_op jit(solution)/shard_map/ppermute | solution.py:579

commit v3 on v2

--- a/solution.py
+++ b/solution.py
@@ -68,19 +68,31 @@
 
 
 def prepare_kernel(
-    count, cell, offset, noise, obs, cov,
-    sb, info, rank_out, sv, gv, ut, bounds, mix, mat, band_rows, band_cols, edge,
-    table, sorted_rows,
+    count, cell_any, offset_any, noise_any, obs_any, base_any,
+    base, z, strips, sb, info, rank_out, own, sv, gv, ut, bounds,
+    cell_v, offset_v, noise_v, obs_v, bounds_v, table, sorted_rows, copies,
 ):
-    steps, slots = obs.shape
+    base_copy = pltpu.make_async_copy(base_any, base, copies.at[0])
+    base_copy.start()
+    small = [
+        pltpu.make_async_copy(source, target, copies.at[1 + place])
+        for place, (source, target) in enumerate(
+            ((cell_any, cell_v), (offset_any, offset_v), (noise_any, noise_v), (obs_any, obs_v))
+        )
+    ]
+    for copy in small:
+        copy.start()
+    for copy in small:
+        copy.wait()
+    cell, noise = cell_v[0], noise_v[0]
+    steps, slots = own.shape
     tiles = slots // LANES
-    rows = band_rows.shape[0]
+    rows = base.shape[1]
     groups = rows // GROUP
-    wide = steps * GROUP
     slot = iota((1, slots), 1)
     live = slot < count[0, 0]
-    where_row = cell[...] // LANES
-    where_col = cell[...] - where_row * LANES
+    where_row = cell // LANES
+    where_col = cell - where_row * LANES
     key = jnp.where(live, where_row, rows) * slots + slot
     key = key.astype(F32)
     total = jnp.zeros((1, slots), F32)
@@ -93,12 +105,14 @@
     rank = total.astype(jnp.int32)
     rank_out[...] = rank
     lived = jnp.where(live, 1.0, 0.0)
-    table[pl.ds(0, steps), :] = obs[...] * lived
+    for step in range(steps):
+        own[pl.ds(step, 1), :] = obs_v[step, 0] * lived
+    table[pl.ds(0, steps), :] = own[...]
     table[pl.ds(steps, 1), :] = where_row.astype(F32)
     table[pl.ds(steps + 1, 1), :] = where_col.astype(F32)
-    table[pl.ds(steps + 2, 1), :] = offset[0:1, :]
-    table[pl.ds(steps + 3, 1), :] = offset[1:2, :]
-    table[pl.ds(steps + 4, 1), :] = noise[...]
+    table[pl.ds(steps + 2, 1), :] = offset_v[0, 0]
+    table[pl.ds(steps + 3, 1), :] = offset_v[1, 0]
+    table[pl.ds(steps + 4, 1), :] = noise
     table[pl.ds(steps + 5, 1), :] = lived
     table[pl.ds(steps + 6, 2), :] = jnp.zeros((2, slots), F32)
     pieces = three(table[...])
@@ -125,9 +139,11 @@
     stop_tile = jnp.where(high > low, jnp.floor((high - 1.0) * (1.0 / LANES)) + 1.0, 0.0)
     lane = iota((groups, LANES), 1)
     span = jnp.max(stop_tile - start_tile, axis=0, keepdims=True)
-    bounds[...] = jnp.where(
+    bounds_v[...] = jnp.where(
         lane == 0, start_tile, jnp.where(lane == 1, stop_tile, span)
     ).astype(jnp.int32)
+    bounds_copy = pltpu.make_async_copy(bounds_v, bounds, copies.at[5])
+    bounds_copy.start()
     extra = pl.ds(slots, 2 * LANES)
     sb[:, :, extra] = jnp.zeros((steps, GROUP, 2 * LANES), F32)
     info[:, :, extra] = jnp.zeros((2, GROUP, 2 * LANES), F32)
@@ -161,6 +177,15 @@
             sb[step, :, lanes] = jnp.broadcast_to(
                 sorted_rows[pl.ds(step, 1), lanes], (GROUP, LANES)
             )
+    bounds_copy.wait()
+    base_copy.wait()
+    scatter_all(base, z, strips, sb, ut, sv, bounds)
+
+
+def matrices_kernel(cov, mix, mat, band_rows, band_cols, edge):
+    steps = cov.shape[0]
+    rows = band_rows.shape[0]
+    wide = steps * GROUP
     spread = (iota((wide, steps), 0) // GROUP == iota((wide, steps), 1)).astype(F32)
     spread_t = (iota((steps, wide), 1) // GROUP == iota((steps, wide), 0)).astype(F32)
     expanded = jnp.dot(
@@ -222,7 +247,9 @@
     groups = base.shape[1] // GROUP
 
     def run(g, carry):
-        z[:, rows_of(g), :] = base[:, rows_of(g), :] + spread_tiles(g, bounds[g, 0], 2, sb, ut, sv)
+        value = base[:, rows_of(g), :] + spread_tiles(g, bounds[g, 0], 2, sb, ut, sv)
+        z[:, rows_of(g), :] = value
+        pack_group(g, value, strips)
         return carry
 
     lax.fori_loop(0, groups, run, 0, unroll=2)
@@ -234,30 +261,26 @@
                 z[:, rows_of(g), :] += spread_tiles(g, index, 1, sb, ut, sv)
                 return inner
 
-            return lax.fori_loop(bounds[g, 0] + 2, bounds[g, 1], more, carry)
+            lax.fori_loop(bounds[g, 0] + 2, bounds[g, 1], more, 0)
+            pack_group(g, z[:, rows_of(g), :], strips)
+            return carry
 
         lax.fori_loop(0, groups, crowded, 0)
 
-    def pack(g, carry):
-        pack_group(g, z, strips)
-        return carry
-
-    lax.fori_loop(0, groups, pack, 0, unroll=2)
-
-
-def pack_group(g, z, strips):
-    steps = z.shape[0]
+
+def pack_group(g, value, strips):
+    steps = value.shape[0]
     per = LANES // GROUP
     slot = iota((GROUP, LANES), 1) // GROUP
     for half in range(steps // per):
         left = jnp.zeros((GROUP, LANES), F32)
         right = jnp.zeros((GROUP, LANES), F32)
         for local in range(per):
-            value = z[half * per + local, rows_of(g), :]
+            moved = value[half * per + local]
             if local:
-                value = pltpu.roll(value, local * GROUP, 1)
-            left = jnp.where(slot == local, value, left)
-            right = jnp.where(slot == (local - 1) % per, value, right)
+                moved = pltpu.roll(moved, local * GROUP, 1)
+            left = jnp.where(slot == local, moved, left)
+            right = jnp.where(slot == (local - 1) % per, moved, right)
         lanes = pl.ds(half * LANES, LANES)
         strips[0, rows_of(g), lanes] = left
         strips[1, rows_of(g), lanes] = right
@@ -271,10 +294,6 @@
     both = jnp.where(lane // GROUP == local, sides[0, where_rows, lanes], sides[1, where_rows, lanes])
     both = pltpu.roll(both, (LANES - local * GROUP) % LANES, 1)
     return jnp.where((lane < GROUP) | (lane >= LANES - GROUP), both, 0.0)
-
-
-def scatter_kernel(bounds, base, sb, ut, sv, z, strips):
-    scatter_all(base, z, strips, sb, ut, sv, bounds)
 
 
 def first_filter_kernel(z, mix, band_cols, u, u_edges, y):
@@ -305,6 +324,22 @@
     lax.fori_loop(0, groups // 2, mixing, 0, unroll=2)
     u_edges[0] = u[:, pl.ds(0, GROUP), :]
     u_edges[1] = u[:, pl.ds(rows - GROUP, GROUP), :]
+
+
+def filter_unsort_kernel(z, mix, band_cols, flat_rows, rank, u, u_edges, unsorted, y):
+    first_filter_kernel(z, mix, band_cols, u, u_edges, y)
+    steps, slots = flat_rows.shape
+    tiles = slots // LANES
+    pieces = three(flat_rows[...])
+
+    def unsort_block(block, carry):
+        lanes = tile_lanes(block, 1)
+        order = (iota((slots, LANES), 0) == rank[:, lanes]).astype(F32).astype(BF16)
+        out = dot(pieces, order)
+        unsorted[:, lanes] = out[:steps] + out[steps : 2 * steps] + out[2 * steps :]
+        return carry
+
+    lax.fori_loop(0, tiles, unsort_block, 0)
 
 
 def second_filter_kernel(u, sides, band_rows, w):
@@ -378,12 +413,12 @@
 
 
 def image_one_kernel(
-    bounds, w, above, below, edge, noise, b, sb, info, ut, gv, sv, rank,
-    p, ps, z, strips, sums, unsorted, acc, extra, flat_rows,
+    bounds, w, above, below, edge, noise, b, sb, info, ut, gv, sv,
+    p, ps, z, strips, sums, flat_rows, acc, extra,
 ):
     steps, rows, _ = w.shape
     groups = rows // GROUP
-    slots = rank.shape[1]
+    slots = sb.shape[2] - 2 * LANES
     tiles = slots // LANES
     fill_extra(extra, above, below, edge)
     acc[...] = jnp.zeros_like(acc)
@@ -442,16 +477,6 @@
     value = jnp.where(lane == 3, pp, value)
     sums[...] = value
     scatter_all(p, z, strips, ps, ut, sv, bounds)
-    pieces = three(flat_rows[...])
-
-    def unsort_block(block, carry):
-        lanes = tile_lanes(block, 1)
-        order = (iota((slots, LANES), 0) == rank[:, lanes]).astype(F32).astype(BF16)
-        out = dot(pieces, order)
-        unsorted[:, lanes] = out[:steps] + out[steps : 2 * steps] + out[2 * steps :]
-        return carry
-
-    lax.fori_loop(0, tiles, unsort_block, 0)
 
 
 def image_two_kernel(
@@ -503,7 +528,10 @@
     message[...] = jnp.broadcast_to(value, message.shape)
 
 
-def final_kernel(received, b, p, q, obs, unsorted, count, solution_out, residual_out, station_out):
+def final_kernel(
+    received, b, p, q, own, unsorted, solution_out, residual_out, station_out,
+    solution_v, residual_v, station_v, sems, station_sem,
+):
     everything = received[...]
 
     def column(index):
@@ -526,37 +554,56 @@
     alpha_next = norm_next / (energy - beta * norm_next / alpha)
     along = alpha + alpha_next * (1.0 + beta)
     twice = alpha_next * alpha
-    part = solution_out.shape[0]
-    rows = solution_out.shape[1]
-    start = pl.program_id(0) * part
+    steps, rows, _ = b.shape
     chunk = 64
-    wide_along = jnp.broadcast_to(along, (chunk, LANES))
-    wide_twice = jnp.broadcast_to(twice, (chunk, LANES))
-    pieces = rows // chunk
-
-    def run(index, carry):
-        step = index // pieces
-        here = pl.ds(pl.multiple_of((index % pieces) * chunk, chunk), chunk)
-        first = b[start + step, here, :]
-        second = p[start + step, here, :]
-        solution_out[step, here, :] = wide_along * first - wide_twice * second
-        residual_out[step, here, :] = (
-            first - wide_along * second + wide_twice * q[start + step, here, :]
-        )
+    tall = (chunk // GROUP, GROUP, LANES)
+    wide_along = jnp.broadcast_to(along, (GROUP, LANES))[None]
+    wide_twice = jnp.broadcast_to(twice, (GROUP, LANES))[None]
+
+    def copies(place):
+        here = pl.ds(place * 2, 2)
+        return (
+            pltpu.make_async_copy(solution_v.at[here], solution_out.at[here], sems.at[0, place]),
+            pltpu.make_async_copy(residual_v.at[here], residual_out.at[here], sems.at[1, place]),
+        )
+
+    def run(place, carry):
+        for inner in range(2):
+            step = place * 2 + inner
+            for piece in range(rows // chunk):
+                here = pl.ds(piece * chunk, chunk)
+                first = b[step, here, :].reshape(tall)
+                second = p[step, here, :].reshape(tall)
+                third = q[step, here, :].reshape(tall)
+                solution_v[step, here, :] = (wide_along * first - wide_twice * second).reshape(
+                    chunk, LANES
+                )
+                residual_v[step, here, :] = (
+                    first - wide_along * second + wide_twice * third
+                ).reshape(chunk, LANES)
+        for copy in copies(place):
+            copy.start()
         return carry
 
-    lax.fori_loop(0, part * pieces, run, 0, unroll=2)
-
-    @pl.when(pl.program_id(0) == 0)
-    def _():
-        steps, slots = obs.shape
-        live = iota((steps, slots), 1) < count[0, 0]
-        own = jnp.where(live, obs[...], 0.0)
-        station_out[...] = along * own - twice * unsorted[...]
+    lax.fori_loop(0, steps // 2, run, 0)
+    stations = along * own[...] - twice * unsorted[...]
+    for step in range(steps):
+        station_v[step, 0] = stations[step : step + 1]
+    station_copy = pltpu.make_async_copy(station_v, station_out, station_sem)
+    station_copy.start()
+
+    def finish(place, carry):
+        for copy in copies(place):
+            copy.wait()
+        return carry
+
+    lax.fori_loop(0, steps // 2, finish, 0)
+    station_copy.wait()
 
 
 VMEM = pl.BlockSpec(memory_space=pltpu.VMEM)
 SMEM = pl.BlockSpec(memory_space=pltpu.SMEM)
+ANY = pl.BlockSpec(memory_space=pltpu.HBM)
 
 
 def call(kernel, outs, ins, operands, scratch=(), flops=10**9, moved=10**7, limit=8, **extra):
@@ -589,55 +636,68 @@
     groups = rows // GROUP
     lanes = slots + 2 * LANES
     devices = lax.axis_size("row") * lax.axis_size("col")
-    obs = station_obs.reshape(steps, slots)
     shape = jax.ShapeDtypeStruct
     field = shape((steps, rows, cols), F32)
     rim = shape((2, steps, GROUP, cols), F32)
     strips_shape = shape((2, rows, wide), F32)
     station_field = shape((steps, GROUP, lanes), F32)
     extra = pltpu.VMEM((3, steps, GROUP, LANES), F32)
-    sb, info, rank, sv, gv, ut, bounds, mix, mat, band_rows, band_cols, edge = call(
+    b, z_first, strips, sb, info, rank, own, sv, gv, ut, bounds = pl.pallas_call(
         prepare_kernel,
-        [
+        out_shape=[
+            field,
+            field,
+            strips_shape,
             station_field,
             shape((2, GROUP, lanes), F32),
             shape((1, slots), jnp.int32),
+            shape((steps, slots), F32),
             shape((2, lanes, 2 * LANES), BF16),
             shape((3 * LANES, lanes), BF16),
             shape((rows, lanes), F32),
             shape((groups, LANES), jnp.int32),
+        ],
+        in_specs=[SMEM] + [ANY] * 5,
+        out_specs=[VMEM] * 10 + [SMEM],
+        scratch_shapes=[
+            pltpu.VMEM((1, 1, slots), jnp.int32),
+            pltpu.VMEM((2, 1, 1, slots), F32),
+            pltpu.VMEM((1, 1, slots), F32),
+            pltpu.VMEM((steps, 1, 1, slots), F32),
+            pltpu.VMEM((groups, LANES), jnp.int32),
+            pltpu.VMEM((steps + 8, slots), F32),
+            pltpu.VMEM((steps + 8, slots), F32),
+            pltpu.SemaphoreType.DMA((6,)),
+        ],
+        compiler_params=pltpu.CompilerParams(vmem_limit_bytes=8 * 2**20),
+        cost_estimate=pl.CostEstimate(flops=10**9, bytes_accessed=10**7, transcendentals=0),
+    )(
+        station_count,
+        *(
+            pltpu.with_memory_space_constraint(x, pltpu.HBM)
+            for x in (station_cell, station_offset, station_noise, station_obs, grid_obs)
+        ),
+    )
+    mix, mat, band_rows, band_cols, edge = call(
+        matrices_kernel,
+        [
             shape((wide, 3 * wide), BF16),
             shape((4, wide, wide), BF16),
             shape((rows, 3 * rows), BF16),
             shape((2 * LANES, 2 * LANES), BF16),
             shape((4, wide, wide), BF16),
         ],
-        [SMEM] + [VMEM] * 5,
-        (
-            station_count,
-            station_cell.reshape(1, slots),
-            station_offset.reshape(2, slots),
-            station_noise.reshape(1, slots),
-            obs,
-            time_cov,
-        ),
-        [pltpu.VMEM((steps + 8, slots), F32), pltpu.VMEM((steps + 8, slots), F32)],
-    )
-    z_first, strips = call(
-        scatter_kernel,
-        [field, strips_shape],
-        [SMEM] + [VMEM] * 4,
-        (bounds, grid_obs, sb, ut, sv),
-        limit=4,
-    )
-
-    def smooth(z, strips):
+        [VMEM],
+        (time_cov,),
+    )
+
+    def smooth(z, strips, *more):
         from_left, from_right = exchange(strips[1], strips[0], "col")
-        u, u_edges = call(
-            first_filter_kernel,
-            [field, rim],
-            [VMEM] * 3,
-            (z, mix, band_cols),
+        u, u_edges, *unsorted = call(
+            filter_unsort_kernel if more else first_filter_kernel,
+            [field, rim] + [shape((steps, slots), F32)] * bool(more),
+            [VMEM] * (3 + len(more)),
+            (z, mix, band_cols, *more),
             [pltpu.VMEM((groups // 2, 2, wide, 2 * LANES), BF16)],
         )
         sides, full_edges = call(
@@ -651,37 +711,41 @@
         (w,) = call(
             second_filter_kernel, [field], [VMEM] * 3, (u, sides, band_rows), limit=4
         )
-        return w, above, below
+        return w, above, below, *unsorted
 
     w, above, below = smooth(z_first, strips)
-    p, ps, z, strips, sums, unsorted = call(
+    p, ps, z, strips, sums, flat_rows = call(
         image_one_kernel,
         [field, station_field, field, strips_shape, shape((GROUP, LANES), F32), shape((steps, slots), F32)],
-        [SMEM] + [VMEM] * 12,
-        (bounds, w, above, below, edge, grid_noise, grid_obs, sb, info, ut, gv, sv, rank),
-        [pltpu.VMEM((steps, GROUP, lanes), F32), extra, pltpu.VMEM((steps, slots), F32)],
-    )
-    w, above, below = smooth(z, strips)
+        [SMEM] + [VMEM] * 11,
+        (bounds, w, above, below, edge, grid_noise, b, sb, info, ut, gv, sv),
+        [pltpu.VMEM((steps, GROUP, lanes), F32), extra],
+    )
+    w, above, below, unsorted = smooth(z, strips, flat_rows, rank)
     q, message = call(
         image_two_kernel,
         [field, shape((devices, LANES), F32)],
         [VMEM] * 13,
-        (w, above, below, edge, grid_noise, grid_obs, p, z_first, z, sb, ps, info, sums),
+        (w, above, below, edge, grid_noise, b, p, z_first, z, sb, ps, info, sums),
         [extra],
         limit=4,
     )
     received = lax.all_to_all(message, ("row", "col"), 0, 0, tiled=True)
-    parts = 8
-    block = pl.BlockSpec((steps // parts, rows, cols), lambda i: (i, 0, 0))
     solution_grid, residual_grid, solution_stations = pl.pallas_call(
         final_kernel,
-        grid=(parts,),
-        out_shape=[field, field, shape((steps, slots), F32)],
-        in_specs=[VMEM] * 6 + [SMEM],
-        out_specs=[block, block, pl.BlockSpec((steps, slots), lambda i: (0, 0))],
-        compiler_params=pltpu.CompilerParams(vmem_limit_bytes=6 * 2**20),
-    )(received, grid_obs, p, q, obs, unsorted, station_count)
-    return solution_grid, solution_stations.reshape(steps, 1, 1, slots), residual_grid
+        out_shape=[field, field, shape((steps, 1, 1, slots), F32)],
+        in_specs=[VMEM] * 6,
+        out_specs=[ANY, ANY, ANY],
+        scratch_shapes=[
+            pltpu.VMEM((steps, rows, cols), F32),
+            pltpu.VMEM((steps, rows, cols), F32),
+            pltpu.VMEM((steps, 1, 1, slots), F32),
+            pltpu.SemaphoreType.DMA((2, steps // 2)),
+            pltpu.SemaphoreType.DMA(()),
+        ],
+        compiler_params=pltpu.CompilerParams(vmem_limit_bytes=10 * 2**20),
+    )(received, b, p, q, own, unsorted)
+    return solution_grid, solution_stations, residual_grid
 
 
 def solution(mesh):

time: 109 us -> 98 us (0.90)
  local copies, waits for them, and re-layouts: 6.82 us -> 0.12 us
  Pallas kernels: 62.3 us -> 59.4 us
  blocking collectives: 15.5 us -> 14.4 us
    pallas_call x10 -> x9, Pallas kernels: 54.2 us -> 42.1 us  [call(): pl.pallas_call(kernel, out_shape=outs, in_specs=ins, out_specs=[VMEM] * l...]
    pallas_call x1 -> x2, Pallas kernels: 8.06 us -> 17.3 us  [the longest x1 13 us: body(): pl.pallas_call(prepare_kernel, out_shape=[field, field, strips_shape, sta...]
    unnamed x15 -> x4, local copies, waits for them, and re-layouts: 6.71 us -> 0.01 us
    all_to_all x1, blocking collectives: 15.5 us -> 14.4 us  [body(): received = lax.all_to_all(message, ('row', 'col'), 0, 0, tiled=True)]
  transfers between devices with their start and end apart: 8 -> 8, of which waited for: 1 -> 0; matrix products, arithmetic and copies ran while one was open for 0% -> 0% of each run, Pallas kernels for 16% -> 21%
where the time goes in v3:
time: 98 us; the launch traced here: 97.5 us
  Pallas kernels  59.4 us (61%)
  starting transfers between devices  22 us (22%)
  blocking collectives  14.4 us (15%)
  between operations  1.55 us (2%)
    pallas_call x9, Pallas kernels, call(): pl.pallas_call(kernel, out_shape=outs, in_specs=ins, out_specs=[VMEM] * l...  42.1 us
    ppermute x4, starting transfers between devices, exchange(): lax.ppermute(first, axis, forward)  16.8 us
    all_to_all x1, blocking collectives, body(): received = lax.all_to_all(message, ('row', 'col'), 0, 0, tiled=True)  14.4 us
    pallas_call x1, Pallas kernels, body(): pl.pallas_call(prepare_kernel, out_shape=[field, field, strips_shape, sta...  13 us
    ppermute x4, starting transfers between devices, exchange(): lax.ppermute(second, axis, backward)  5.17 us
    pallas_call x1, Pallas kernels, body(): pl.pallas_call(final_kernel, out_shape=[field, field, shape((steps, 1, 1,...  4.34 us
  transfers between devices with their start and end apart: 8, of which 0 were waited for; matrix products, arithmetic and copies ran while one was open for 0% of the time, Pallas kernels for 21%

profile of v3, /device:TPU:0, one launch (start us, length us, event | category | flops | bytes accessed | tf_op | source)
XLA Modules:
  0.0 97.5 jit_solution(16959870138266824428)
XLA Ops:
  0.6 0.0 copy-start.1
  1.3 13.0 %shard_map.103 = (f32[32,256,128]{2,1,0:T(8,128)S(1)}, f32[32,256,128]{2,1,0:T(8,128)S(1)}, f32[2,256,256]{2,1,0:T(8,128)S(1)}, f32[32,8,1280]{2,1,0:T(8,128)S(1...) custom-call(s32[1,1]{1,0:T(1,128)S(6)} %copy.12.count, ...), custom_call_target="tpu_custom_call" | custom-call | flops 1000000000 | bytes 10000000 | tf_op jit(solution)/shard_map/pallas_call | solution.py:645
  14.3 1.3 %collective-permute-start.1 = (f32[256,256]{1,0:T(8,128)S(1)}, f32[256,256]{1,0:T(8,128)S(1)}, u32[]{:S(2)}, u32[]{:S(2)}) collective-permute-start(f32[256,256]{1,0:T(8,128)S(1)} %get-tuple-element.77), channel_id=1, source_target_pairs={{1,0},{2,1},{3,2},{5,4},{6,5},{7,6},{9,8},{10,9},{11,10},{13,12},{... | collective-permute-start | bytes 786440 | tf_op jit(solution)/shard_map/ppermute | solution.py:626
  15.6 5.6 %collective-permute-start = (f32[256,256]{1,0:T(8,128)S(1)}, f32[256,256]{1,0:T(8,128)S(1)}, u32[]{:S(2)}, u32[]{:S(2)}) collective-permute-start(f32[256,256]{1,0:T(8,128)S(1)} %get-tuple-element.78), channel_id=1, source_target_pairs={{0,1},{1,2},{2,3},{4,5},{5,6},{6,7},{8,9},{9,10},{10,11},{12,13},{... | collective-permute-start | bytes 786440 | tf_op jit(solution)/shard_map/ppermute | solution.py:626
  21.3 0.0 copy-done.1
  21.3 1.2 %shard_map.104 = (bf16[256,768]{1,0:T(8,128)(2,1)S(1)}, bf16[4,256,256]{2,1,0:T(8,128)(2,1)S(1)}, bf16[256,768]{1,0:T(8,128)(2,1)S(1)}, bf16[256,256]{1,0:T(8,128)(2,1)S(1)}, bf16[4,256,256]{2,1,0:T(8,128)(2,1)S(1)}) custom-call(f32[32,32]{1,0:T(8,128)S(1)} %copy-done.1), custom_call_target="tpu_custom_call" | custom-call | flops 1000000000 | bytes 10000000 | tf_op jit(solution)/shard_map/pallas_call | solution.py:610
  22.5 5.5 %shard_map.105 = (f32[32,256,128]{2,1,0:T(8,128)S(1)}, f32[2,32,8,128]{3,2,1,0:T(8,128)S(1)}) custom-call(f32[32,256,128]{2,1,0:T(8,128)S(1)} %get-tuple-element.40.z.z_first, bf16[256,768]{1,0:T(8,128)(2,1)S(1)} %get-tuple-element.41.mix, bf16[256,256]{1,0:T(8,128)(2,1)S(1)} %get-tuple-element.42.band_cols), custom_call_target="tpu_custom_call" | custom-call | flops 1000000000 | bytes 10000000 | tf_op jit(solution)/shard_map/pallas_call | solution.py:610
  28.0 0.0 collective-permute-done.1.from_right
  28.0 0.0 collective-permute-done.from_left
  28.0 0.7 shard_map.106
  28.8 1.3 %collective-permute-start.3 = (f32[32,8,128]{2,1,0:T(8,128)S(1)}, f32[32,8,128]{2,1,0:T(8,128)S(1)}, u32[]{:S(2)}, u32[]{:S(2)}) collective-permute-start(f32[32,8,128]{2,1,0:T(8,128)S(1)} %get-tuple-element.81), channel_id=1, source_target_pairs={{4,0},{8,4},{12,8},{16,12},{20,16},{24,20},{28,24},{5,1},{9,5},{13... | collective-permute-start | bytes 393224 | tf_op jit(solution)/shard_map/ppermute | solution.py:626
  30.1 3.0 %collective-permute-start.2 = (f32[32,8,128]{2,1,0:T(8,128)S(1)}, f32[32,8,128]{2,1,0:T(8,128)S(1)}, u32[]{:S(2)}, u32[]{:S(2)}) collective-permute-start(f32[32,8,128]{2,1,0:T(8,128)S(1)} %get-tuple-element.82), channel_id=1, source_target_pairs={{0,4},{4,8},{8,12},{12,16},{16,20},{20,24},{24,28},{1,5},{5,9},{9,... | collective-permute-start | bytes 393224 | tf_op jit(solution)/shard_map/ppermute | solution.py:626
  33.1 0.0 copy-start
  33.1 3.2 %shard_map.107.w = f32[32,256,128]{2,1,0:T(8,128)S(1)} custom-call(f32[32,256,128]{2,1,0:T(8,128)S(1)} %get-tuple-element.43.u, f32[2,256,256]{2,1,0:T(8,128)S(1)} %get-tuple-element.48.sides, bf16[256,768]{1,0:T(8,128)(2,1)S(1)} %get-tuple-element.47.band_rows), custom_call_target="tpu_custom_call" | custom-call | flops 1000000000 | bytes 10000000 | tf_op jit(solution)/shard_map/pallas_call | solution.py:610
  36.4 0.0 collective-permute-done.3.below
  36.4 0.0 collective-permute-done.2.above
  36.4 0.0 copy-done
  36.4 13.8 %shard_map.108 = (f32[32,256,128]{2,1,0:T(8,128)S(1)}, f32[32,8,1280]{2,1,0:T(8,128)S(1)}, f32[32,256,128]{2,1,0:T(8,128)S(1)}, f32[2,256,256]{2,1,0:T(8,128)S(1...) custom-call(s32[32,128]{1,0:T(8,128)S(1)} %get-tuple-element.39.bounds, f32[32,256,128]{2,1,0:T(8,128)S(1)} %shard_map.107.w, ...), custom_call_target="tpu_custom_call" | custom-call | flops 1000000000 | bytes 10000000 | tf_op jit(solution)/shard_map/pallas_call | solution.py:610
  50.3 1.3 %collective-permute-start.5 = (f32[256,256]{1,0:T(8,128)S(1)}, f32[256,256]{1,0:T(8,128)S(1)}, u32[]{:S(2)}, u32[]{:S(2)}) collective-permute-start(f32[256,256]{1,0:T(8,128)S(1)} %get-tuple-element.75), channel_id=1, source_target_pairs={{1,0},{2,1},{3,2},{5,4},{6,5},{7,6},{9,8},{10,9},{11,10},{13,12},{... | collective-permute-start | bytes 786440 | tf_op jit(solution)/shard_map/ppermute | solution.py:626
  51.6 4.6 %collective-permute-start.4 = (f32[256,256]{1,0:T(8,128)S(1)}, f32[256,256]{1,0:T(8,128)S(1)}, u32[]{:S(2)}, u32[]{:S(2)}) collective-permute-start(f32[256,256]{1,0:T(8,128)S(1)} %get-tuple-element.76), channel_id=1, source_target_pairs={{0,1},{1,2},{2,3},{4,5},{5,6},{6,7},{8,9},{9,10},{10,11},{12,13},{... | collective-permute-start | bytes 786440 | tf_op jit(solution)/shard_map/ppermute | solution.py:626
  56.2 7.2 %shard_map.109 = (f32[32,256,128]{2,1,0:T(8,128)S(1)}, f32[2,32,8,128]{3,2,1,0:T(8,128)S(1)}, f32[32,1024]{1,0:T(8,128)S(1)}) custom-call(f32[32,256,128]{2,1,0:T(8,128)S(1)} %get-tuple-element.57.z, bf16[256,768]{1,0:T(8,128)(2,1)S(1)} %get-tuple-element.41.mix, bf16[256,256]{1,0:T(8,128)(2,1)S(1)} %get-tuple-element.42.band_cols, ...), custom_call_target="tpu_custom_call" | custom-call | flops 1000000000 | bytes 10000000 | tf_op jit(solution)/shard_map/pallas_call | solution.py:610
  63.4 0.0 collective-permute-done.5.from_right
  63.4 0.0 collective-permute-done.4.from_left
  63.4 0.7 shard_map.110
  64.2 1.3 %collective-permute-start.7 = (f32[32,8,128]{2,1,0:T(8,128)S(1)}, f32[32,8,128]{2,1,0:T(8,128)S(1)}, u32[]{:S(2)}, u32[]{:S(2)}) collective-permute-start(f32[32,8,128]{2,1,0:T(8,128)S(1)} %get-tuple-element.79), channel_id=1, source_target_pairs={{4,0},{8,4},{12,8},{16,12},{20,16},{24,20},{28,24},{5,1},{9,5},{13... | collective-permute-start | bytes 393224 | tf_op jit(solution)/shard_map/ppermute | solution.py:626
  65.5 3.6 %collective-permute-start.6 = (f32[32,8,128]{2,1,0:T(8,128)S(1)}, f32[32,8,128]{2,1,0:T(8,128)S(1)}, u32[]{:S(2)}, u32[]{:S(2)}) collective-permute-start(f32[32,8,128]{2,1,0:T(8,128)S(1)} %get-tuple-element.80), channel_id=1, source_target_pairs={{0,4},{4,8},{8,12},{12,16},{16,20},{20,24},{24,28},{1,5},{5,9},{9,... | collective-permute-start | bytes 393224 | tf_op jit(solution)/shard_map/ppermute | solution.py:626
  69.1 3.2 %shard_map.111.w = f32[32,256,128]{2,1,0:T(8,128)S(1)} custom-call(f32[32,256,128]{2,1,0:T(8,128)S(1)} %get-tuple-element.60.u, f32[2,256,256]{2,1,0:T(8,128)S(1)} %get-tuple-element.63.sides, bf16[256,768]{1,0:T(8,128)(2,1)S(1)} %get-tuple-element.47.band_rows), custom_call_target="tpu_custom_call" | custom-call | flops 1000000000 | bytes 10000000 | tf_op jit(solution)/shard_map/pallas_call | solution.py:610
  72.3 0.0 collective-permute-done.7.below
  72.3 0.0 collective-permute-done.6.above
  72.3 6.4 %shard_map.112 = (f32[32,256,128]{2,1,0:T(8,128)S(1)}, f32[32,128]{1,0:T(8,128)S(1)}) custom-call(f32[32,256,128]{2,1,0:T(8,128)S(1)} %shard_map.111.w, f32[32,8,128]{2,1,0:T(8,128)S(1)} %collective-permute-done.6.above, f32[32,8,128]{2,1,0:T(8,128)S(1)} %collective-permute-done.7.below, bf16[4,256,256]{2,1,0:T(8,128)(2,1)S(1)} %get-tuple-element.50.edge, ...), custom_call_target="tpu_custom_call" | custom-call | flops 1000000000 | bytes 10000000 | tf_op jit(solution)/shard_map/pallas_call | solution.py:610
  78.8 14.4 %all_to_all.11 = f32[32,1,128]{2,1,0:T(1,128)S(1)} all-to-all(f32[32,1,128]{2,1,0:T(1,128)S(1)} %bitcast.21), channel_id=1, replica_groups=mesh['row'=8,'col'=4] {'row','col'}, dimensions={0} | all-to-all | bytes 32768 | tf_op jit(solution)/shard_map/all_to_all | solution.py:733
  93.2 4.3 %shard_map.113 = (f32[32,256,128]{2,1,0:T(8,128)}, f32[32,256,128]{2,1,0:T(8,128)}, f32[32,1,1,1024]{3,2,1,0:T(1,128)}) custom-call(f32[32,128]{1,0:T(8,128)S(1)} %bitcast.20, f32[32,256,128]{2,1,0:T(8,128)S(1)} %get-tuple-element.51.b, f32[32,256,128]{2,1,0:T(8,128)S(1)} %get-tuple-element.65.p, f32[32,256,128]{2,1,0:T(8,128)S(1)} %get-tuple-element.69.q, ...), custom_call_target="tpu_custom_call" | custom-call | tf_op jit(solution)/shard_map/pallas_call | solution.py:734
  (4 shorter events, 0.1 us)
Async XLA Ops:
  0.6 20.7 %copy-start.1 = (f32[32,32]{1,0:T(8,128)S(1)}, f32[32,32]{1,0:T(8,128)}, u32[]{:S(2)}) copy-start(f32[32,32]{1,0:T(8,128)} %cov.1) | copy-start | bytes 12292
  14.3 13.7 %collective-permute-start.1 = (f32[256,256]{1,0:T(8,128)S(1)}, f32[256,256]{1,0:T(8,128)S(1)}, u32[]{:S(2)}, u32[]{:S(2)}) collective-permute-start(f32[256,256]{1,0:T(8,128)S(1)} %get-tuple-element.77), channel_id=1, source_target_pairs={{1,0},{2,1},{3,2},{5,4},{6,5},{7,6},{9,8},{10,9},{11,10},{13,12},{... | collective-permute-start | bytes 786440 | tf_op jit(solution)/shard_map/ppermute | solution.py:626
  15.6 12.4 %collective-permute-start = (f32[256,256]{1,0:T(8,128)S(1)}, f32[256,256]{1,0:T(8,128)S(1)}, u32[]{:S(2)}, u32[]{:S(2)}) collective-permute-start(f32[256,256]{1,0:T(8,128)S(1)} %get-tuple-element.78), channel_id=1, source_target_pairs={{0,1},{1,2},{2,3},{4,5},{5,6},{6,7},{8,9},{9,10},{10,11},{12,13},{... | collective-permute-start | bytes 786440 | tf_op jit(solution)/shard_map/ppermute | solution.py:626
  28.8 7.6 %collective-permute-start.3 = (f32[32,8,128]{2,1,0:T(8,128)S(1)}, f32[32,8,128]{2,1,0:T(8,128)S(1)}, u32[]{:S(2)}, u32[]{:S(2)}) collective-permute-start(f32[32,8,128]{2,1,0:T(8,128)S(1)} %get-tuple-element.81), channel_id=1, source_target_pairs={{4,0},{8,4},{12,8},{16,12},{20,16},{24,20},{28,24},{5,1},{9,5},{13... | collective-permute-start | bytes 393224 | tf_op jit(solution)/shard_map/ppermute | solution.py:626
  30.1 6.3 %collective-permute-start.2 = (f32[32,8,128]{2,1,0:T(8,128)S(1)}, f32[32,8,128]{2,1,0:T(8,128)S(1)}, u32[]{:S(2)}, u32[]{:S(2)}) collective-permute-start(f32[32,8,128]{2,1,0:T(8,128)S(1)} %get-tuple-element.82), channel_id=1, source_target_pairs={{0,4},{4,8},{8,12},{12,16},{16,20},{20,24},{24,28},{1,5},{5,9},{9,... | collective-permute-start | bytes 393224 | tf_op jit(solution)/shard_map/ppermute | solution.py:626
  33.1 3.3 %copy-start = (f32[256,128]{1,0:T(8,128)S(1)}, f32[256,128]{1,0:T(8,128)}, u32[]{:S(2)}) copy-start(f32[256,128]{1,0:T(8,128)} %noise.3) | copy-start | bytes 393220
  50.3 13.1 %collective-permute-start.5 = (f32[256,256]{1,0:T(8,128)S(1)}, f32[256,256]{1,0:T(8,128)S(1)}, u32[]{:S(2)}, u32[]{:S(2)}) collective-permute-start(f32[256,256]{1,0:T(8,128)S(1)} %get-tuple-element.75), channel_id=1, source_target_pairs={{1,0},{2,1},{3,2},{5,4},{6,5},{7,6},{9,8},{10,9},{11,10},{13,12},{... | collective-permute-start | bytes 786440 | tf_op jit(solution)/shard_map/ppermute | solution.py:626
  51.6 11.8 %collective-permute-start.4 = (f32[256,256]{1,0:T(8,128)S(1)}, f32[256,256]{1,0:T(8,128)S(1)}, u32[]{:S(2)}, u32[]{:S(2)}) collective-permute-start(f32[256,256]{1,0:T(8,128)S(1)} %get-tuple-element.76), channel_id=1, source_target_pairs={{0,1},{1,2},{2,3},{4,5},{5,6},{6,7},{8,9},{9,10},{10,11},{12,13},{... | collective-permute-start | bytes 786440 | tf_op jit(solution)/shard_map/ppermute | solution.py:626
  64.2 8.1 %collective-permute-start.7 = (f32[32,8,128]{2,1,0:T(8,128)S(1)}, f32[32,8,128]{2,1,0:T(8,128)S(1)}, u32[]{:S(2)}, u32[]{:S(2)}) collective-permute-start(f32[32,8,128]{2,1,0:T(8,128)S(1)} %get-tuple-element.79), channel_id=1, source_target_pairs={{4,0},{8,4},{12,8},{16,12},{20,16},{24,20},{28,24},{5,1},{9,5},{13... | collective-permute-start | bytes 393224 | tf_op jit(solution)/shard_map/ppermute | solution.py:626
  65.5 6.9 %collective-permute-start.6 = (f32[32,8,128]{2,1,0:T(8,128)S(1)}, f32[32,8,128]{2,1,0:T(8,128)S(1)}, u32[]{:S(2)}, u32[]{:S(2)}) collective-permute-start(f32[32,8,128]{2,1,0:T(8,128)S(1)} %get-tuple-element.80), channel_id=1, source_target_pairs={{0,4},{4,8},{8,12},{12,16},{16,20},{20,24},{24,28},{1,5},{5,9},{9,... | collective-permute-start | bytes 393224 | tf_op jit(solution)/shard_map/ppermute | solution.py:626

commit v4 on v3

--- a/solution.py
+++ b/solution.py
@@ -61,6 +61,15 @@
         lax.slice_in_dim(x, start, start + LANES, axis=axis)
         for start in range(0, x.shape[axis], LANES)
     ]
+
+
+def slot_of(axis, side):
+    odd = lax.rem(lax.axis_index(axis), 2)
+    return odd if side else 1 - odd
+
+
+def chunks(steps, size=GROUP):
+    return [pl.ds(start, size) for start in range(0, steps, size)]
 
 
 def rows_of(g):
@@ -237,8 +246,14 @@
 def spread_tiles(g, first, count, sb, ut, sv):
     steps = sb.shape[0]
     lanes = tile_lanes(first, count)
-    scaled = sb[:, :, lanes] * ut[rows_of(g), lanes][None]
-    left = pair(scaled.reshape(steps * GROUP, count * LANES))
+    weight = ut[rows_of(g), lanes][None]
+    left = jnp.concatenate(
+        [
+            pair((sb[times, :, lanes] * weight).reshape(GROUP * GROUP, count * LANES))
+            for times in chunks(steps)
+        ],
+        axis=0,
+    )
     right = jnp.concatenate([sv[0, lanes, :], sv[1, lanes, :]], axis=0)
     return halves(dot(left, right)).reshape(steps, GROUP, LANES)
 
@@ -282,8 +297,8 @@
             left = jnp.where(slot == local, moved, left)
             right = jnp.where(slot == (local - 1) % per, moved, right)
         lanes = pl.ds(half * LANES, LANES)
-        strips[0, rows_of(g), lanes] = left
-        strips[1, rows_of(g), lanes] = right
+        strips[slot_of("col", 0), rows_of(g), lanes] = left
+        strips[slot_of("col", 1), rows_of(g), lanes] = right
 
 
 def unpack(sides, where_rows, count, step):
@@ -359,17 +374,19 @@
     lax.fori_loop(0, steps // 2, along, 0, unroll=2)
 
 
-def edge_kernel(from_left, from_right, u_edges, mat, band_rows, sides, full_edges):
+def edge_kernel(first, second, u_edges, mat, band_rows, sides, full_edges):
     steps = u_edges.shape[1]
-    rows = from_left.shape[0]
-    for side, source in ((0, from_left), (1, from_right)):
+    rows = first.shape[0]
+    for place, source in ((0, first), (1, second)):
+        side = slot_of("col", place)
         high, low = split(source[...])
         value = dot(high, mat[2 * side]) + dot(low, mat[2 * side])
         value = value + dot(high, mat[2 * side + 1])
         sides[side] = value
     for which, start in ((0, 0), (1, rows - GROUP)):
+        slot = slot_of("row", which)
         for step in range(steps):
-            full_edges[which, step] = u_edges[which, step] + unpack(
+            full_edges[slot, step] = u_edges[which, step] + unpack(
                 sides, pl.ds(start, GROUP), GROUP, step
             )
     for side in range(2):
@@ -377,10 +394,11 @@
         sides[side] = dot(band_rows[...], jnp.concatenate([high, low, high], axis=0))
 
 
-def fill_extra(extra, above, below, edge):
-    steps = above.shape[0]
+def fill_extra(extra, first, second, edge):
+    steps = first.shape[0]
     flat = (steps * GROUP, LANES)
-    for which, source in ((0, above), (1, below)):
+    for place, source in ((0, first), (1, second)):
+        which = slot_of("row", place)
         both = pair(source[...].reshape(flat))
         value = halves(dot(edge[2 * which], both)) + dot(edge[2 * which + 1], both[:, :LANES])
         extra[which] = value.reshape(steps, GROUP, LANES)
@@ -395,7 +413,9 @@
     steps = acc.shape[0]
     lanes = tile_lanes(first, count)
     out = dot(both, gv[:, lanes]).reshape(steps, GROUP, count * LANES)
-    acc[:, :, lanes] += out * ut[rows_of(g), lanes][None]
+    weight = ut[rows_of(g), lanes][None]
+    for times in chunks(steps):
+        acc[times, :, lanes] += out[times.start : times.start + times.size] * weight
 
 
 def left_of(value):
@@ -424,16 +444,22 @@
     acc[...] = jnp.zeros_like(acc)
 
     def run(g, carry):
-        value = w[:, rows_of(g), :] + extra[which_extra(g, groups)]
-        mine = b[:, rows_of(g), :]
-        image = value + noise[rows_of(g), :][None] * mine
-        p[:, rows_of(g), :] = image
-        gather_tiles(g, left_of(value), bounds[g, 0], 2, acc, ut, gv)
-        return (
-            carry[0] + fold(mine * mine),
-            carry[1] + fold(mine * image),
-            carry[2] + fold(image * image),
-        )
+        here = rows_of(g)
+        which = which_extra(g, groups)
+        spread = noise[here, :][None]
+        first, second, third = carry
+        left = []
+        for times in chunks(steps):
+            value = w[times, here, :] + extra[which, times]
+            left.append(left_of(value))
+            mine = b[times, here, :]
+            image = value + spread * mine
+            p[times, here, :] = image
+            first = first + fold(mine * mine)
+            second = second + fold(mine * image)
+            third = third + fold(image * image)
+        gather_tiles(g, jnp.concatenate(left, axis=0), bounds[g, 0], 2, acc, ut, gv)
+        return first, second, third
 
     zero = jnp.zeros((GROUP, LANES), F32)
     carry = lax.fori_loop(0, groups, run, (zero,) * 3, unroll=2)
@@ -491,18 +517,21 @@
 
     def run(g, carry):
         here = rows_of(g)
-        value = w[:, here, :] + extra[which_extra(g, groups)]
-        mine = p[:, here, :]
-        scaled = noise[here, :][None] * mine
-        q[:, here, :] = value + scaled
-        residual = b[:, here, :] - shift * mine
-        second = z[:, here, :]
-        moved = z_first[:, here, :] - shift * second
-        return (
-            carry[0] + fold(residual * residual),
-            carry[1] + fold(moved * value + residual * scaled),
-            carry[2] + fold(second * value + mine * scaled),
-        )
+        which = which_extra(g, groups)
+        spread = noise[here, :][None]
+        first, second, third = carry
+        for times in chunks(steps, 4):
+            value = w[times, here, :] + extra[which, times]
+            mine = p[times, here, :]
+            scaled = spread * mine
+            q[times, here, :] = value + scaled
+            residual = b[times, here, :] - shift * mine
+            image = z[times, here, :]
+            moved = z_first[times, here, :] - shift * image
+            first = first + fold(residual * residual)
+            second = second + fold(moved * value + residual * scaled)
+            third = third + fold(image * value + mine * scaled)
+        return first, second, third
 
     zero = jnp.zeros((GROUP, LANES), F32)
     carry = lax.fori_loop(0, groups, run, (zero,) * 3)
@@ -619,11 +648,13 @@
     )(*operands)
 
 
-def exchange(first, second, axis):
+def exchange(both, axis):
     count = lax.axis_size(axis)
-    forward = [(i, i + 1) for i in range(count - 1)]
-    backward = [(target, source) for source, target in forward]
-    return lax.ppermute(first, axis, forward), lax.ppermute(second, axis, backward)
+    pairs = [[(i, i + 1) for i in range(start, count - 1, 2)] for start in (0, 1)]
+    return tuple(
+        lax.ppermute(both[place], axis, found + [(b, a) for a, b in found])
+        for place, found in enumerate(pairs)
+    )
 
 
 def body(
@@ -692,7 +723,7 @@
     )
 
     def smooth(z, strips, *more):
-        from_left, from_right = exchange(strips[1], strips[0], "col")
+        from_left, from_right = exchange(strips, "col")
         u, u_edges, *unsorted = call(
             filter_unsort_kernel if more else first_filter_kernel,
             [field, rim] + [shape((steps, slots), F32)] * bool(more),
@@ -707,7 +738,7 @@
             (from_left, from_right, u_edges, mat, band_rows),
             limit=4,
         )
-        above, below = exchange(full_edges[1], full_edges[0], "row")
+        above, below = exchange(full_edges, "row")
         (w,) = call(
             second_filter_kernel, [field], [VMEM] * 3, (u, sides, band_rows), limit=4
         )

time: 98 us -> 89.3 us (0.911)
  starting transfers between devices: 22 us -> 17.1 us
  blocking collectives: 14.4 us -> 12.2 us
  Pallas kernels: 59.4 us -> 57.9 us
    ppermute x8, starting transfers between devices: 22 us -> 17.1 us  [exchange(): lax.ppermute(both[place], axis, found + [(b, a) for a, b in found])]
    all_to_all x1, blocking collectives: 14.4 us -> 12.2 us  [body(): received = lax.all_to_all(message, ('row', 'col'), 0, 0, tiled=True)]
    pallas_call x9, Pallas kernels: 42.1 us -> 40.6 us  [call(): pl.pallas_call(kernel, out_shape=outs, in_specs=ins, out_specs=[VMEM] * l...]
  transfers between devices with their start and end apart: 8 -> 8, of which waited for: 0 -> 0; matrix products, arithmetic and copies ran while one was open for 0% -> 0% of each run, Pallas kernels for 21% -> 23%
where the time goes in v4:
time: 89.3 us; the launch traced here: 88.9 us
  Pallas kernels  57.9 us (65%)
  starting transfers between devices  17.1 us (19%)
  blocking collectives  12.2 us (14%)
  between operations  1.5 us (2%)
    pallas_call x9, Pallas kernels, call(): pl.pallas_call(kernel, out_shape=outs, in_specs=ins, out_specs=[VMEM] * l...  40.6 us
    ppermute x8, starting transfers between devices, exchange(): lax.ppermute(both[place], axis, found + [(b, a) for a, b in found])  17.1 us
    pallas_call x1, Pallas kernels, body(): pl.pallas_call(prepare_kernel, out_shape=[field, field, strips_shape, sta...  12.9 us
    all_to_all x1, blocking collectives, body(): received = lax.all_to_all(message, ('row', 'col'), 0, 0, tiled=True)  12.2 us
    pallas_call x1, Pallas kernels, body(): pl.pallas_call(final_kernel, out_shape=[field, field, shape((steps, 1, 1,...  4.34 us
  transfers between devices with their start and end apart: 8, of which 0 were waited for; matrix products, arithmetic and copies ran while one was open for 0% of the time, Pallas kernels for 23%

profile of v4, /device:TPU:0, one launch (start us, length us, event | category | flops | bytes accessed | tf_op | source)
XLA Modules:
  0.0 88.9 jit_solution(12004176063488540962)
XLA Ops:
  0.6 0.0 copy-start.1
  1.3 12.9 %shard_map.103 = (f32[32,256,128]{2,1,0:T(8,128)S(1)}, f32[32,256,128]{2,1,0:T(8,128)S(1)}, f32[2,256,256]{2,1,0:T(8,128)S(1)}, f32[32,8,1280]{2,1,0:T(8,128)S(1...) custom-call(s32[1,1]{1,0:T(1,128)S(6)} %copy.12.count, ...), custom_call_target="tpu_custom_call" | custom-call | flops 1000000000 | bytes 10000000 | tf_op jit(solution)/shard_map/pallas_call | solution.py:676
  14.3 0.7 collective-permute-start.1
  15.0 6.0 %collective-permute-start = (f32[256,256]{1,0:T(8,128)S(1)}, f32[256,256]{1,0:T(8,128)S(1)}, u32[]{:S(2)}, u32[]{:S(2)}) collective-permute-start(f32[256,256]{1,0:T(8,128)S(1)} %get-tuple-element.78), channel_id=1, source_target_pairs={{0,1},{2,3},{1,0},{3,2},{4,5},{6,7},{5,4},{7,6},{8,9},{10,11},{9,8... | collective-permute-start | bytes 786440 | tf_op jit(solution)/shard_map/ppermute | solution.py:655
  20.9 0.0 copy-done.1
  20.9 1.2 %shard_map.104 = (bf16[256,768]{1,0:T(8,128)(2,1)S(1)}, bf16[4,256,256]{2,1,0:T(8,128)(2,1)S(1)}, bf16[256,768]{1,0:T(8,128)(2,1)S(1)}, bf16[256,256]{1,0:T(8,128)(2,1)S(1)}, bf16[4,256,256]{2,1,0:T(8,128)(2,1)S(1)}) custom-call(f32[32,32]{1,0:T(8,128)S(1)} %copy-done.1), custom_call_target="tpu_custom_call" | custom-call | flops 1000000000 | bytes 10000000 | tf_op jit(solution)/shard_map/pallas_call | solution.py:639
  22.1 5.5 %shard_map.105 = (f32[32,256,128]{2,1,0:T(8,128)S(1)}, f32[2,32,8,128]{3,2,1,0:T(8,128)S(1)}) custom-call(f32[32,256,128]{2,1,0:T(8,128)S(1)} %get-tuple-element.40.z.z_first, bf16[256,768]{1,0:T(8,128)(2,1)S(1)} %get-tuple-element.41.mix, bf16[256,256]{1,0:T(8,128)(2,1)S(1)} %get-tuple-element.42.band_cols), custom_call_target="tpu_custom_call" | custom-call | flops 1000000000 | bytes 10000000 | tf_op jit(solution)/shard_map/pallas_call | solution.py:639
  27.7 0.0 collective-permute-done.1.second
  27.7 0.0 collective-permute-done.first
  27.7 0.8 shard_map.106
  28.6 0.7 collective-permute-start.3
  29.2 2.9 %collective-permute-start.2 = (f32[32,8,128]{2,1,0:T(8,128)S(1)}, f32[32,8,128]{2,1,0:T(8,128)S(1)}, u32[]{:S(2)}, u32[]{:S(2)}) collective-permute-start(f32[32,8,128]{2,1,0:T(8,128)S(1)} %get-tuple-element.82), channel_id=1, source_target_pairs={{0,4},{8,12},{16,20},{24,28},{4,0},{12,8},{20,16},{28,24},{1,5},{9... | collective-permute-start | bytes 393224 | tf_op jit(solution)/shard_map/ppermute | solution.py:655
  32.1 0.0 copy-start
  32.1 3.2 %shard_map.107.w = f32[32,256,128]{2,1,0:T(8,128)S(1)} custom-call(f32[32,256,128]{2,1,0:T(8,128)S(1)} %get-tuple-element.43.u, f32[2,256,256]{2,1,0:T(8,128)S(1)} %get-tuple-element.48.sides, bf16[256,768]{1,0:T(8,128)(2,1)S(1)} %get-tuple-element.47.band_rows), custom_call_target="tpu_custom_call" | custom-call | flops 1000000000 | bytes 10000000 | tf_op jit(solution)/shard_map/pallas_call | solution.py:639
  35.4 0.0 collective-permute-done.3.below
  35.4 0.0 collective-permute-done.2.above
  35.4 0.0 copy-done
  35.4 14.0 %shard_map.108 = (f32[32,256,128]{2,1,0:T(8,128)S(1)}, f32[32,8,1280]{2,1,0:T(8,128)S(1)}, f32[32,256,128]{2,1,0:T(8,128)S(1)}, f32[2,256,256]{2,1,0:T(8,128)S(1...) custom-call(s32[32,128]{1,0:T(8,128)S(1)} %get-tuple-element.39.bounds, f32[32,256,128]{2,1,0:T(8,128)S(1)} %shard_map.107.w, ...), custom_call_target="tpu_custom_call" | custom-call | flops 1000000000 | bytes 10000000 | tf_op jit(solution)/shard_map/pallas_call | solution.py:639
  49.4 0.7 collective-permute-start.5
  50.1 2.9 %collective-permute-start.4 = (f32[256,256]{1,0:T(8,128)S(1)}, f32[256,256]{1,0:T(8,128)S(1)}, u32[]{:S(2)}, u32[]{:S(2)}) collective-permute-start(f32[256,256]{1,0:T(8,128)S(1)} %get-tuple-element.76), channel_id=1, source_target_pairs={{0,1},{2,3},{1,0},{3,2},{4,5},{6,7},{5,4},{7,6},{8,9},{10,11},{9,8... | collective-permute-start | bytes 786440 | tf_op jit(solution)/shard_map/ppermute | solution.py:655
  53.0 7.2 %shard_map.109 = (f32[32,256,128]{2,1,0:T(8,128)S(1)}, f32[2,32,8,128]{3,2,1,0:T(8,128)S(1)}, f32[32,1024]{1,0:T(8,128)S(1)}) custom-call(f32[32,256,128]{2,1,0:T(8,128)S(1)} %get-tuple-element.57.z, bf16[256,768]{1,0:T(8,128)(2,1)S(1)} %get-tuple-element.41.mix, bf16[256,256]{1,0:T(8,128)(2,1)S(1)} %get-tuple-element.42.band_cols, ...), custom_call_target="tpu_custom_call" | custom-call | flops 1000000000 | bytes 10000000 | tf_op jit(solution)/shard_map/pallas_call | solution.py:639
  60.2 0.0 collective-permute-done.5.second
  60.2 0.0 collective-permute-done.4.first
  60.2 0.8 shard_map.110
  61.1 0.7 collective-permute-start.7
  61.8 2.7 %collective-permute-start.6 = (f32[32,8,128]{2,1,0:T(8,128)S(1)}, f32[32,8,128]{2,1,0:T(8,128)S(1)}, u32[]{:S(2)}, u32[]{:S(2)}) collective-permute-start(f32[32,8,128]{2,1,0:T(8,128)S(1)} %get-tuple-element.80), channel_id=1, source_target_pairs={{0,4},{8,12},{16,20},{24,28},{4,0},{12,8},{20,16},{28,24},{1,5},{9... | collective-permute-start | bytes 393224 | tf_op jit(solution)/shard_map/ppermute | solution.py:655
  64.5 3.2 %shard_map.111.w = f32[32,256,128]{2,1,0:T(8,128)S(1)} custom-call(f32[32,256,128]{2,1,0:T(8,128)S(1)} %get-tuple-element.60.u, f32[2,256,256]{2,1,0:T(8,128)S(1)} %get-tuple-element.63.sides, bf16[256,768]{1,0:T(8,128)(2,1)S(1)} %get-tuple-element.47.band_rows), custom_call_target="tpu_custom_call" | custom-call | flops 1000000000 | bytes 10000000 | tf_op jit(solution)/shard_map/pallas_call | solution.py:639
  67.7 0.0 collective-permute-done.7.below
  67.7 0.0 collective-permute-done.6.above
  67.7 4.6 %shard_map.112 = (f32[32,256,128]{2,1,0:T(8,128)S(1)}, f32[32,128]{1,0:T(8,128)S(1)}) custom-call(f32[32,256,128]{2,1,0:T(8,128)S(1)} %shard_map.111.w, f32[32,8,128]{2,1,0:T(8,128)S(1)} %collective-permute-done.6.above, f32[32,8,128]{2,1,0:T(8,128)S(1)} %collective-permute-done.7.below, bf16[4,256,256]{2,1,0:T(8,128)(2,1)S(1)} %get-tuple-element.50.edge, ...), custom_call_target="tpu_custom_call" | custom-call | flops 1000000000 | bytes 10000000 | tf_op jit(solution)/shard_map/pallas_call | solution.py:639
  72.3 12.2 %all_to_all.11 = f32[32,1,128]{2,1,0:T(1,128)S(1)} all-to-all(f32[32,1,128]{2,1,0:T(1,128)S(1)} %bitcast.21), channel_id=1, replica_groups=mesh['row'=8,'col'=4] {'row','col'}, dimensions={0} | all-to-all | bytes 32768 | tf_op jit(solution)/shard_map/all_to_all | solution.py:764
  84.6 4.3 %shard_map.113 = (f32[32,256,128]{2,1,0:T(8,128)}, f32[32,256,128]{2,1,0:T(8,128)}, f32[32,1,1,1024]{3,2,1,0:T(1,128)}) custom-call(f32[32,128]{1,0:T(8,128)S(1)} %bitcast.20, f32[32,256,128]{2,1,0:T(8,128)S(1)} %get-tuple-element.51.b, f32[32,256,128]{2,1,0:T(8,128)S(1)} %get-tuple-element.65.p, f32[32,256,128]{2,1,0:T(8,128)S(1)} %get-tuple-element.69.q, ...), custom_call_target="tpu_custom_call" | custom-call | tf_op jit(solution)/shard_map/pallas_call | solution.py:765
  (4 shorter events, 0.1 us)
Async XLA Ops:
  0.6 20.3 %copy-start.1 = (f32[32,32]{1,0:T(8,128)S(1)}, f32[32,32]{1,0:T(8,128)}, u32[]{:S(2)}) copy-start(f32[32,32]{1,0:T(8,128)} %cov.1) | copy-start | bytes 12292
  14.3 13.4 %collective-permute-start.1 = (f32[256,256]{1,0:T(8,128)S(1)}, f32[256,256]{1,0:T(8,128)S(1)}, u32[]{:S(2)}, u32[]{:S(2)}) collective-permute-start(f32[256,256]{1,0:T(8,128)S(1)} %get-tuple-element.77), channel_id=1, source_target_pairs={{1,2},{2,1},{5,6},{6,5},{9,10},{10,9},{13,14},{14,13},{17,18},{18,... | collective-permute-start | bytes 786440 | tf_op jit(solution)/shard_map/ppermute | solution.py:655
  15.0 12.7 %collective-permute-start = (f32[256,256]{1,0:T(8,128)S(1)}, f32[256,256]{1,0:T(8,128)S(1)}, u32[]{:S(2)}, u32[]{:S(2)}) collective-permute-start(f32[256,256]{1,0:T(8,128)S(1)} %get-tuple-element.78), channel_id=1, source_target_pairs={{0,1},{2,3},{1,0},{3,2},{4,5},{6,7},{5,4},{7,6},{8,9},{10,11},{9,8... | collective-permute-start | bytes 786440 | tf_op jit(solution)/shard_map/ppermute | solution.py:655
  28.6 6.8 %collective-permute-start.3 = (f32[32,8,128]{2,1,0:T(8,128)S(1)}, f32[32,8,128]{2,1,0:T(8,128)S(1)}, u32[]{:S(2)}, u32[]{:S(2)}) collective-permute-start(f32[32,8,128]{2,1,0:T(8,128)S(1)} %get-tuple-element.81), channel_id=1, source_target_pairs={{4,8},{12,16},{20,24},{8,4},{16,12},{24,20},{5,9},{13,17},{21,25},... | collective-permute-start | bytes 393224 | tf_op jit(solution)/shard_map/ppermute | solution.py:655
  29.2 6.2 %collective-permute-start.2 = (f32[32,8,128]{2,1,0:T(8,128)S(1)}, f32[32,8,128]{2,1,0:T(8,128)S(1)}, u32[]{:S(2)}, u32[]{:S(2)}) collective-permute-start(f32[32,8,128]{2,1,0:T(8,128)S(1)} %get-tuple-element.82), channel_id=1, source_target_pairs={{0,4},{8,12},{16,20},{24,28},{4,0},{12,8},{20,16},{28,24},{1,5},{9... | collective-permute-start | bytes 393224 | tf_op jit(solution)/shard_map/ppermute | solution.py:655
  32.1 3.3 %copy-start = (f32[256,128]{1,0:T(8,128)S(1)}, f32[256,128]{1,0:T(8,128)}, u32[]{:S(2)}) copy-start(f32[256,128]{1,0:T(8,128)} %noise.3) | copy-start | bytes 393220
  49.4 10.8 %collective-permute-start.5 = (f32[256,256]{1,0:T(8,128)S(1)}, f32[256,256]{1,0:T(8,128)S(1)}, u32[]{:S(2)}, u32[]{:S(2)}) collective-permute-start(f32[256,256]{1,0:T(8,128)S(1)} %get-tuple-element.75), channel_id=1, source_target_pairs={{1,2},{2,1},{5,6},{6,5},{9,10},{10,9},{13,14},{14,13},{17,18},{18,... | collective-permute-start | bytes 786440 | tf_op jit(solution)/shard_map/ppermute | solution.py:655
  50.1 10.1 %collective-permute-start.4 = (f32[256,256]{1,0:T(8,128)S(1)}, f32[256,256]{1,0:T(8,128)S(1)}, u32[]{:S(2)}, u32[]{:S(2)}) collective-permute-start(f32[256,256]{1,0:T(8,128)S(1)} %get-tuple-element.76), channel_id=1, source_target_pairs={{0,1},{2,3},{1,0},{3,2},{4,5},{6,7},{5,4},{7,6},{8,9},{10,11},{9,8... | collective-permute-start | bytes 786440 | tf_op jit(solution)/shard_map/ppermute | solution.py:655
  61.1 6.6 %collective-permute-start.7 = (f32[32,8,128]{2,1,0:T(8,128)S(1)}, f32[32,8,128]{2,1,0:T(8,128)S(1)}, u32[]{:S(2)}, u32[]{:S(2)}) collective-permute-start(f32[32,8,128]{2,1,0:T(8,128)S(1)} %get-tuple-element.79), channel_id=1, source_target_pairs={{4,8},{12,16},{20,24},{8,4},{16,12},{24,20},{5,9},{13,17},{21,25},... | collective-permute-start | bytes 393224 | tf_op jit(solution)/shard_map/ppermute | solution.py:655
  61.8 6.0 %collective-permute-start.6 = (f32[32,8,128]{2,1,0:T(8,128)S(1)}, f32[32,8,128]{2,1,0:T(8,128)S(1)}, u32[]{:S(2)}, u32[]{:S(2)}) collective-permute-start(f32[32,8,128]{2,1,0:T(8,128)S(1)} %get-tuple-element.80), channel_id=1, source_target_pairs={{0,4},{8,12},{16,20},{24,28},{4,0},{12,8},{20,16},{28,24},{1,5},{9... | collective-permute-start | bytes 393224 | tf_op jit(solution)/shard_map/ppermute | solution.py:655

commit v5 on v4

--- a/solution.py
+++ b/solution.py
@@ -9,6 +9,7 @@
 
 REACH = 8
 LANES = 128
+HALF = LANES // 2
 GROUP = 8
 F32 = jnp.float32
 BF16 = jnp.bfloat16
@@ -33,6 +34,17 @@
 def pair(x):
     high, low = split(x)
     return jnp.concatenate([high, low], axis=1)
+
+
+def doubled(weights):
+    high, low = split(weights)
+    return jnp.concatenate(
+        [
+            jnp.concatenate([high, low], axis=1),
+            jnp.concatenate([high, jnp.zeros_like(low)], axis=1),
+        ],
+        axis=0,
+    )
 
 
 def dot(a, b):
@@ -79,7 +91,7 @@
 def prepare_kernel(
     count, cell_any, offset_any, noise_any, obs_any, base_any,
     base, z, strips, sb, info, rank_out, own, sv, gv, ut, bounds,
-    cell_v, offset_v, noise_v, obs_v, bounds_v, table, sorted_rows, copies,
+    cell_v, offset_v, noise_v, obs_v, bounds_v, table, sorted_rows, shifted_rows, copies,
 ):
     base_copy = pltpu.make_async_copy(base_any, base, copies.at[0])
     base_copy.start()
@@ -136,7 +148,7 @@
         )
         return carry
 
-    lax.fori_loop(0, tiles, sort_block, 0)
+    lax.fori_loop(0, tiles, sort_block, 0, unroll=2)
     ordered_row = sorted_rows[pl.ds(steps, 1), :]
     ordered_live = sorted_rows[pl.ds(steps + 5, 1), :]
     first_row = (iota((groups, slots), 0) * GROUP).astype(F32)
@@ -144,48 +156,54 @@
     until = jnp.where(ordered_row < first_row + GROUP, ordered_live, 0.0)
     low = jnp.sum(before, axis=1, keepdims=True)
     high = jnp.sum(until, axis=1, keepdims=True)
-    start_tile = jnp.where(high > low, jnp.floor(low * (1.0 / LANES)), float(tiles))
-    stop_tile = jnp.where(high > low, jnp.floor((high - 1.0) * (1.0 / LANES)) + 1.0, 0.0)
+    start_tile = jnp.where(high > low, jnp.floor(low * (1.0 / HALF)), float(2 * tiles))
+    reached = jnp.where(high > low, high - HALF * start_tile, 1.0)
+    needed = jnp.floor((reached + (LANES - 1.0)) * (1.0 / LANES))
+    most = jnp.max(needed, axis=0, keepdims=True)
     lane = iota((groups, LANES), 1)
-    span = jnp.max(stop_tile - start_tile, axis=0, keepdims=True)
     bounds_v[...] = jnp.where(
-        lane == 0, start_tile, jnp.where(lane == 1, stop_tile, span)
+        lane == 0, start_tile, jnp.where(lane == 1, needed, most)
     ).astype(jnp.int32)
     bounds_copy = pltpu.make_async_copy(bounds_v, bounds, copies.at[5])
     bounds_copy.start()
-    extra = pl.ds(slots, 2 * LANES)
-    sb[:, :, extra] = jnp.zeros((steps, GROUP, 2 * LANES), F32)
-    info[:, :, extra] = jnp.zeros((2, GROUP, 2 * LANES), F32)
-    sv[:, extra, :] = jnp.zeros((2, 2 * LANES, 2 * LANES), BF16)
-    gv[:, extra] = jnp.zeros((3 * LANES, 2 * LANES), BF16)
-    ut[:, extra] = jnp.zeros((rows, 2 * LANES), F32)
+    lane = iota(shifted_rows.shape[:1] + (LANES,), 1)
     for block in range(tiles):
         lanes = pl.ds(block * LANES, LANES)
-        at_row = sorted_rows[pl.ds(steps, 1), lanes].astype(jnp.int32)
-        at_col = sorted_rows[pl.ds(steps + 1, 1), lanes].astype(jnp.int32)
-        along_row = sorted_rows[pl.ds(steps + 2, 1), lanes]
-        along_col = sorted_rows[pl.ds(steps + 3, 1), lanes]
-        row = iota((rows, LANES), 0)
-        ut[:, lanes] = jnp.where(row == at_row, 1.0 - along_row, 0.0) + jnp.where(
-            row == at_row + 1, along_row, 0.0
-        )
-        col = iota((LANES, LANES), 0)
-        across = jnp.where(col == at_col, 1.0 - along_col, 0.0) + jnp.where(
-            col == at_col + 1, along_col, 0.0
-        )
-        high_part, low_part = split(across)
-        gv[:, lanes] = jnp.concatenate([high_part, high_part, low_part], axis=0)
-        high_part, low_part = split(jnp.transpose(across))
-        sv[0, lanes, :] = jnp.concatenate([high_part, low_part], axis=1)
-        sv[1, lanes, :] = jnp.concatenate([high_part, jnp.zeros_like(low_part)], axis=1)
+        after = jnp.zeros((shifted_rows.shape[0], LANES), F32)
+        if block + 1 < tiles:
+            after = sorted_rows[:, pl.ds((block + 1) * LANES, LANES)]
+        shifted_rows[:, lanes] = pltpu.roll(
+            jnp.where(lane < HALF, after, sorted_rows[:, lanes]), HALF, 1
+        )
         for place in range(2):
             info[place, :, lanes] = jnp.broadcast_to(
                 sorted_rows[pl.ds(steps + 4 + place, 1), lanes], (GROUP, LANES)
             )
+    none = tile_lanes(2 * tiles, 1)
+    sb[:, :, none] = jnp.zeros((steps, GROUP, LANES), F32)
+    ut[:, none] = jnp.zeros((rows, LANES), F32)
+    for target in (sv, gv):
+        target[2 * tiles] = jnp.zeros((2 * LANES, 2 * LANES), BF16)
+    for tile in range(2 * tiles):
+        source = shifted_rows if tile % 2 else sorted_rows
+        place = pl.ds(tile // 2 * LANES, LANES)
+        lanes = pl.ds(tile * LANES, LANES)
+        at_row = source[pl.ds(steps, 1), place].astype(jnp.int32)
+        at_col = source[pl.ds(steps + 1, 1), place].astype(jnp.int32)
+        along_row = source[pl.ds(steps + 2, 1), place]
+        along_col = source[pl.ds(steps + 3, 1), place]
+        row = iota((rows, LANES), 0)
+        ut[:, lanes] = jnp.where(
+            row == at_row, 1.0 - along_row, jnp.where(row == at_row + 1, along_row, 0.0)
+        )
+        col = iota((LANES, LANES), 0)
+        across = jnp.where(
+            col == at_col, 1.0 - along_col, jnp.where(col == at_col + 1, along_col, 0.0)
+        )
+        gv[tile] = doubled(across)
+        sv[tile] = doubled(jnp.transpose(across))
         for step in range(steps):
-            sb[step, :, lanes] = jnp.broadcast_to(
-                sorted_rows[pl.ds(step, 1), lanes], (GROUP, LANES)
-            )
+            sb[step, :, lanes] = jnp.broadcast_to(source[pl.ds(step, 1), place], (GROUP, LANES))
     bounds_copy.wait()
     base_copy.wait()
     scatter_all(base, z, strips, sb, ut, sv, bounds)
@@ -224,14 +242,7 @@
     band_rows[...] = jnp.concatenate([high_part, high_part, low_part], axis=1)
     ca = iota((LANES, LANES), 0)
     cb = iota((LANES, LANES), 1)
-    high_part, low_part = split(taper(ca - cb))
-    band_cols[...] = jnp.concatenate(
-        [
-            jnp.concatenate([high_part, low_part], axis=1),
-            jnp.concatenate([high_part, jnp.zeros_like(low_part)], axis=1),
-        ],
-        axis=0,
-    )
+    band_cols[...] = doubled(taper(ca - cb))
     block_same = (a // GROUP) == (b // GROUP)
     above = 0.25 * taper((a % GROUP) + REACH - (b % GROUP))
     below = 0.25 * taper(REACH + (b % GROUP) - (a % GROUP))
@@ -243,40 +254,39 @@
     return pl.ds(pl.multiple_of(index * LANES, LANES), count * LANES)
 
 
-def spread_tiles(g, first, count, sb, ut, sv):
+def spread_tile(g, index, sb, ut, sv):
     steps = sb.shape[0]
-    lanes = tile_lanes(first, count)
+    lanes = tile_lanes(index, 1)
     weight = ut[rows_of(g), lanes][None]
     left = jnp.concatenate(
         [
-            pair((sb[times, :, lanes] * weight).reshape(GROUP * GROUP, count * LANES))
+            pair((sb[times, :, lanes] * weight).reshape(GROUP * GROUP, LANES))
             for times in chunks(steps)
         ],
         axis=0,
     )
-    right = jnp.concatenate([sv[0, lanes, :], sv[1, lanes, :]], axis=0)
-    return halves(dot(left, right)).reshape(steps, GROUP, LANES)
+    return halves(dot(left, sv[index])).reshape(steps, GROUP, LANES)
 
 
 def scatter_all(base, z, strips, sb, ut, sv, bounds):
     groups = base.shape[1] // GROUP
 
     def run(g, carry):
-        value = base[:, rows_of(g), :] + spread_tiles(g, bounds[g, 0], 2, sb, ut, sv)
+        value = base[:, rows_of(g), :] + spread_tile(g, bounds[g, 0], sb, ut, sv)
         z[:, rows_of(g), :] = value
         pack_group(g, value, strips)
         return carry
 
     lax.fori_loop(0, groups, run, 0, unroll=2)
 
-    @pl.when(bounds[0, 2] > 2)
+    @pl.when(bounds[0, 2] > 1)
     def _():
         def crowded(g, carry):
             def more(index, inner):
-                z[:, rows_of(g), :] += spread_tiles(g, index, 1, sb, ut, sv)
+                z[:, rows_of(g), :] += spread_tile(g, bounds[g, 0] + 2 * index, sb, ut, sv)
                 return inner
 
-            lax.fori_loop(bounds[g, 0] + 2, bounds[g, 1], more, 0)
+            lax.fori_loop(1, bounds[g, 1], more, 0)
             pack_group(g, z[:, rows_of(g), :], strips)
             return carry
 
@@ -409,19 +419,13 @@
     return jnp.where(g == 0, 0, jnp.where(g == groups - 1, 1, 2))
 
 
-def gather_tiles(g, both, first, count, acc, ut, gv):
+def gather_tile(g, both, index, acc, ut, gv):
     steps = acc.shape[0]
-    lanes = tile_lanes(first, count)
-    out = dot(both, gv[:, lanes]).reshape(steps, GROUP, count * LANES)
+    lanes = tile_lanes(index, 1)
+    out = halves(dot(both, gv[index])).reshape(steps, GROUP, LANES)
     weight = ut[rows_of(g), lanes][None]
     for times in chunks(steps):
         acc[times, :, lanes] += out[times.start : times.start + times.size] * weight
-
-
-def left_of(value):
-    steps = value.shape[0]
-    high, low = split(value.reshape(steps * GROUP, LANES))
-    return jnp.concatenate([high, low, high], axis=1)
 
 
 def whole(x):
@@ -438,8 +442,7 @@
 ):
     steps, rows, _ = w.shape
     groups = rows // GROUP
-    slots = sb.shape[2] - 2 * LANES
-    tiles = slots // LANES
+    tiles = info.shape[2] // LANES
     fill_extra(extra, above, below, edge)
     acc[...] = jnp.zeros_like(acc)
 
@@ -451,50 +454,73 @@
         left = []
         for times in chunks(steps):
             value = w[times, here, :] + extra[which, times]
-            left.append(left_of(value))
+            left.append(pair(value.reshape(GROUP * GROUP, LANES)))
             mine = b[times, here, :]
             image = value + spread * mine
             p[times, here, :] = image
             first = first + fold(mine * mine)
             second = second + fold(mine * image)
             third = third + fold(image * image)
-        gather_tiles(g, jnp.concatenate(left, axis=0), bounds[g, 0], 2, acc, ut, gv)
+        gather_tile(g, jnp.concatenate(left, axis=0), bounds[g, 0], acc, ut, gv)
         return first, second, third
 
     zero = jnp.zeros((GROUP, LANES), F32)
     carry = lax.fori_loop(0, groups, run, (zero,) * 3, unroll=2)
 
-    @pl.when(bounds[0, 2] > 2)
+    @pl.when(bounds[0, 2] > 1)
     def _():
         def crowded(g, inner):
             value = w[:, rows_of(g), :] + extra[which_extra(g, groups)]
+            both = pair(value.reshape(steps * GROUP, LANES))
 
             def more(index, innermost):
-                gather_tiles(g, left_of(value), index, 1, acc, ut, gv)
+                gather_tile(g, both, bounds[g, 0] + 2 * index, acc, ut, gv)
                 return innermost
 
-            return lax.fori_loop(bounds[g, 0] + 2, bounds[g, 1], more, inner)
+            return lax.fori_loop(1, bounds[g, 1], more, inner)
 
         lax.fori_loop(0, groups, crowded, 0)
 
+    lane = iota((1, 1, LANES), 2)
+    none = 2 * tiles
+
     def stations(index, carry):
-        lanes = tile_lanes(index, 1)
-        sampled = jnp.sum(acc[:, :, lanes], axis=1, keepdims=True)
-        mine = sb[:, :, lanes]
-        live = info[1, :, lanes][None]
-        image = live * (sampled + info[0, :, lanes][None] * mine) + (1.0 - live) * mine
-        ps[:, :, lanes] = image
-        for step in range(steps):
-            flat_rows[pl.ds(step, 1), lanes] = image[step, 0:1]
+        lanes = tile_lanes(2 * index, 1)
+        place = tile_lanes(index, 1)
+        before = tile_lanes(jnp.where(index == 0, none, 2 * index - 1), 1)
+        after = tile_lanes(2 * index + 1, 1)
+        first, second, third = carry
         part = 1.0 / GROUP
-        return (
-            carry[0] + part * fold(mine * mine),
-            carry[1] + part * fold(mine * image),
-            carry[2] + part * fold(image * image),
-        )
+        live = info[1, :, place][None]
+        spread = live * info[0, :, place][None] + (1.0 - live)
+        for times in chunks(steps):
+            other = jnp.where(lane < HALF, acc[times, :, after], acc[times, :, before])
+            mixed = acc[times, :, lanes] + pltpu.roll(other, HALF, 2)
+            sampled = jnp.sum(mixed, axis=1, keepdims=True)
+            mine = sb[times, :, lanes]
+            image = live * sampled + spread * mine
+            ps[times, :, lanes] = image
+            for step in range(GROUP):
+                flat_rows[pl.ds(times.start + step, 1), place] = image[step, 0:1]
+            first = first + part * fold(mine * mine)
+            second = second + part * fold(mine * image)
+            third = third + part * fold(image * image)
+        return first, second, third
 
     carry = lax.fori_loop(0, tiles, stations, carry)
-    ps[:, :, pl.ds(slots, 2 * LANES)] = jnp.zeros((steps, GROUP, 2 * LANES), F32)
+    ps[:, :, tile_lanes(none, 1)] = jnp.zeros((steps, GROUP, LANES), F32)
+
+    def between(index, inner):
+        for times in chunks(steps):
+            other = jnp.where(
+                lane < HALF,
+                ps[times, :, tile_lanes(2 * index + 2, 1)],
+                ps[times, :, tile_lanes(2 * index, 1)],
+            )
+            ps[times, :, tile_lanes(2 * index + 1, 1)] = pltpu.roll(other, HALF, 2)
+        return inner
+
+    lax.fori_loop(0, tiles, between, 0)
     bb, bp, pp = (whole(x) for x in carry)
     lane = iota((GROUP, LANES), 1)
     value = jnp.where(lane == 0, bb / bp, 0.0)
@@ -511,7 +537,7 @@
 ):
     steps, rows, _ = w.shape
     groups = rows // GROUP
-    tiles = sb.shape[2] // LANES - 2
+    tiles = info.shape[2] // LANES
     fill_extra(extra, above, below, edge)
     shift = jnp.broadcast_to(sums[0:1, 0:1], (GROUP, LANES))[None]
 
@@ -537,10 +563,11 @@
     carry = lax.fori_loop(0, groups, run, (zero,) * 3)
 
     def stations(index, carry):
-        lanes = tile_lanes(index, 1)
+        lanes = tile_lanes(2 * index, 1)
+        place = tile_lanes(index, 1)
         mine = ps[:, :, lanes]
-        live = info[1, :, lanes]
-        scaled = (live * info[0, :, lanes] + (1.0 - live))[None] * mine
+        live = info[1, :, place]
+        scaled = (live * info[0, :, place] + (1.0 - live))[None] * mine
         residual = sb[:, :, lanes] - shift * mine
         part = 1.0 / GROUP
         return (
@@ -665,7 +692,8 @@
     slots = station_obs.shape[3]
     wide = steps * GROUP
     groups = rows // GROUP
-    lanes = slots + 2 * LANES
+    tiles = 2 * (slots // LANES) + 1
+    lanes = tiles * LANES
     devices = lax.axis_size("row") * lax.axis_size("col")
     shape = jax.ShapeDtypeStruct
     field = shape((steps, rows, cols), F32)
@@ -680,11 +708,11 @@
             field,
             strips_shape,
             station_field,
-            shape((2, GROUP, lanes), F32),
+            shape((2, GROUP, slots), F32),
             shape((1, slots), jnp.int32),
             shape((steps, slots), F32),
-            shape((2, lanes, 2 * LANES), BF16),
-            shape((3 * LANES, lanes), BF16),
+            shape((tiles, 2 * LANES, 2 * LANES), BF16),
+            shape((tiles, 2 * LANES, 2 * LANES), BF16),
             shape((rows, lanes), F32),
             shape((groups, LANES), jnp.int32),
         ],
@@ -696,6 +724,7 @@
             pltpu.VMEM((1, 1, slots), F32),
             pltpu.VMEM((steps, 1, 1, slots), F32),
             pltpu.VMEM((groups, LANES), jnp.int32),
+            pltpu.VMEM((steps + 8, slots), F32),
             pltpu.VMEM((steps + 8, slots), F32),
             pltpu.VMEM((steps + 8, slots), F32),
             pltpu.SemaphoreType.DMA((6,)),

time: 89.3 us -> 88.6 us (level)
  Pallas kernels: 57.9 us -> 57 us
where the time goes in v5:
time: 88.6 us; the launch traced here: 88.4 us
  Pallas kernels  57 us (64%)
  starting transfers between devices  17.2 us (19%)
  blocking collectives  12.5 us (14%)
  between operations  1.5 us (2%)
    pallas_call x9, Pallas kernels, call(): pl.pallas_call(kernel, out_shape=outs, in_specs=ins, out_specs=[VMEM] * l...  40.6 us
    ppermute x8, starting transfers between devices, exchange(): lax.ppermute(both[place], axis, found + [(b, a) for a, b in found])  17.2 us
    all_to_all x1, blocking collectives, body(): received = lax.all_to_all(message, ('row', 'col'), 0, 0, tiled=True)  12.5 us
    pallas_call x1, Pallas kernels, body(): pl.pallas_call(prepare_kernel, out_shape=[field, field, strips_shape, sta...  12.1 us
    pallas_call x1, Pallas kernels, body(): pl.pallas_call(final_kernel, out_shape=[field, field, shape((steps, 1, 1,...  4.34 us
  transfers between devices with their start and end apart: 8, of which 0 were waited for; matrix products, arithmetic and copies ran while one was open for 0% of the time, Pallas kernels for 23%

profile of v5, /device:TPU:0, one launch (start us, length us, event | category | flops | bytes accessed | tf_op | source)
XLA Modules:
  0.0 88.4 jit_solution(4831394731888275071)
XLA Ops:
  0.6 0.0 copy-start.1
  1.3 12.1 %shard_map.103 = (f32[32,256,128]{2,1,0:T(8,128)S(1)}, f32[32,256,128]{2,1,0:T(8,128)S(1)}, f32[2,256,256]{2,1,0:T(8,128)S(1)}, f32[32,8,2176]{2,1,0:T(8,128)S(1...) custom-call(s32[1,1]{1,0:T(1,128)S(6)} %copy.12.count, ...), custom_call_target="tpu_custom_call" | custom-call | flops 1000000000 | bytes 10000000 | tf_op jit(solution)/shard_map/pallas_call | solution.py:704
  13.4 0.7 collective-permute-start.1
  14.1 5.9 %collective-permute-start = (f32[256,256]{1,0:T(8,128)S(1)}, f32[256,256]{1,0:T(8,128)S(1)}, u32[]{:S(2)}, u32[]{:S(2)}) collective-permute-start(f32[256,256]{1,0:T(8,128)S(1)} %get-tuple-element.78), channel_id=1, source_target_pairs={{0,1},{2,3},{1,0},{3,2},{4,5},{6,7},{5,4},{7,6},{8,9},{10,11},{9,8... | collective-permute-start | bytes 786440 | tf_op jit(solution)/shard_map/ppermute | solution.py:682
  20.0 0.0 copy-done.1
  20.0 1.2 %shard_map.104 = (bf16[256,768]{1,0:T(8,128)(2,1)S(1)}, bf16[4,256,256]{2,1,0:T(8,128)(2,1)S(1)}, bf16[256,768]{1,0:T(8,128)(2,1)S(1)}, bf16[256,256]{1,0:T(8,128)(2,1)S(1)}, bf16[4,256,256]{2,1,0:T(8,128)(2,1)S(1)}) custom-call(f32[32,32]{1,0:T(8,128)S(1)} %copy-done.1), custom_call_target="tpu_custom_call" | custom-call | flops 1000000000 | bytes 10000000 | tf_op jit(solution)/shard_map/pallas_call | solution.py:666
  21.2 5.5 %shard_map.105 = (f32[32,256,128]{2,1,0:T(8,128)S(1)}, f32[2,32,8,128]{3,2,1,0:T(8,128)S(1)}) custom-call(f32[32,256,128]{2,1,0:T(8,128)S(1)} %get-tuple-element.40.z.z_first, bf16[256,768]{1,0:T(8,128)(2,1)S(1)} %get-tuple-element.41.mix, bf16[256,256]{1,0:T(8,128)(2,1)S(1)} %get-tuple-element.42.band_cols), custom_call_target="tpu_custom_call" | custom-call | flops 1000000000 | bytes 10000000 | tf_op jit(solution)/shard_map/pallas_call | solution.py:666
  26.7 0.0 collective-permute-done.1.second
  26.7 0.0 collective-permute-done.first
  26.7 0.8 shard_map.106
  27.6 0.7 collective-permute-start.3
  28.3 2.9 %collective-permute-start.2 = (f32[32,8,128]{2,1,0:T(8,128)S(1)}, f32[32,8,128]{2,1,0:T(8,128)S(1)}, u32[]{:S(2)}, u32[]{:S(2)}) collective-permute-start(f32[32,8,128]{2,1,0:T(8,128)S(1)} %get-tuple-element.82), channel_id=1, source_target_pairs={{0,4},{8,12},{16,20},{24,28},{4,0},{12,8},{20,16},{28,24},{1,5},{9... | collective-permute-start | bytes 393224 | tf_op jit(solution)/shard_map/ppermute | solution.py:682
  31.2 0.0 copy-start
  31.2 3.2 %shard_map.107.w = f32[32,256,128]{2,1,0:T(8,128)S(1)} custom-call(f32[32,256,128]{2,1,0:T(8,128)S(1)} %get-tuple-element.43.u, f32[2,256,256]{2,1,0:T(8,128)S(1)} %get-tuple-element.48.sides, bf16[256,768]{1,0:T(8,128)(2,1)S(1)} %get-tuple-element.47.band_rows), custom_call_target="tpu_custom_call" | custom-call | flops 1000000000 | bytes 10000000 | tf_op jit(solution)/shard_map/pallas_call | solution.py:666
  34.5 0.0 collective-permute-done.3.below
  34.5 0.0 collective-permute-done.2.above
  34.5 0.0 copy-done
  34.5 14.1 %shard_map.108 = (f32[32,256,128]{2,1,0:T(8,128)S(1)}, f32[32,8,2176]{2,1,0:T(8,128)S(1)}, f32[32,256,128]{2,1,0:T(8,128)S(1)}, f32[2,256,256]{2,1,0:T(8,128)S(1...) custom-call(s32[32,128]{1,0:T(8,128)S(1)} %get-tuple-element.39.bounds, f32[32,256,128]{2,1,0:T(8,128)S(1)} %shard_map.107.w, ...), custom_call_target="tpu_custom_call" | custom-call | flops 1000000000 | bytes 10000000 | tf_op jit(solution)/shard_map/pallas_call | solution.py:666
  48.6 0.7 collective-permute-start.5
  49.3 2.8 %collective-permute-start.4 = (f32[256,256]{1,0:T(8,128)S(1)}, f32[256,256]{1,0:T(8,128)S(1)}, u32[]{:S(2)}, u32[]{:S(2)}) collective-permute-start(f32[256,256]{1,0:T(8,128)S(1)} %get-tuple-element.76), channel_id=1, source_target_pairs={{0,1},{2,3},{1,0},{3,2},{4,5},{6,7},{5,4},{7,6},{8,9},{10,11},{9,8... | collective-permute-start | bytes 786440 | tf_op jit(solution)/shard_map/ppermute | solution.py:682
  52.1 7.2 %shard_map.109 = (f32[32,256,128]{2,1,0:T(8,128)S(1)}, f32[2,32,8,128]{3,2,1,0:T(8,128)S(1)}, f32[32,1024]{1,0:T(8,128)S(1)}) custom-call(f32[32,256,128]{2,1,0:T(8,128)S(1)} %get-tuple-element.57.z, bf16[256,768]{1,0:T(8,128)(2,1)S(1)} %get-tuple-element.41.mix, bf16[256,256]{1,0:T(8,128)(2,1)S(1)} %get-tuple-element.42.band_cols, ...), custom_call_target="tpu_custom_call" | custom-call | flops 1000000000 | bytes 10000000 | tf_op jit(solution)/shard_map/pallas_call | solution.py:666
  59.3 0.0 collective-permute-done.5.second
  59.3 0.0 collective-permute-done.4.first
  59.3 0.8 shard_map.110
  60.2 0.7 collective-permute-start.7
  60.9 2.9 %collective-permute-start.6 = (f32[32,8,128]{2,1,0:T(8,128)S(1)}, f32[32,8,128]{2,1,0:T(8,128)S(1)}, u32[]{:S(2)}, u32[]{:S(2)}) collective-permute-start(f32[32,8,128]{2,1,0:T(8,128)S(1)} %get-tuple-element.80), channel_id=1, source_target_pairs={{0,4},{8,12},{16,20},{24,28},{4,0},{12,8},{20,16},{28,24},{1,5},{9... | collective-permute-start | bytes 393224 | tf_op jit(solution)/shard_map/ppermute | solution.py:682
  63.8 3.2 %shard_map.111.w = f32[32,256,128]{2,1,0:T(8,128)S(1)} custom-call(f32[32,256,128]{2,1,0:T(8,128)S(1)} %get-tuple-element.60.u, f32[2,256,256]{2,1,0:T(8,128)S(1)} %get-tuple-element.63.sides, bf16[256,768]{1,0:T(8,128)(2,1)S(1)} %get-tuple-element.47.band_rows), custom_call_target="tpu_custom_call" | custom-call | flops 1000000000 | bytes 10000000 | tf_op jit(solution)/shard_map/pallas_call | solution.py:666
  67.0 0.0 collective-permute-done.7.below
  67.0 0.0 collective-permute-done.6.above
  67.0 4.6 %shard_map.112 = (f32[32,256,128]{2,1,0:T(8,128)S(1)}, f32[32,128]{1,0:T(8,128)S(1)}) custom-call(f32[32,256,128]{2,1,0:T(8,128)S(1)} %shard_map.111.w, f32[32,8,128]{2,1,0:T(8,128)S(1)} %collective-permute-done.6.above, f32[32,8,128]{2,1,0:T(8,128)S(1)} %collective-permute-done.7.below, bf16[4,256,256]{2,1,0:T(8,128)(2,1)S(1)} %get-tuple-element.50.edge, ...), custom_call_target="tpu_custom_call" | custom-call | flops 1000000000 | bytes 10000000 | tf_op jit(solution)/shard_map/pallas_call | solution.py:666
  71.5 12.5 %all_to_all.11 = f32[32,1,128]{2,1,0:T(1,128)S(1)} all-to-all(f32[32,1,128]{2,1,0:T(1,128)S(1)} %bitcast.21), channel_id=1, replica_groups=mesh['row'=8,'col'=4] {'row','col'}, dimensions={0} | all-to-all | bytes 32768 | tf_op jit(solution)/shard_map/all_to_all | solution.py:793
  84.0 4.3 %shard_map.113 = (f32[32,256,128]{2,1,0:T(8,128)}, f32[32,256,128]{2,1,0:T(8,128)}, f32[32,1,1,1024]{3,2,1,0:T(1,128)}) custom-call(f32[32,128]{1,0:T(8,128)S(1)} %bitcast.20, f32[32,256,128]{2,1,0:T(8,128)S(1)} %get-tuple-element.51.b, f32[32,256,128]{2,1,0:T(8,128)S(1)} %get-tuple-element.65.p, f32[32,256,128]{2,1,0:T(8,128)S(1)} %get-tuple-element.69.q, ...), custom_call_target="tpu_custom_call" | custom-call | tf_op jit(solution)/shard_map/pallas_call | solution.py:794
  (4 shorter events, 0.1 us)
Async XLA Ops:
  0.6 19.4 %copy-start.1 = (f32[32,32]{1,0:T(8,128)S(1)}, f32[32,32]{1,0:T(8,128)}, u32[]{:S(2)}) copy-start(f32[32,32]{1,0:T(8,128)} %cov.1) | copy-start | bytes 12292
  13.4 13.3 %collective-permute-start.1 = (f32[256,256]{1,0:T(8,128)S(1)}, f32[256,256]{1,0:T(8,128)S(1)}, u32[]{:S(2)}, u32[]{:S(2)}) collective-permute-start(f32[256,256]{1,0:T(8,128)S(1)} %get-tuple-element.77), channel_id=1, source_target_pairs={{1,2},{2,1},{5,6},{6,5},{9,10},{10,9},{13,14},{14,13},{17,18},{18,... | collective-permute-start | bytes 786440 | tf_op jit(solution)/shard_map/ppermute | solution.py:682
  14.1 12.6 %collective-permute-start = (f32[256,256]{1,0:T(8,128)S(1)}, f32[256,256]{1,0:T(8,128)S(1)}, u32[]{:S(2)}, u32[]{:S(2)}) collective-permute-start(f32[256,256]{1,0:T(8,128)S(1)} %get-tuple-element.78), channel_id=1, source_target_pairs={{0,1},{2,3},{1,0},{3,2},{4,5},{6,7},{5,4},{7,6},{8,9},{10,11},{9,8... | collective-permute-start | bytes 786440 | tf_op jit(solution)/shard_map/ppermute | solution.py:682
  27.6 6.9 %collective-permute-start.3 = (f32[32,8,128]{2,1,0:T(8,128)S(1)}, f32[32,8,128]{2,1,0:T(8,128)S(1)}, u32[]{:S(2)}, u32[]{:S(2)}) collective-permute-start(f32[32,8,128]{2,1,0:T(8,128)S(1)} %get-tuple-element.81), channel_id=1, source_target_pairs={{4,8},{12,16},{20,24},{8,4},{16,12},{24,20},{5,9},{13,17},{21,25},... | collective-permute-start | bytes 393224 | tf_op jit(solution)/shard_map/ppermute | solution.py:682
  28.3 6.2 %collective-permute-start.2 = (f32[32,8,128]{2,1,0:T(8,128)S(1)}, f32[32,8,128]{2,1,0:T(8,128)S(1)}, u32[]{:S(2)}, u32[]{:S(2)}) collective-permute-start(f32[32,8,128]{2,1,0:T(8,128)S(1)} %get-tuple-element.82), channel_id=1, source_target_pairs={{0,4},{8,12},{16,20},{24,28},{4,0},{12,8},{20,16},{28,24},{1,5},{9... | collective-permute-start | bytes 393224 | tf_op jit(solution)/shard_map/ppermute | solution.py:682
  31.2 3.3 %copy-start = (f32[256,128]{1,0:T(8,128)S(1)}, f32[256,128]{1,0:T(8,128)}, u32[]{:S(2)}) copy-start(f32[256,128]{1,0:T(8,128)} %noise.3) | copy-start | bytes 393220
  48.6 10.7 %collective-permute-start.5 = (f32[256,256]{1,0:T(8,128)S(1)}, f32[256,256]{1,0:T(8,128)S(1)}, u32[]{:S(2)}, u32[]{:S(2)}) collective-permute-start(f32[256,256]{1,0:T(8,128)S(1)} %get-tuple-element.75), channel_id=1, source_target_pairs={{1,2},{2,1},{5,6},{6,5},{9,10},{10,9},{13,14},{14,13},{17,18},{18,... | collective-permute-start | bytes 786440 | tf_op jit(solution)/shard_map/ppermute | solution.py:682
  49.3 10.0 %collective-permute-start.4 = (f32[256,256]{1,0:T(8,128)S(1)}, f32[256,256]{1,0:T(8,128)S(1)}, u32[]{:S(2)}, u32[]{:S(2)}) collective-permute-start(f32[256,256]{1,0:T(8,128)S(1)} %get-tuple-element.76), channel_id=1, source_target_pairs={{0,1},{2,3},{1,0},{3,2},{4,5},{6,7},{5,4},{7,6},{8,9},{10,11},{9,8... | collective-permute-start | bytes 786440 | tf_op jit(solution)/shard_map/ppermute | solution.py:682
  60.2 6.8 %collective-permute-start.7 = (f32[32,8,128]{2,1,0:T(8,128)S(1)}, f32[32,8,128]{2,1,0:T(8,128)S(1)}, u32[]{:S(2)}, u32[]{:S(2)}) collective-permute-start(f32[32,8,128]{2,1,0:T(8,128)S(1)} %get-tuple-element.79), channel_id=1, source_target_pairs={{4,8},{12,16},{20,24},{8,4},{16,12},{24,20},{5,9},{13,17},{21,25},... | collective-permute-start | bytes 393224 | tf_op jit(solution)/shard_map/ppermute | solution.py:682
  60.9 6.1 %collective-permute-start.6 = (f32[32,8,128]{2,1,0:T(8,128)S(1)}, f32[32,8,128]{2,1,0:T(8,128)S(1)}, u32[]{:S(2)}, u32[]{:S(2)}) collective-permute-start(f32[32,8,128]{2,1,0:T(8,128)S(1)} %get-tuple-element.80), channel_id=1, source_target_pairs={{0,4},{8,12},{16,20},{24,28},{4,0},{12,8},{20,16},{28,24},{1,5},{9... | collective-permute-start | bytes 393224 | tf_op jit(solution)/shard_map/ppermute | solution.py:682

commit v6 on v5

--- a/solution.py
+++ b/solution.py
@@ -84,13 +84,32 @@
     return [pl.ds(start, size) for start in range(0, steps, size)]
 
 
+def shifted_block(source, block, blocks):
+    here = source[:, pl.ds(block * LANES, LANES)]
+    after = jnp.zeros_like(here)
+    if block + 1 < blocks:
+        after = source[:, pl.ds((block + 1) * LANES, LANES)]
+    return pltpu.roll(jnp.where(iota(here.shape, 1) < HALF, after, here), HALF, 1)
+
+
+def spread_rows(even, odd, target, steps, blocks):
+    for tile in range(2 * blocks):
+        source = odd if tile % 2 else even
+        place = pl.ds(tile // 2 * LANES, LANES)
+        for step in range(steps):
+            target[step, :, pl.ds(tile * LANES, LANES)] = jnp.broadcast_to(
+                source[pl.ds(step, 1), place], (GROUP, LANES)
+            )
+
+
 def rows_of(g):
     return pl.ds(pl.multiple_of(g * GROUP, GROUP), GROUP)
 
 
 def prepare_kernel(
     count, cell_any, offset_any, noise_any, obs_any, base_any,
-    base, z, strips, sb, info, rank_out, own, sv, gv, ut, bounds,
+    base, z, strips, sb, ordered, info, rank_out, own, sv, gv, spots,
+    band_rows, band_cols, edge, bounds,
     cell_v, offset_v, noise_v, obs_v, bounds_v, table, sorted_rows, shifted_rows, copies,
 ):
     base_copy = pltpu.make_async_copy(base_any, base, copies.at[0])
@@ -103,6 +122,7 @@
     ]
     for copy in small:
         copy.start()
+    fixed_matrices(band_rows, band_cols, edge)
     for copy in small:
         copy.wait()
     cell, noise = cell_v[0], noise_v[0]
@@ -166,52 +186,44 @@
     ).astype(jnp.int32)
     bounds_copy = pltpu.make_async_copy(bounds_v, bounds, copies.at[5])
     bounds_copy.start()
-    lane = iota(shifted_rows.shape[:1] + (LANES,), 1)
+    ordered[...] = sorted_rows[pl.ds(0, steps), :]
+    alive = sorted_rows[pl.ds(steps + 5, 1), :]
+    info[pl.ds(0, 1), :] = alive * sorted_rows[pl.ds(steps + 4, 1), :] + (1.0 - alive)
+    info[pl.ds(1, 1), :] = alive
     for block in range(tiles):
-        lanes = pl.ds(block * LANES, LANES)
-        after = jnp.zeros((shifted_rows.shape[0], LANES), F32)
-        if block + 1 < tiles:
-            after = sorted_rows[:, pl.ds((block + 1) * LANES, LANES)]
-        shifted_rows[:, lanes] = pltpu.roll(
-            jnp.where(lane < HALF, after, sorted_rows[:, lanes]), HALF, 1
-        )
-        for place in range(2):
-            info[place, :, lanes] = jnp.broadcast_to(
-                sorted_rows[pl.ds(steps + 4 + place, 1), lanes], (GROUP, LANES)
-            )
+        shifted_rows[:, pl.ds(block * LANES, LANES)] = shifted_block(sorted_rows, block, tiles)
     none = tile_lanes(2 * tiles, 1)
     sb[:, :, none] = jnp.zeros((steps, GROUP, LANES), F32)
-    ut[:, none] = jnp.zeros((rows, LANES), F32)
+    spots[:, :, none] = jnp.full((2, GROUP, LANES), -1000.0, F32)
     for target in (sv, gv):
         target[2 * tiles] = jnp.zeros((2 * LANES, 2 * LANES), BF16)
+    spread_rows(sorted_rows, shifted_rows, sb, steps, tiles)
     for tile in range(2 * tiles):
         source = shifted_rows if tile % 2 else sorted_rows
         place = pl.ds(tile // 2 * LANES, LANES)
         lanes = pl.ds(tile * LANES, LANES)
-        at_row = source[pl.ds(steps, 1), place].astype(jnp.int32)
+        spots[0, :, lanes] = jnp.broadcast_to(source[pl.ds(steps, 1), place], (GROUP, LANES))
+        spots[1, :, lanes] = jnp.broadcast_to(source[pl.ds(steps + 2, 1), place], (GROUP, LANES))
         at_col = source[pl.ds(steps + 1, 1), place].astype(jnp.int32)
-        along_row = source[pl.ds(steps + 2, 1), place]
         along_col = source[pl.ds(steps + 3, 1), place]
-        row = iota((rows, LANES), 0)
-        ut[:, lanes] = jnp.where(
-            row == at_row, 1.0 - along_row, jnp.where(row == at_row + 1, along_row, 0.0)
-        )
         col = iota((LANES, LANES), 0)
         across = jnp.where(
             col == at_col, 1.0 - along_col, jnp.where(col == at_col + 1, along_col, 0.0)
         )
         gv[tile] = doubled(across)
-        sv[tile] = doubled(jnp.transpose(across))
-        for step in range(steps):
-            sb[step, :, lanes] = jnp.broadcast_to(source[pl.ds(step, 1), place], (GROUP, LANES))
+        if tile % 2 == 0:
+            sv[tile] = doubled(jnp.transpose(across))
+    for tile in range(1, 2 * tiles, 2):
+        for start in (0, LANES):
+            sv[tile, pl.ds(start, HALF), :] = sv[tile - 1, pl.ds(start + HALF, HALF), :]
+            sv[tile, pl.ds(start + HALF, HALF), :] = sv[tile + 1, pl.ds(start, HALF), :]
     bounds_copy.wait()
     base_copy.wait()
-    scatter_all(base, z, strips, sb, ut, sv, bounds)
-
-
-def matrices_kernel(cov, mix, mat, band_rows, band_cols, edge):
+    scatter_all(base, z, strips, sb, spots, sv, bounds)
+
+
+def matrices_kernel(cov, mix, mat):
     steps = cov.shape[0]
-    rows = band_rows.shape[0]
     wide = steps * GROUP
     spread = (iota((wide, steps), 0) // GROUP == iota((wide, steps), 1)).astype(F32)
     spread_t = (iota((steps, wide), 1) // GROUP == iota((steps, wide), 0)).astype(F32)
@@ -236,6 +248,13 @@
         [pltpu.roll(x, LANES - GROUP, 1) for x in cut(far, 1)], axis=1
     )
     mat[2], mat[3] = split(far)
+
+
+def fixed_matrices(band_rows, band_cols, edge):
+    rows = band_rows.shape[0]
+    wide = edge.shape[1]
+    a = iota((wide, wide), 0)
+    b = iota((wide, wide), 1)
     ra = iota((rows, rows), 0)
     rb = iota((rows, rows), 1)
     high_part, low_part = split(0.25 * taper(ra - rb))
@@ -254,10 +273,17 @@
     return pl.ds(pl.multiple_of(index * LANES, LANES), count * LANES)
 
 
-def spread_tile(g, index, sb, ut, sv):
+def row_weights(g, lanes, spots):
+    row = (iota((GROUP, LANES), 0) + g * GROUP).astype(F32)
+    offset = row - spots[0, :, lanes]
+    along = spots[1, :, lanes]
+    return jnp.where(offset == 0.0, 1.0 - along, jnp.where(offset == 1.0, along, 0.0))[None]
+
+
+def spread_tile(g, index, sb, spots, sv):
     steps = sb.shape[0]
     lanes = tile_lanes(index, 1)
-    weight = ut[rows_of(g), lanes][None]
+    weight = row_weights(g, lanes, spots)
     left = jnp.concatenate(
         [
             pair((sb[times, :, lanes] * weight).reshape(GROUP * GROUP, LANES))
@@ -268,11 +294,11 @@
     return halves(dot(left, sv[index])).reshape(steps, GROUP, LANES)
 
 
-def scatter_all(base, z, strips, sb, ut, sv, bounds):
+def scatter_all(base, z, strips, sb, spots, sv, bounds):
     groups = base.shape[1] // GROUP
 
     def run(g, carry):
-        value = base[:, rows_of(g), :] + spread_tile(g, bounds[g, 0], sb, ut, sv)
+        value = base[:, rows_of(g), :] + spread_tile(g, bounds[g, 0], sb, spots, sv)
         z[:, rows_of(g), :] = value
         pack_group(g, value, strips)
         return carry
@@ -283,7 +309,7 @@
     def _():
         def crowded(g, carry):
             def more(index, inner):
-                z[:, rows_of(g), :] += spread_tile(g, bounds[g, 0] + 2 * index, sb, ut, sv)
+                z[:, rows_of(g), :] += spread_tile(g, bounds[g, 0] + 2 * index, sb, spots, sv)
                 return inner
 
             lax.fori_loop(1, bounds[g, 1], more, 0)
@@ -419,11 +445,11 @@
     return jnp.where(g == 0, 0, jnp.where(g == groups - 1, 1, 2))
 
 
-def gather_tile(g, both, index, acc, ut, gv):
+def gather_tile(g, both, index, acc, spots, gv):
     steps = acc.shape[0]
     lanes = tile_lanes(index, 1)
     out = halves(dot(both, gv[index])).reshape(steps, GROUP, LANES)
-    weight = ut[rows_of(g), lanes][None]
+    weight = row_weights(g, lanes, spots)
     for times in chunks(steps):
         acc[times, :, lanes] += out[times.start : times.start + times.size] * weight
 
@@ -436,13 +462,17 @@
     return jnp.sum(x, axis=0)
 
 
+def fold_flat(x):
+    return fold(x.reshape(x.shape[0] // GROUP, GROUP, LANES))
+
+
 def image_one_kernel(
-    bounds, w, above, below, edge, noise, b, sb, info, ut, gv, sv,
-    p, ps, z, strips, sums, flat_rows, acc, extra,
+    bounds, w, above, below, edge, noise, b, ordered, info, spots, gv, sv,
+    p, z, strips, sums, flat_rows, acc, extra, ps, compact, shifted,
 ):
     steps, rows, _ = w.shape
     groups = rows // GROUP
-    tiles = info.shape[2] // LANES
+    tiles = info.shape[1] // LANES
     fill_extra(extra, above, below, edge)
     acc[...] = jnp.zeros_like(acc)
 
@@ -461,7 +491,7 @@
             first = first + fold(mine * mine)
             second = second + fold(mine * image)
             third = third + fold(image * image)
-        gather_tile(g, jnp.concatenate(left, axis=0), bounds[g, 0], acc, ut, gv)
+        gather_tile(g, jnp.concatenate(left, axis=0), bounds[g, 0], acc, spots, gv)
         return first, second, third
 
     zero = jnp.zeros((GROUP, LANES), F32)
@@ -474,53 +504,46 @@
             both = pair(value.reshape(steps * GROUP, LANES))
 
             def more(index, innermost):
-                gather_tile(g, both, bounds[g, 0] + 2 * index, acc, ut, gv)
+                gather_tile(g, both, bounds[g, 0] + 2 * index, acc, spots, gv)
                 return innermost
 
             return lax.fori_loop(1, bounds[g, 1], more, inner)
 
         lax.fori_loop(0, groups, crowded, 0)
 
-    lane = iota((1, 1, LANES), 2)
-    none = 2 * tiles
-
-    def stations(index, carry):
-        lanes = tile_lanes(2 * index, 1)
-        place = tile_lanes(index, 1)
-        before = tile_lanes(jnp.where(index == 0, none, 2 * index - 1), 1)
-        after = tile_lanes(2 * index + 1, 1)
-        first, second, third = carry
-        part = 1.0 / GROUP
-        live = info[1, :, place][None]
-        spread = live * info[0, :, place][None] + (1.0 - live)
-        for times in chunks(steps):
-            other = jnp.where(lane < HALF, acc[times, :, after], acc[times, :, before])
-            mixed = acc[times, :, lanes] + pltpu.roll(other, HALF, 2)
-            sampled = jnp.sum(mixed, axis=1, keepdims=True)
-            mine = sb[times, :, lanes]
-            image = live * sampled + spread * mine
-            ps[times, :, lanes] = image
-            for step in range(GROUP):
-                flat_rows[pl.ds(times.start + step, 1), place] = image[step, 0:1]
-            first = first + part * fold(mine * mine)
-            second = second + part * fold(mine * image)
-            third = third + part * fold(image * image)
-        return first, second, third
-
-    carry = lax.fori_loop(0, tiles, stations, carry)
-    ps[:, :, tile_lanes(none, 1)] = jnp.zeros((steps, GROUP, LANES), F32)
-
-    def between(index, inner):
-        for times in chunks(steps):
-            other = jnp.where(
-                lane < HALF,
-                ps[times, :, tile_lanes(2 * index + 2, 1)],
-                ps[times, :, tile_lanes(2 * index, 1)],
-            )
-            ps[times, :, tile_lanes(2 * index + 1, 1)] = pltpu.roll(other, HALF, 2)
+    wide = steps * GROUP
+    adds = (iota((steps, 2 * wide), 1) % wide // GROUP == iota((steps, 2 * wide), 0)).astype(F32)
+    adds = adds.astype(BF16)
+
+    def fold_rows(index, inner):
+        lanes = tile_lanes(2 * index, 2)
+        high, low = split(acc[:, :, lanes].reshape(wide, 2 * LANES))
+        compact[:, lanes] = dot(adds, jnp.concatenate([high, low], axis=0))
         return inner
 
-    lax.fori_loop(0, tiles, between, 0)
+    lax.fori_loop(0, tiles, fold_rows, 0)
+    lane = iota((steps, LANES), 1)
+    first, second, third = carry
+    for block in range(tiles):
+        place = pl.ds(block * LANES, LANES)
+        before = jnp.zeros((steps, LANES), F32)
+        if block:
+            before = compact[:, pl.ds((2 * block - 1) * LANES, LANES)]
+        after = compact[:, pl.ds((2 * block + 1) * LANES, LANES)]
+        sampled = compact[:, pl.ds(2 * block * LANES, LANES)] + pltpu.roll(
+            jnp.where(lane < HALF, after, before), HALF, 1
+        )
+        mine = ordered[:, place]
+        image = info[pl.ds(1, 1), place] * sampled + info[pl.ds(0, 1), place] * mine
+        flat_rows[:, place] = image
+        first = first + fold_flat(mine * mine)
+        second = second + fold_flat(mine * image)
+        third = third + fold_flat(image * image)
+    carry = first, second, third
+    for block in range(tiles):
+        shifted[:, pl.ds(block * LANES, LANES)] = shifted_block(flat_rows, block, tiles)
+    ps[:, :, tile_lanes(2 * tiles, 1)] = jnp.zeros((steps, GROUP, LANES), F32)
+    spread_rows(flat_rows, shifted, ps, steps, tiles)
     bb, bp, pp = (whole(x) for x in carry)
     lane = iota((GROUP, LANES), 1)
     value = jnp.where(lane == 0, bb / bp, 0.0)
@@ -528,16 +551,16 @@
     value = jnp.where(lane == 2, bp, value)
     value = jnp.where(lane == 3, pp, value)
     sums[...] = value
-    scatter_all(p, z, strips, ps, ut, sv, bounds)
+    scatter_all(p, z, strips, ps, spots, sv, bounds)
 
 
 def image_two_kernel(
-    w, above, below, edge, noise, b, p, z_first, z, sb, ps, info, sums,
+    w, above, below, edge, noise, b, p, z_first, z, ordered, flat_rows, info, sums,
     q, message, extra,
 ):
     steps, rows, _ = w.shape
     groups = rows // GROUP
-    tiles = info.shape[2] // LANES
+    tiles = info.shape[1] // LANES
     fill_extra(extra, above, below, edge)
     shift = jnp.broadcast_to(sums[0:1, 0:1], (GROUP, LANES))[None]
 
@@ -562,21 +585,17 @@
     zero = jnp.zeros((GROUP, LANES), F32)
     carry = lax.fori_loop(0, groups, run, (zero,) * 3)
 
-    def stations(index, carry):
-        lanes = tile_lanes(2 * index, 1)
-        place = tile_lanes(index, 1)
-        mine = ps[:, :, lanes]
-        live = info[1, :, place]
-        scaled = (live * info[0, :, place] + (1.0 - live))[None] * mine
-        residual = sb[:, :, lanes] - shift * mine
-        part = 1.0 / GROUP
-        return (
-            carry[0] + part * fold(residual * residual),
-            carry[1] + part * fold(residual * scaled),
-            carry[2] + part * fold(mine * scaled),
-        )
-
-    carry = lax.fori_loop(0, tiles, stations, carry)
+    first, second, third = carry
+    own_shift = sums[0:1, 0:1]
+    for block in range(tiles):
+        place = pl.ds(block * LANES, LANES)
+        mine = flat_rows[:, place]
+        scaled = info[pl.ds(0, 1), place] * mine
+        residual = ordered[:, place] - own_shift * mine
+        first = first + fold_flat(residual * residual)
+        second = second + fold_flat(residual * scaled)
+        third = third + fold_flat(mine * scaled)
+    carry = first, second, third
     lane = iota((1, LANES), 1)
     value = jnp.where(lane < 4, sums[0:1, :], 0.0)
     for place, x in enumerate(carry):
@@ -701,23 +720,30 @@
     strips_shape = shape((2, rows, wide), F32)
     station_field = shape((steps, GROUP, lanes), F32)
     extra = pltpu.VMEM((3, steps, GROUP, LANES), F32)
-    b, z_first, strips, sb, info, rank, own, sv, gv, ut, bounds = pl.pallas_call(
+    (
+        b, z_first, strips, sb, ordered, info, rank, own, sv, gv, spots,
+        band_rows, band_cols, edge, bounds,
+    ) = pl.pallas_call(
         prepare_kernel,
         out_shape=[
             field,
             field,
             strips_shape,
             station_field,
-            shape((2, GROUP, slots), F32),
+            shape((steps, slots), F32),
+            shape((2, slots), F32),
             shape((1, slots), jnp.int32),
             shape((steps, slots), F32),
             shape((tiles, 2 * LANES, 2 * LANES), BF16),
             shape((tiles, 2 * LANES, 2 * LANES), BF16),
-            shape((rows, lanes), F32),
+            shape((2, GROUP, lanes), F32),
+            shape((rows, 3 * rows), BF16),
+            shape((2 * LANES, 2 * LANES), BF16),
+            shape((4, wide, wide), BF16),
             shape((groups, LANES), jnp.int32),
         ],
         in_specs=[SMEM] + [ANY] * 5,
-        out_specs=[VMEM] * 10 + [SMEM],
+        out_specs=[VMEM] * 14 + [SMEM],
         scratch_shapes=[
             pltpu.VMEM((1, 1, slots), jnp.int32),
             pltpu.VMEM((2, 1, 1, slots), F32),
@@ -738,15 +764,9 @@
             for x in (station_cell, station_offset, station_noise, station_obs, grid_obs)
         ),
     )
-    mix, mat, band_rows, band_cols, edge = call(
+    mix, mat = call(
         matrices_kernel,
-        [
-            shape((wide, 3 * wide), BF16),
-            shape((4, wide, wide), BF16),
-            shape((rows, 3 * rows), BF16),
-            shape((2 * LANES, 2 * LANES), BF16),
-            shape((4, wide, wide), BF16),
-        ],
+        [shape((wide, 3 * wide), BF16), shape((4, wide, wide), BF16)],
         [VMEM],
         (time_cov,),
     )
@@ -774,19 +794,26 @@
         return w, above, below, *unsorted
 
     w, above, below = smooth(z_first, strips)
-    p, ps, z, strips, sums, flat_rows = call(
+    p, z, strips, sums, flat_rows = call(
         image_one_kernel,
-        [field, station_field, field, strips_shape, shape((GROUP, LANES), F32), shape((steps, slots), F32)],
+        [field, field, strips_shape, shape((GROUP, LANES), F32), shape((steps, slots), F32)],
         [SMEM] + [VMEM] * 11,
-        (bounds, w, above, below, edge, grid_noise, b, sb, info, ut, gv, sv),
-        [pltpu.VMEM((steps, GROUP, lanes), F32), extra],
+        (bounds, w, above, below, edge, grid_noise, b, ordered, info, spots, gv, sv),
+        [
+            pltpu.VMEM((steps, GROUP, lanes), F32),
+            extra,
+            pltpu.VMEM((steps, GROUP, lanes), F32),
+            pltpu.VMEM((steps, lanes), F32),
+            pltpu.VMEM((steps, slots), F32),
+        ],
+        limit=12,
     )
     w, above, below, unsorted = smooth(z, strips, flat_rows, rank)
     q, message = call(
         image_two_kernel,
         [field, shape((devices, LANES), F32)],
         [VMEM] * 13,
-        (w, above, below, edge, grid_noise, b, p, z_first, z, sb, ps, info, sums),
+        (w, above, below, edge, grid_noise, b, p, z_first, z, ordered, flat_rows, info, sums),
         [extra],
         limit=4,
     )

time: 88.6 us -> 86.2 us (0.973)
  Pallas kernels: 57 us -> 54.4 us
    pallas_call x9, Pallas kernels: 40.6 us -> 38.1 us  [call(): pl.pallas_call(kernel, out_shape=outs, in_specs=ins, out_specs=[VMEM] * l...]
where the time goes in v6:
time: 86.2 us; the launch traced here: 85.9 us
  Pallas kernels  54.4 us (63%)
  starting transfers between devices  17.3 us (20%)
  blocking collectives  12.5 us (15%)
  between operations  1.51 us (2%)
    pallas_call x9, Pallas kernels, call(): pl.pallas_call(kernel, out_shape=outs, in_specs=ins, out_specs=[VMEM] * l...  38.1 us
    ppermute x8, starting transfers between devices, exchange(): lax.ppermute(both[place], axis, found + [(b, a) for a, b in found])  17.3 us
    all_to_all x1, blocking collectives, body(): received = lax.all_to_all(message, ('row', 'col'), 0, 0, tiled=True)  12.5 us
    pallas_call x1, Pallas kernels, body(): pl.pallas_call(prepare_kernel, out_shape=[field, field, strips_shape, sta...  11.9 us
    pallas_call x1, Pallas kernels, body(): pl.pallas_call(final_kernel, out_shape=[field, field, shape((steps, 1, 1,...  4.34 us
  transfers between devices with their start and end apart: 8, of which 0 were waited for; matrix products, arithmetic and copies ran while one was open for 0% of the time, Pallas kernels for 23%

profile of v6, /device:TPU:0, one launch (start us, length us, event | category | flops | bytes accessed | tf_op | source)
XLA Modules:
  0.0 85.9 jit_solution(9153071354566272571)
XLA Ops:
  0.6 0.0 copy-start.1
  1.3 11.9 %shard_map.103 = (f32[32,256,128]{2,1,0:T(8,128)S(1)}, f32[32,256,128]{2,1,0:T(8,128)S(1)}, f32[2,256,256]{2,1,0:T(8,128)S(1)}, f32[32,8,2176]{2,1,0:T(8,128)}, ...) custom-call(s32[1,1]{1,0:T(1,128)S(6)} %copy.12.count, ...), custom_call_target="tpu_custom_call" | custom-call | flops 1000000000 | bytes 10000000 | tf_op jit(solution)/shard_map/pallas_call | solution.py:726
  13.3 0.7 collective-permute-start.1
  13.9 5.9 %collective-permute-start = (f32[256,256]{1,0:T(8,128)S(1)}, f32[256,256]{1,0:T(8,128)S(1)}, u32[]{:S(2)}, u32[]{:S(2)}) collective-permute-start(f32[256,256]{1,0:T(8,128)S(1)} %get-tuple-element.76), channel_id=1, source_target_pairs={{0,1},{2,3},{1,0},{3,2},{4,5},{6,7},{5,4},{7,6},{8,9},{10,11},{9,8... | collective-permute-start | bytes 786440 | tf_op jit(solution)/shard_map/ppermute | solution.py:701
  19.9 0.0 copy-done.1
  19.9 1.0 %shard_map.104 = (bf16[256,768]{1,0:T(8,128)(2,1)S(1)}, bf16[4,256,256]{2,1,0:T(8,128)(2,1)S(1)}) custom-call(f32[32,32]{1,0:T(8,128)S(1)} %copy-done.1), custom_call_target="tpu_custom_call" | custom-call | flops 1000000000 | bytes 10000000 | tf_op jit(solution)/shard_map/pallas_call | solution.py:685
  20.9 5.5 %shard_map.105 = (f32[32,256,128]{2,1,0:T(8,128)S(1)}, f32[2,32,8,128]{3,2,1,0:T(8,128)S(1)}) custom-call(f32[32,256,128]{2,1,0:T(8,128)S(1)} %get-tuple-element.39.z.z_first, bf16[256,768]{1,0:T(8,128)(2,1)S(1)} %get-tuple-element.40.mix, bf16[256,256]{1,0:T(8,128)(2,1)S(1)} %get-tuple-element.41.band_cols), custom_call_target="tpu_custom_call" | custom-call | flops 1000000000 | bytes 10000000 | tf_op jit(solution)/shard_map/pallas_call | solution.py:685
  26.4 0.0 collective-permute-done.1.second
  26.4 0.0 collective-permute-done.first
  26.5 0.8 shard_map.106
  27.3 0.7 collective-permute-start.3
  28.0 2.9 %collective-permute-start.2 = (f32[32,8,128]{2,1,0:T(8,128)S(1)}, f32[32,8,128]{2,1,0:T(8,128)S(1)}, u32[]{:S(2)}, u32[]{:S(2)}) collective-permute-start(f32[32,8,128]{2,1,0:T(8,128)S(1)} %get-tuple-element.80), channel_id=1, source_target_pairs={{0,4},{8,12},{16,20},{24,28},{4,0},{12,8},{20,16},{28,24},{1,5},{9... | collective-permute-start | bytes 393224 | tf_op jit(solution)/shard_map/ppermute | solution.py:701
  30.9 0.0 copy-start
  30.9 3.2 %shard_map.107.w = f32[32,256,128]{2,1,0:T(8,128)S(1)} custom-call(f32[32,256,128]{2,1,0:T(8,128)S(1)} %get-tuple-element.42.u, f32[2,256,256]{2,1,0:T(8,128)S(1)} %get-tuple-element.47.sides, bf16[256,768]{1,0:T(8,128)(2,1)S(1)} %get-tuple-element.46.band_rows), custom_call_target="tpu_custom_call" | custom-call | flops 1000000000 | bytes 10000000 | tf_op jit(solution)/shard_map/pallas_call | solution.py:685
  34.1 0.0 collective-permute-done.3.below
  34.1 0.0 collective-permute-done.2.above
  34.1 0.0 copy-done
  34.1 12.1 %shard_map.108 = (f32[32,256,128]{2,1,0:T(8,128)S(1)}, f32[32,256,128]{2,1,0:T(8,128)S(1)}, f32[2,256,256]{2,1,0:T(8,128)S(1)}, f32[8,128]{1,0:T(8,128)S(1)}, f32[32,1024]{1,0:T(8,128)S(1)}) custom-call(s32[32,128]{1,0:T(8,128)S(1)} %get-tuple-element.38.bounds, f32[32,256,128]{2,1,0:T(8,128)S(1)} %shard_map.107.w, ...), custom_call_target="tpu_custom_call" | custom-call | flops 1000000000 | bytes 10000000 | tf_op jit(solution)/shard_map/pallas_call | solution.py:685
  46.3 0.7 collective-permute-start.5
  47.0 2.9 %collective-permute-start.4 = (f32[256,256]{1,0:T(8,128)S(1)}, f32[256,256]{1,0:T(8,128)S(1)}, u32[]{:S(2)}, u32[]{:S(2)}) collective-permute-start(f32[256,256]{1,0:T(8,128)S(1)} %get-tuple-element.74), channel_id=1, source_target_pairs={{0,1},{2,3},{1,0},{3,2},{4,5},{6,7},{5,4},{7,6},{8,9},{10,11},{9,8... | collective-permute-start | bytes 786440 | tf_op jit(solution)/shard_map/ppermute | solution.py:701
  49.9 7.2 %shard_map.109 = (f32[32,256,128]{2,1,0:T(8,128)S(1)}, f32[2,32,8,128]{3,2,1,0:T(8,128)S(1)}, f32[32,1024]{1,0:T(8,128)S(1)}) custom-call(f32[32,256,128]{2,1,0:T(8,128)S(1)} %get-tuple-element.56.z, bf16[256,768]{1,0:T(8,128)(2,1)S(1)} %get-tuple-element.40.mix, bf16[256,256]{1,0:T(8,128)(2,1)S(1)} %get-tuple-element.41.band_cols, ...), custom_call_target="tpu_custom_call" | custom-call | flops 1000000000 | bytes 10000000 | tf_op jit(solution)/shard_map/pallas_call | solution.py:685
  57.1 0.0 collective-permute-done.5.second
  57.1 0.0 collective-permute-done.4.first
  57.2 0.8 shard_map.110
  58.0 0.7 collective-permute-start.7
  58.7 2.9 %collective-permute-start.6 = (f32[32,8,128]{2,1,0:T(8,128)S(1)}, f32[32,8,128]{2,1,0:T(8,128)S(1)}, u32[]{:S(2)}, u32[]{:S(2)}) collective-permute-start(f32[32,8,128]{2,1,0:T(8,128)S(1)} %get-tuple-element.78), channel_id=1, source_target_pairs={{0,4},{8,12},{16,20},{24,28},{4,0},{12,8},{20,16},{28,24},{1,5},{9... | collective-permute-start | bytes 393224 | tf_op jit(solution)/shard_map/ppermute | solution.py:701
  61.6 3.2 %shard_map.111.w = f32[32,256,128]{2,1,0:T(8,128)S(1)} custom-call(f32[32,256,128]{2,1,0:T(8,128)S(1)} %get-tuple-element.59.u, f32[2,256,256]{2,1,0:T(8,128)S(1)} %get-tuple-element.62.sides, bf16[256,768]{1,0:T(8,128)(2,1)S(1)} %get-tuple-element.46.band_rows), custom_call_target="tpu_custom_call" | custom-call | flops 1000000000 | bytes 10000000 | tf_op jit(solution)/shard_map/pallas_call | solution.py:685
  64.8 0.0 collective-permute-done.7.below
  64.8 0.0 collective-permute-done.6.above
  64.9 4.2 %shard_map.112 = (f32[32,256,128]{2,1,0:T(8,128)S(1)}, f32[32,128]{1,0:T(8,128)S(1)}) custom-call(f32[32,256,128]{2,1,0:T(8,128)S(1)} %shard_map.111.w, f32[32,8,128]{2,1,0:T(8,128)S(1)} %collective-permute-done.6.above, f32[32,8,128]{2,1,0:T(8,128)S(1)} %collective-permute-done.7.below, bf16[4,256,256]{2,1,0:T(8,128)(2,1)S(1)} %get-tuple-element.49.edge, ...), custom_call_target="tpu_custom_call" | custom-call | flops 1000000000 | bytes 10000000 | tf_op jit(solution)/shard_map/pallas_call | solution.py:685
  69.1 12.5 %all_to_all.11 = f32[32,1,128]{2,1,0:T(1,128)S(1)} all-to-all(f32[32,1,128]{2,1,0:T(1,128)S(1)} %bitcast.21), channel_id=1, replica_groups=mesh['row'=8,'col'=4] {'row','col'}, dimensions={0} | all-to-all | bytes 32768 | tf_op jit(solution)/shard_map/all_to_all | solution.py:820
  81.6 4.3 %shard_map.113 = (f32[32,256,128]{2,1,0:T(8,128)}, f32[32,256,128]{2,1,0:T(8,128)}, f32[32,1,1,1024]{3,2,1,0:T(1,128)}) custom-call(f32[32,128]{1,0:T(8,128)S(1)} %bitcast.20, f32[32,256,128]{2,1,0:T(8,128)S(1)} %get-tuple-element.50.b, f32[32,256,128]{2,1,0:T(8,128)S(1)} %get-tuple-element.64.p, f32[32,256,128]{2,1,0:T(8,128)S(1)} %get-tuple-element.67.q, ...), custom_call_target="tpu_custom_call" | custom-call | tf_op jit(solution)/shard_map/pallas_call | solution.py:821
  (4 shorter events, 0.1 us)
Async XLA Ops:
  0.6 19.3 %copy-start.1 = (f32[32,32]{1,0:T(8,128)S(1)}, f32[32,32]{1,0:T(8,128)}, u32[]{:S(2)}) copy-start(f32[32,32]{1,0:T(8,128)} %cov.1) | copy-start | bytes 12292
  13.3 13.2 %collective-permute-start.1 = (f32[256,256]{1,0:T(8,128)S(1)}, f32[256,256]{1,0:T(8,128)S(1)}, u32[]{:S(2)}, u32[]{:S(2)}) collective-permute-start(f32[256,256]{1,0:T(8,128)S(1)} %get-tuple-element.75), channel_id=1, source_target_pairs={{1,2},{2,1},{5,6},{6,5},{9,10},{10,9},{13,14},{14,13},{17,18},{18,... | collective-permute-start | bytes 786440 | tf_op jit(solution)/shard_map/ppermute | solution.py:701
  13.9 12.5 %collective-permute-start = (f32[256,256]{1,0:T(8,128)S(1)}, f32[256,256]{1,0:T(8,128)S(1)}, u32[]{:S(2)}, u32[]{:S(2)}) collective-permute-start(f32[256,256]{1,0:T(8,128)S(1)} %get-tuple-element.76), channel_id=1, source_target_pairs={{0,1},{2,3},{1,0},{3,2},{4,5},{6,7},{5,4},{7,6},{8,9},{10,11},{9,8... | collective-permute-start | bytes 786440 | tf_op jit(solution)/shard_map/ppermute | solution.py:701
  27.3 6.8 %collective-permute-start.3 = (f32[32,8,128]{2,1,0:T(8,128)S(1)}, f32[32,8,128]{2,1,0:T(8,128)S(1)}, u32[]{:S(2)}, u32[]{:S(2)}) collective-permute-start(f32[32,8,128]{2,1,0:T(8,128)S(1)} %get-tuple-element.79), channel_id=1, source_target_pairs={{4,8},{12,16},{20,24},{8,4},{16,12},{24,20},{5,9},{13,17},{21,25},... | collective-permute-start | bytes 393224 | tf_op jit(solution)/shard_map/ppermute | solution.py:701
  28.0 6.1 %collective-permute-start.2 = (f32[32,8,128]{2,1,0:T(8,128)S(1)}, f32[32,8,128]{2,1,0:T(8,128)S(1)}, u32[]{:S(2)}, u32[]{:S(2)}) collective-permute-start(f32[32,8,128]{2,1,0:T(8,128)S(1)} %get-tuple-element.80), channel_id=1, source_target_pairs={{0,4},{8,12},{16,20},{24,28},{4,0},{12,8},{20,16},{28,24},{1,5},{9... | collective-permute-start | bytes 393224 | tf_op jit(solution)/shard_map/ppermute | solution.py:701
  30.9 3.2 %copy-start = (f32[256,128]{1,0:T(8,128)S(1)}, f32[256,128]{1,0:T(8,128)}, u32[]{:S(2)}) copy-start(f32[256,128]{1,0:T(8,128)} %noise.3) | copy-start | bytes 393220
  46.3 10.8 %collective-permute-start.5 = (f32[256,256]{1,0:T(8,128)S(1)}, f32[256,256]{1,0:T(8,128)S(1)}, u32[]{:S(2)}, u32[]{:S(2)}) collective-permute-start(f32[256,256]{1,0:T(8,128)S(1)} %get-tuple-element.73), channel_id=1, source_target_pairs={{1,2},{2,1},{5,6},{6,5},{9,10},{10,9},{13,14},{14,13},{17,18},{18,... | collective-permute-start | bytes 786440 | tf_op jit(solution)/shard_map/ppermute | solution.py:701
  47.0 10.1 %collective-permute-start.4 = (f32[256,256]{1,0:T(8,128)S(1)}, f32[256,256]{1,0:T(8,128)S(1)}, u32[]{:S(2)}, u32[]{:S(2)}) collective-permute-start(f32[256,256]{1,0:T(8,128)S(1)} %get-tuple-element.74), channel_id=1, source_target_pairs={{0,1},{2,3},{1,0},{3,2},{4,5},{6,7},{5,4},{7,6},{8,9},{10,11},{9,8... | collective-permute-start | bytes 786440 | tf_op jit(solution)/shard_map/ppermute | solution.py:701
  58.0 6.8 %collective-permute-start.7 = (f32[32,8,128]{2,1,0:T(8,128)S(1)}, f32[32,8,128]{2,1,0:T(8,128)S(1)}, u32[]{:S(2)}, u32[]{:S(2)}) collective-permute-start(f32[32,8,128]{2,1,0:T(8,128)S(1)} %get-tuple-element.77), channel_id=1, source_target_pairs={{4,8},{12,16},{20,24},{8,4},{16,12},{24,20},{5,9},{13,17},{21,25},... | collective-permute-start | bytes 393224 | tf_op jit(solution)/shard_map/ppermute | solution.py:701
  58.7 6.1 %collective-permute-start.6 = (f32[32,8,128]{2,1,0:T(8,128)S(1)}, f32[32,8,128]{2,1,0:T(8,128)S(1)}, u32[]{:S(2)}, u32[]{:S(2)}) collective-permute-start(f32[32,8,128]{2,1,0:T(8,128)S(1)} %get-tuple-element.78), channel_id=1, source_target_pairs={{0,4},{8,12},{16,20},{24,28},{4,0},{12,8},{20,16},{28,24},{1,5},{9... | collective-permute-start | bytes 393224 | tf_op jit(solution)/shard_map/ppermute | solution.py:701

commit v7 on v6

--- a/solution.py
+++ b/solution.py
@@ -112,8 +112,6 @@
     band_rows, band_cols, edge, bounds,
     cell_v, offset_v, noise_v, obs_v, bounds_v, table, sorted_rows, shifted_rows, copies,
 ):
-    base_copy = pltpu.make_async_copy(base_any, base, copies.at[0])
-    base_copy.start()
     small = [
         pltpu.make_async_copy(source, target, copies.at[1 + place])
         for place, (source, target) in enumerate(
@@ -122,6 +120,8 @@
     ]
     for copy in small:
         copy.start()
+    base_copy = pltpu.make_async_copy(base_any, base, copies.at[0])
+    base_copy.start()
     fixed_matrices(band_rows, band_cols, edge)
     for copy in small:
         copy.wait()
@@ -303,7 +303,7 @@
         pack_group(g, value, strips)
         return carry
 
-    lax.fori_loop(0, groups, run, 0, unroll=2)
+    lax.fori_loop(0, groups, run, 0, unroll=8)
 
     @pl.when(bounds[0, 2] > 1)
     def _():
@@ -363,7 +363,7 @@
                 ]
         return carry
 
-    lax.fori_loop(0, groups // 4, across, 0)
+    lax.fori_loop(0, groups // 4, across, 0, unroll=4)
 
     def mixing(two, carry):
         right = jnp.concatenate([y[two, 0], y[two, 1], y[two, 0]], axis=0)
@@ -372,7 +372,7 @@
         u[:, rows_of(2 * two + 1), :] = out[:, LANES:].reshape(steps, GROUP, LANES)
         return carry
 
-    lax.fori_loop(0, groups // 2, mixing, 0, unroll=2)
+    lax.fori_loop(0, groups // 2, mixing, 0, unroll=8)
     u_edges[0] = u[:, pl.ds(0, GROUP), :]
     u_edges[1] = u[:, pl.ds(rows - GROUP, GROUP), :]
 
@@ -407,7 +407,7 @@
         w[2 * two + 1] = out[:, LANES:] + unpack(sides, everything, rows, 2 * two + 1)
         return carry
 
-    lax.fori_loop(0, steps // 2, along, 0, unroll=2)
+    lax.fori_loop(0, steps // 2, along, 0, unroll=8)
 
 
 def edge_kernel(first, second, u_edges, mat, band_rows, sides, full_edges):
@@ -583,7 +583,7 @@
         return first, second, third
 
     zero = jnp.zeros((GROUP, LANES), F32)
-    carry = lax.fori_loop(0, groups, run, (zero,) * 3)
+    carry = lax.fori_loop(0, groups, run, (zero,) * 3, unroll=1)
 
     first, second, third = carry
     own_shift = sums[0:1, 0:1]

time: 86.2 us -> 77.6 us (0.900)
  Pallas kernels: 54.4 us -> 41.6 us
  waiting for transfers between devices: 0.02 us -> 3.35 us
    pallas_call x9, Pallas kernels: 38.1 us -> 29.4 us  [call(): pl.pallas_call(kernel, out_shape=outs, in_specs=ins, out_specs=[VMEM] * l...]
    pallas_call x1, Pallas kernels: 11.9 us -> 7.86 us  [body(): pl.pallas_call(prepare_kernel, out_shape=[field, field, strips_shape, sta...]
    ppermute x8, waiting for transfers between devices: 0.02 us -> 3.35 us  [exchange(): lax.ppermute(both[place], axis, found + [(b, a) for a, b in found])]
  transfers between devices with their start and end apart: 8 -> 8, of which waited for: 0 -> 2; matrix products, arithmetic and copies ran while one was open for 0% -> 0% of each run, Pallas kernels for 23% -> 18%
where the time goes in v7:
time: 77.6 us; the launch traced here: 77.3 us
  Pallas kernels  41.6 us (54%)
  starting transfers between devices  17.9 us (23%)
  blocking collectives  12.9 us (17%)
  waiting for transfers between devices  3.35 us (4%)
  between operations  1.49 us (2%)
    pallas_call x9, Pallas kernels, call(): pl.pallas_call(kernel, out_shape=outs, in_specs=ins, out_specs=[VMEM] * l...  29.4 us
    ppermute x8, starting transfers between devices, exchange(): lax.ppermute(both[place], axis, found + [(b, a) for a, b in found])  17.9 us
    all_to_all x1, blocking collectives, body(): received = lax.all_to_all(message, ('row', 'col'), 0, 0, tiled=True)  12.9 us
    pallas_call x1, Pallas kernels, body(): pl.pallas_call(prepare_kernel, out_shape=[field, field, strips_shape, sta...  7.86 us
    pallas_call x1, Pallas kernels, body(): pl.pallas_call(final_kernel, out_shape=[field, field, shape((steps, 1, 1,...  4.34 us
    ppermute x8, waiting for transfers between devices, exchange(): lax.ppermute(both[place], axis, found + [(b, a) for a, b in found])  3.35 us
  transfers between devices with their start and end apart: 8, of which 2 were waited for; matrix products, arithmetic and copies ran while one was open for 0% of the time, Pallas kernels for 18%

profile of v7, /device:TPU:0, one launch (start us, length us, event | category | flops | bytes accessed | tf_op | source)
XLA Modules:
  0.0 77.3 jit_solution(3194747383411794125)
XLA Ops:
  0.6 0.0 copy-start.1
  1.3 7.9 %shard_map.103 = (f32[32,256,128]{2,1,0:T(8,128)S(1)}, f32[32,256,128]{2,1,0:T(8,128)S(1)}, f32[2,256,256]{2,1,0:T(8,128)S(1)}, f32[32,8,2176]{2,1,0:T(8,128)}, ...) custom-call(s32[1,1]{1,0:T(1,128)S(6)} %copy.12.count, ...), custom_call_target="tpu_custom_call" | custom-call | flops 1000000000 | bytes 10000000 | tf_op jit(solution)/shard_map/pallas_call | solution.py:726
  9.2 0.7 collective-permute-start.1
  9.9 5.9 %collective-permute-start = (f32[256,256]{1,0:T(8,128)S(1)}, f32[256,256]{1,0:T(8,128)S(1)}, u32[]{:S(2)}, u32[]{:S(2)}) collective-permute-start(f32[256,256]{1,0:T(8,128)S(1)} %get-tuple-element.76), channel_id=1, source_target_pairs={{0,1},{2,3},{1,0},{3,2},{4,5},{6,7},{5,4},{7,6},{8,9},{10,11},{9,8... | collective-permute-start | bytes 786440 | tf_op jit(solution)/shard_map/ppermute | solution.py:701
  15.8 0.0 copy-done.1
  15.8 1.0 %shard_map.104 = (bf16[256,768]{1,0:T(8,128)(2,1)S(1)}, bf16[4,256,256]{2,1,0:T(8,128)(2,1)S(1)}) custom-call(f32[32,32]{1,0:T(8,128)S(1)} %copy-done.1), custom_call_target="tpu_custom_call" | custom-call | flops 1000000000 | bytes 10000000 | tf_op jit(solution)/shard_map/pallas_call | solution.py:685
  16.8 3.5 %shard_map.105 = (f32[32,256,128]{2,1,0:T(8,128)S(1)}, f32[2,32,8,128]{3,2,1,0:T(8,128)S(1)}) custom-call(f32[32,256,128]{2,1,0:T(8,128)S(1)} %get-tuple-element.39.z.z_first, bf16[256,768]{1,0:T(8,128)(2,1)S(1)} %get-tuple-element.40.mix, bf16[256,256]{1,0:T(8,128)(2,1)S(1)} %get-tuple-element.41.band_cols), custom_call_target="tpu_custom_call" | custom-call | flops 1000000000 | bytes 10000000 | tf_op jit(solution)/shard_map/pallas_call | solution.py:685
  20.4 0.0 collective-permute-done.1.second
  20.4 1.5 %collective-permute-done.first = f32[256,256]{1,0:T(8,128)S(1)} collective-permute-done((f32[256,256]{1,0:T(8,128)S(1)}, f32[256,256]{1,0:T(8,128)S(1)}, u32[]{:S(2)}, u32[]{:S(2)}) %collective-permute-start) | collective-permute-done | bytes 262176 | tf_op jit(solution)/shard_map/ppermute | solution.py:701
  21.9 0.8 %shard_map.106 = (f32[2,256,256]{2,1,0:T(8,128)S(1)}, f32[2,32,8,128]{3,2,1,0:T(8,128)S(1)}) custom-call(f32[256,256]{1,0:T(8,128)S(1)} %collective-permute-done.first, f32[256,256]{1,0:T(8,128)S(1)} %collective-permute-done.1.second, f32[2,32,8,128]{3,2,1,0:T(8,128)S(1)} %get-tuple-element.44.u_edges, bf16[4,256,256]{2,1,0:T(8,128)(2,1)S(1)} %get-tuple-element.45.mat, ...), custom_call_target="tpu_custom_call" | custom-call | flops 1000000000 | bytes 10000000 | tf_op jit(solution)/shard_map/pallas_call | solution.py:685
  22.7 0.7 collective-permute-start.3
  23.4 2.9 %collective-permute-start.2 = (f32[32,8,128]{2,1,0:T(8,128)S(1)}, f32[32,8,128]{2,1,0:T(8,128)S(1)}, u32[]{:S(2)}, u32[]{:S(2)}) collective-permute-start(f32[32,8,128]{2,1,0:T(8,128)S(1)} %get-tuple-element.80), channel_id=1, source_target_pairs={{0,4},{8,12},{16,20},{24,28},{4,0},{12,8},{20,16},{28,24},{1,5},{9... | collective-permute-start | bytes 393224 | tf_op jit(solution)/shard_map/ppermute | solution.py:701
  26.3 0.0 copy-start
  26.3 2.1 %shard_map.107.w = f32[32,256,128]{2,1,0:T(8,128)S(1)} custom-call(f32[32,256,128]{2,1,0:T(8,128)S(1)} %get-tuple-element.42.u, f32[2,256,256]{2,1,0:T(8,128)S(1)} %get-tuple-element.47.sides, bf16[256,768]{1,0:T(8,128)(2,1)S(1)} %get-tuple-element.46.band_rows), custom_call_target="tpu_custom_call" | custom-call | flops 1000000000 | bytes 10000000 | tf_op jit(solution)/shard_map/pallas_call | solution.py:685
  28.5 0.0 collective-permute-done.3.below
  28.5 0.0 collective-permute-done.2.above
  28.5 0.0 copy-done
  28.5 9.4 %shard_map.108 = (f32[32,256,128]{2,1,0:T(8,128)S(1)}, f32[32,256,128]{2,1,0:T(8,128)S(1)}, f32[2,256,256]{2,1,0:T(8,128)S(1)}, f32[8,128]{1,0:T(8,128)S(1)}, f32[32,1024]{1,0:T(8,128)S(1)}) custom-call(s32[32,128]{1,0:T(8,128)S(1)} %get-tuple-element.38.bounds, f32[32,256,128]{2,1,0:T(8,128)S(1)} %shard_map.107.w, ...), custom_call_target="tpu_custom_call" | custom-call | flops 1000000000 | bytes 10000000 | tf_op jit(solution)/shard_map/pallas_call | solution.py:685
  37.9 0.7 collective-permute-start.5
  38.6 3.4 %collective-permute-start.4 = (f32[256,256]{1,0:T(8,128)S(1)}, f32[256,256]{1,0:T(8,128)S(1)}, u32[]{:S(2)}, u32[]{:S(2)}) collective-permute-start(f32[256,256]{1,0:T(8,128)S(1)} %get-tuple-element.74), channel_id=1, source_target_pairs={{0,1},{2,3},{1,0},{3,2},{4,5},{6,7},{5,4},{7,6},{8,9},{10,11},{9,8... | collective-permute-start | bytes 786440 | tf_op jit(solution)/shard_map/ppermute | solution.py:701
  42.0 5.2 %shard_map.109 = (f32[32,256,128]{2,1,0:T(8,128)S(1)}, f32[2,32,8,128]{3,2,1,0:T(8,128)S(1)}, f32[32,1024]{1,0:T(8,128)S(1)}) custom-call(f32[32,256,128]{2,1,0:T(8,128)S(1)} %get-tuple-element.56.z, bf16[256,768]{1,0:T(8,128)(2,1)S(1)} %get-tuple-element.40.mix, bf16[256,256]{1,0:T(8,128)(2,1)S(1)} %get-tuple-element.41.band_cols, ...), custom_call_target="tpu_custom_call" | custom-call | flops 1000000000 | bytes 10000000 | tf_op jit(solution)/shard_map/pallas_call | solution.py:685
  47.2 0.0 collective-permute-done.5.second
  47.3 1.8 %collective-permute-done.4.first = f32[256,256]{1,0:T(8,128)S(1)} collective-permute-done((f32[256,256]{1,0:T(8,128)S(1)}, f32[256,256]{1,0:T(8,128)S(1)}, u32[]{:S(2)}, u32[]{:S(2)}) %collective-permute-start.4) | collective-permute-done | bytes 262176 | tf_op jit(solution)/shard_map/ppermute | solution.py:701
  49.1 0.8 %shard_map.110 = (f32[2,256,256]{2,1,0:T(8,128)S(1)}, f32[2,32,8,128]{3,2,1,0:T(8,128)S(1)}) custom-call(f32[256,256]{1,0:T(8,128)S(1)} %collective-permute-done.4.first, f32[256,256]{1,0:T(8,128)S(1)} %collective-permute-done.5.second, f32[2,32,8,128]{3,2,1,0:T(8,128)S(1)} %get-tuple-element.61.u_edges, bf16[4,256,256]{2,1,0:T(8,128)(2,1)S(1)} %get-tuple-element.45.mat, ...), custom_call_target="tpu_custom_call" | custom-call | flops 1000000000 | bytes 10000000 | tf_op jit(solution)/shard_map/pallas_call | solution.py:685
  50.0 0.7 collective-permute-start.7
  50.6 3.0 %collective-permute-start.6 = (f32[32,8,128]{2,1,0:T(8,128)S(1)}, f32[32,8,128]{2,1,0:T(8,128)S(1)}, u32[]{:S(2)}, u32[]{:S(2)}) collective-permute-start(f32[32,8,128]{2,1,0:T(8,128)S(1)} %get-tuple-element.78), channel_id=1, source_target_pairs={{0,4},{8,12},{16,20},{24,28},{4,0},{12,8},{20,16},{28,24},{1,5},{9... | collective-permute-start | bytes 393224 | tf_op jit(solution)/shard_map/ppermute | solution.py:701
  53.6 2.3 %shard_map.111.w = f32[32,256,128]{2,1,0:T(8,128)S(1)} custom-call(f32[32,256,128]{2,1,0:T(8,128)S(1)} %get-tuple-element.59.u, f32[2,256,256]{2,1,0:T(8,128)S(1)} %get-tuple-element.62.sides, bf16[256,768]{1,0:T(8,128)(2,1)S(1)} %get-tuple-element.46.band_rows), custom_call_target="tpu_custom_call" | custom-call | flops 1000000000 | bytes 10000000 | tf_op jit(solution)/shard_map/pallas_call | solution.py:685
  55.9 0.0 collective-permute-done.7.below
  55.9 0.0 collective-permute-done.6.above
  55.9 4.2 %shard_map.112 = (f32[32,256,128]{2,1,0:T(8,128)S(1)}, f32[32,128]{1,0:T(8,128)S(1)}) custom-call(f32[32,256,128]{2,1,0:T(8,128)S(1)} %shard_map.111.w, f32[32,8,128]{2,1,0:T(8,128)S(1)} %collective-permute-done.6.above, f32[32,8,128]{2,1,0:T(8,128)S(1)} %collective-permute-done.7.below, bf16[4,256,256]{2,1,0:T(8,128)(2,1)S(1)} %get-tuple-element.49.edge, ...), custom_call_target="tpu_custom_call" | custom-call | flops 1000000000 | bytes 10000000 | tf_op jit(solution)/shard_map/pallas_call | solution.py:685
  60.1 12.9 %all_to_all.11 = f32[32,1,128]{2,1,0:T(1,128)S(1)} all-to-all(f32[32,1,128]{2,1,0:T(1,128)S(1)} %bitcast.21), channel_id=1, replica_groups=mesh['row'=8,'col'=4] {'row','col'}, dimensions={0} | all-to-all | bytes 32768 | tf_op jit(solution)/shard_map/all_to_all | solution.py:820
  73.0 4.3 %shard_map.113 = (f32[32,256,128]{2,1,0:T(8,128)}, f32[32,256,128]{2,1,0:T(8,128)}, f32[32,1,1,1024]{3,2,1,0:T(1,128)}) custom-call(f32[32,128]{1,0:T(8,128)S(1)} %bitcast.20, f32[32,256,128]{2,1,0:T(8,128)S(1)} %get-tuple-element.50.b, f32[32,256,128]{2,1,0:T(8,128)S(1)} %get-tuple-element.64.p, f32[32,256,128]{2,1,0:T(8,128)S(1)} %get-tuple-element.67.q, ...), custom_call_target="tpu_custom_call" | custom-call | tf_op jit(solution)/shard_map/pallas_call | solution.py:821
  (4 shorter events, 0.1 us)
Async XLA Ops:
  0.6 15.2 %copy-start.1 = (f32[32,32]{1,0:T(8,128)S(1)}, f32[32,32]{1,0:T(8,128)}, u32[]{:S(2)}) copy-start(f32[32,32]{1,0:T(8,128)} %cov.1) | copy-start | bytes 12292
  9.2 11.2 %collective-permute-start.1 = (f32[256,256]{1,0:T(8,128)S(1)}, f32[256,256]{1,0:T(8,128)S(1)}, u32[]{:S(2)}, u32[]{:S(2)}) collective-permute-start(f32[256,256]{1,0:T(8,128)S(1)} %get-tuple-element.75), channel_id=1, source_target_pairs={{1,2},{2,1},{5,6},{6,5},{9,10},{10,9},{13,14},{14,13},{17,18},{18,... | collective-permute-start | bytes 786440 | tf_op jit(solution)/shard_map/ppermute | solution.py:701
  9.9 12.0 %collective-permute-start = (f32[256,256]{1,0:T(8,128)S(1)}, f32[256,256]{1,0:T(8,128)S(1)}, u32[]{:S(2)}, u32[]{:S(2)}) collective-permute-start(f32[256,256]{1,0:T(8,128)S(1)} %get-tuple-element.76), channel_id=1, source_target_pairs={{0,1},{2,3},{1,0},{3,2},{4,5},{6,7},{5,4},{7,6},{8,9},{10,11},{9,8... | collective-permute-start | bytes 786440 | tf_op jit(solution)/shard_map/ppermute | solution.py:701
  22.7 5.7 %collective-permute-start.3 = (f32[32,8,128]{2,1,0:T(8,128)S(1)}, f32[32,8,128]{2,1,0:T(8,128)S(1)}, u32[]{:S(2)}, u32[]{:S(2)}) collective-permute-start(f32[32,8,128]{2,1,0:T(8,128)S(1)} %get-tuple-element.79), channel_id=1, source_target_pairs={{4,8},{12,16},{20,24},{8,4},{16,12},{24,20},{5,9},{13,17},{21,25},... | collective-permute-start | bytes 393224 | tf_op jit(solution)/shard_map/ppermute | solution.py:701
  23.4 5.0 %collective-permute-start.2 = (f32[32,8,128]{2,1,0:T(8,128)S(1)}, f32[32,8,128]{2,1,0:T(8,128)S(1)}, u32[]{:S(2)}, u32[]{:S(2)}) collective-permute-start(f32[32,8,128]{2,1,0:T(8,128)S(1)} %get-tuple-element.80), channel_id=1, source_target_pairs={{0,4},{8,12},{16,20},{24,28},{4,0},{12,8},{20,16},{28,24},{1,5},{9... | collective-permute-start | bytes 393224 | tf_op jit(solution)/shard_map/ppermute | solution.py:701
  26.3 2.2 %copy-start = (f32[256,128]{1,0:T(8,128)S(1)}, f32[256,128]{1,0:T(8,128)}, u32[]{:S(2)}) copy-start(f32[256,128]{1,0:T(8,128)} %noise.3) | copy-start | bytes 393220
  37.9 9.3 %collective-permute-start.5 = (f32[256,256]{1,0:T(8,128)S(1)}, f32[256,256]{1,0:T(8,128)S(1)}, u32[]{:S(2)}, u32[]{:S(2)}) collective-permute-start(f32[256,256]{1,0:T(8,128)S(1)} %get-tuple-element.73), channel_id=1, source_target_pairs={{1,2},{2,1},{5,6},{6,5},{9,10},{10,9},{13,14},{14,13},{17,18},{18,... | collective-permute-start | bytes 786440 | tf_op jit(solution)/shard_map/ppermute | solution.py:701
  38.6 10.5 %collective-permute-start.4 = (f32[256,256]{1,0:T(8,128)S(1)}, f32[256,256]{1,0:T(8,128)S(1)}, u32[]{:S(2)}, u32[]{:S(2)}) collective-permute-start(f32[256,256]{1,0:T(8,128)S(1)} %get-tuple-element.74), channel_id=1, source_target_pairs={{0,1},{2,3},{1,0},{3,2},{4,5},{6,7},{5,4},{7,6},{8,9},{10,11},{9,8... | collective-permute-start | bytes 786440 | tf_op jit(solution)/shard_map/ppermute | solution.py:701
  50.0 5.9 %collective-permute-start.7 = (f32[32,8,128]{2,1,0:T(8,128)S(1)}, f32[32,8,128]{2,1,0:T(8,128)S(1)}, u32[]{:S(2)}, u32[]{:S(2)}) collective-permute-start(f32[32,8,128]{2,1,0:T(8,128)S(1)} %get-tuple-element.77), channel_id=1, source_target_pairs={{4,8},{12,16},{20,24},{8,4},{16,12},{24,20},{5,9},{13,17},{21,25},... | collective-permute-start | bytes 393224 | tf_op jit(solution)/shard_map/ppermute | solution.py:701
  50.6 5.3 %collective-permute-start.6 = (f32[32,8,128]{2,1,0:T(8,128)S(1)}, f32[32,8,128]{2,1,0:T(8,128)S(1)}, u32[]{:S(2)}, u32[]{:S(2)}) collective-permute-start(f32[32,8,128]{2,1,0:T(8,128)S(1)} %get-tuple-element.78), channel_id=1, source_target_pairs={{0,4},{8,12},{16,20},{24,28},{4,0},{12,8},{20,16},{28,24},{1,5},{9... | collective-permute-start | bytes 393224 | tf_op jit(solution)/shard_map/ppermute | solution.py:701

commit v8 on v7

--- a/solution.py
+++ b/solution.py
@@ -168,7 +168,7 @@
         )
         return carry
 
-    lax.fori_loop(0, tiles, sort_block, 0, unroll=2)
+    lax.fori_loop(0, tiles, sort_block, 0, unroll=8)
     ordered_row = sorted_rows[pl.ds(steps, 1), :]
     ordered_live = sorted_rows[pl.ds(steps + 5, 1), :]
     first_row = (iota((groups, slots), 0) * GROUP).astype(F32)
@@ -303,7 +303,7 @@
         pack_group(g, value, strips)
         return carry
 
-    lax.fori_loop(0, groups, run, 0, unroll=8)
+    lax.fori_loop(0, groups, run, 0, unroll=32)
 
     @pl.when(bounds[0, 2] > 1)
     def _():
@@ -363,7 +363,7 @@
                 ]
         return carry
 
-    lax.fori_loop(0, groups // 4, across, 0, unroll=4)
+    lax.fori_loop(0, groups // 4, across, 0, unroll=8)
 
     def mixing(two, carry):
         right = jnp.concatenate([y[two, 0], y[two, 1], y[two, 0]], axis=0)
@@ -372,7 +372,7 @@
         u[:, rows_of(2 * two + 1), :] = out[:, LANES:].reshape(steps, GROUP, LANES)
         return carry
 
-    lax.fori_loop(0, groups // 2, mixing, 0, unroll=8)
+    lax.fori_loop(0, groups // 2, mixing, 0, unroll=16)
     u_edges[0] = u[:, pl.ds(0, GROUP), :]
     u_edges[1] = u[:, pl.ds(rows - GROUP, GROUP), :]
 
@@ -390,7 +390,7 @@
         unsorted[:, lanes] = out[:steps] + out[steps : 2 * steps] + out[2 * steps :]
         return carry
 
-    lax.fori_loop(0, tiles, unsort_block, 0)
+    lax.fori_loop(0, tiles, unsort_block, 0, unroll=4)
 
 
 def second_filter_kernel(u, sides, band_rows, w):
@@ -407,7 +407,7 @@
         w[2 * two + 1] = out[:, LANES:] + unpack(sides, everything, rows, 2 * two + 1)
         return carry
 
-    lax.fori_loop(0, steps // 2, along, 0, unroll=8)
+    lax.fori_loop(0, steps // 2, along, 0, unroll=16)
 
 
 def edge_kernel(first, second, u_edges, mat, band_rows, sides, full_edges):
@@ -495,7 +495,7 @@
         return first, second, third
 
     zero = jnp.zeros((GROUP, LANES), F32)
-    carry = lax.fori_loop(0, groups, run, (zero,) * 3, unroll=2)
+    carry = lax.fori_loop(0, groups, run, (zero,) * 3, unroll=8)
 
     @pl.when(bounds[0, 2] > 1)
     def _():
@@ -583,7 +583,7 @@
         return first, second, third
 
     zero = jnp.zeros((GROUP, LANES), F32)
-    carry = lax.fori_loop(0, groups, run, (zero,) * 3, unroll=1)
+    carry = lax.fori_loop(0, groups, run, (zero,) * 3, unroll=4)
 
     first, second, third = carry
     own_shift = sums[0:1, 0:1]

time: 77.6 us -> 74 us (0.954)
  Pallas kernels: 41.6 us -> 35.2 us
  waiting for transfers between devices: 3.35 us -> 5.1 us
    pallas_call x9, Pallas kernels: 29.4 us -> 24.3 us  [call(): pl.pallas_call(kernel, out_shape=outs, in_specs=ins, out_specs=[VMEM] * l...]
    ppermute x8, waiting for transfers between devices: 3.35 us -> 5.1 us  [exchange(): lax.ppermute(both[place], axis, found + [(b, a) for a, b in found])]
    pallas_call x1, Pallas kernels: 7.86 us -> 6.57 us  [body(): pl.pallas_call(prepare_kernel, out_shape=[field, field, strips_shape, sta...]
  transfers between devices with their start and end apart: 8 -> 8, of which waited for: 2 -> 2; matrix products, arithmetic and copies ran while one was open for 0% -> 0% of each run, Pallas kernels for 18% -> 16%
where the time goes in v8:
time: 74 us; the launch traced here: 73.7 us
  Pallas kernels  35.2 us (48%)
  starting transfers between devices  18.4 us (25%)
  blocking collectives  13.2 us (18%)
  waiting for transfers between devices  5.1 us (7%)
  between operations  1.65 us (2%)
    pallas_call x9, Pallas kernels, call(): pl.pallas_call(kernel, out_shape=outs, in_specs=ins, out_specs=[VMEM] * l...  24.3 us
    ppermute x8, starting transfers between devices, exchange(): lax.ppermute(both[place], axis, found + [(b, a) for a, b in found])  18.4 us
    all_to_all x1, blocking collectives, body(): received = lax.all_to_all(message, ('row', 'col'), 0, 0, tiled=True)  13.2 us
    pallas_call x1, Pallas kernels, body(): pl.pallas_call(prepare_kernel, out_shape=[field, field, strips_shape, sta...  6.57 us
    ppermute x8, waiting for transfers between devices, exchange(): lax.ppermute(both[place], axis, found + [(b, a) for a, b in found])  5.1 us
    pallas_call x1, Pallas kernels, body(): pl.pallas_call(final_kernel, out_shape=[field, field, shape((steps, 1, 1,...  4.34 us
  transfers between devices with their start and end apart: 8, of which 2 were waited for; matrix products, arithmetic and copies ran while one was open for 0% of the time, Pallas kernels for 16%

profile of v8, /device:TPU:0, one launch (start us, length us, event | category | flops | bytes accessed | tf_op | source)
XLA Modules:
  0.0 73.7 jit_solution(10325246753669871426)
XLA Ops:
  0.6 0.0 copy-start.1
  1.3 6.6 %shard_map.103 = (f32[32,256,128]{2,1,0:T(8,128)S(1)}, f32[32,256,128]{2,1,0:T(8,128)S(1)}, f32[2,256,256]{2,1,0:T(8,128)S(1)}, f32[32,8,2176]{2,1,0:T(8,128)}, ...) custom-call(s32[1,1]{1,0:T(1,128)S(6)} %copy.12.count, ...), custom_call_target="tpu_custom_call" | custom-call | flops 1000000000 | bytes 10000000 | tf_op jit(solution)/shard_map/pallas_call | solution.py:726
  7.9 0.7 collective-permute-start.1
  8.6 5.9 %collective-permute-start = (f32[256,256]{1,0:T(8,128)S(1)}, f32[256,256]{1,0:T(8,128)S(1)}, u32[]{:S(2)}, u32[]{:S(2)}) collective-permute-start(f32[256,256]{1,0:T(8,128)S(1)} %get-tuple-element.76), channel_id=1, source_target_pairs={{0,1},{2,3},{1,0},{3,2},{4,5},{6,7},{5,4},{7,6},{8,9},{10,11},{9,8... | collective-permute-start | bytes 786440 | tf_op jit(solution)/shard_map/ppermute | solution.py:701
  14.5 0.0 copy-done.1
  14.5 1.0 %shard_map.104 = (bf16[256,768]{1,0:T(8,128)(2,1)S(1)}, bf16[4,256,256]{2,1,0:T(8,128)(2,1)S(1)}) custom-call(f32[32,32]{1,0:T(8,128)S(1)} %copy-done.1), custom_call_target="tpu_custom_call" | custom-call | flops 1000000000 | bytes 10000000 | tf_op jit(solution)/shard_map/pallas_call | solution.py:685
  15.5 3.0 %shard_map.105 = (f32[32,256,128]{2,1,0:T(8,128)S(1)}, f32[2,32,8,128]{3,2,1,0:T(8,128)S(1)}) custom-call(f32[32,256,128]{2,1,0:T(8,128)S(1)} %get-tuple-element.39.z.z_first, bf16[256,768]{1,0:T(8,128)(2,1)S(1)} %get-tuple-element.40.mix, bf16[256,256]{1,0:T(8,128)(2,1)S(1)} %get-tuple-element.41.band_cols), custom_call_target="tpu_custom_call" | custom-call | flops 1000000000 | bytes 10000000 | tf_op jit(solution)/shard_map/pallas_call | solution.py:685
  18.6 0.0 collective-permute-done.1.second
  18.6 2.0 %collective-permute-done.first = f32[256,256]{1,0:T(8,128)S(1)} collective-permute-done((f32[256,256]{1,0:T(8,128)S(1)}, f32[256,256]{1,0:T(8,128)S(1)}, u32[]{:S(2)}, u32[]{:S(2)}) %collective-permute-start) | collective-permute-done | bytes 262176 | tf_op jit(solution)/shard_map/ppermute | solution.py:701
  20.6 0.8 %shard_map.106 = (f32[2,256,256]{2,1,0:T(8,128)S(1)}, f32[2,32,8,128]{3,2,1,0:T(8,128)S(1)}) custom-call(f32[256,256]{1,0:T(8,128)S(1)} %collective-permute-done.first, f32[256,256]{1,0:T(8,128)S(1)} %collective-permute-done.1.second, f32[2,32,8,128]{3,2,1,0:T(8,128)S(1)} %get-tuple-element.44.u_edges, bf16[4,256,256]{2,1,0:T(8,128)(2,1)S(1)} %get-tuple-element.45.mat, ...), custom_call_target="tpu_custom_call" | custom-call | flops 1000000000 | bytes 10000000 | tf_op jit(solution)/shard_map/pallas_call | solution.py:685
  21.4 0.7 collective-permute-start.3
  22.1 2.9 %collective-permute-start.2 = (f32[32,8,128]{2,1,0:T(8,128)S(1)}, f32[32,8,128]{2,1,0:T(8,128)S(1)}, u32[]{:S(2)}, u32[]{:S(2)}) collective-permute-start(f32[32,8,128]{2,1,0:T(8,128)S(1)} %get-tuple-element.80), channel_id=1, source_target_pairs={{0,4},{8,12},{16,20},{24,28},{4,0},{12,8},{20,16},{28,24},{1,5},{9... | collective-permute-start | bytes 393224 | tf_op jit(solution)/shard_map/ppermute | solution.py:701
  25.0 0.0 copy-start
  25.0 1.8 %shard_map.107.w = f32[32,256,128]{2,1,0:T(8,128)S(1)} custom-call(f32[32,256,128]{2,1,0:T(8,128)S(1)} %get-tuple-element.42.u, f32[2,256,256]{2,1,0:T(8,128)S(1)} %get-tuple-element.47.sides, bf16[256,768]{1,0:T(8,128)(2,1)S(1)} %get-tuple-element.46.band_rows), custom_call_target="tpu_custom_call" | custom-call | flops 1000000000 | bytes 10000000 | tf_op jit(solution)/shard_map/pallas_call | solution.py:685
  26.9 0.0 collective-permute-done.3.below
  26.9 0.0 collective-permute-done.2.above
  26.9 0.0 copy-done
  26.9 7.3 %shard_map.108 = (f32[32,256,128]{2,1,0:T(8,128)S(1)}, f32[32,256,128]{2,1,0:T(8,128)S(1)}, f32[2,256,256]{2,1,0:T(8,128)S(1)}, f32[8,128]{1,0:T(8,128)S(1)}, f32[32,1024]{1,0:T(8,128)S(1)}) custom-call(s32[32,128]{1,0:T(8,128)S(1)} %get-tuple-element.38.bounds, f32[32,256,128]{2,1,0:T(8,128)S(1)} %shard_map.107.w, ...), custom_call_target="tpu_custom_call" | custom-call | flops 1000000000 | bytes 10000000 | tf_op jit(solution)/shard_map/pallas_call | solution.py:685
  34.3 0.7 collective-permute-start.5
  35.0 3.5 %collective-permute-start.4 = (f32[256,256]{1,0:T(8,128)S(1)}, f32[256,256]{1,0:T(8,128)S(1)}, u32[]{:S(2)}, u32[]{:S(2)}) collective-permute-start(f32[256,256]{1,0:T(8,128)S(1)} %get-tuple-element.74), channel_id=1, source_target_pairs={{0,1},{2,3},{1,0},{3,2},{4,5},{6,7},{5,4},{7,6},{8,9},{10,11},{9,8... | collective-permute-start | bytes 786440 | tf_op jit(solution)/shard_map/ppermute | solution.py:701
  38.5 3.8 %shard_map.109 = (f32[32,256,128]{2,1,0:T(8,128)S(1)}, f32[2,32,8,128]{3,2,1,0:T(8,128)S(1)}, f32[32,1024]{1,0:T(8,128)S(1)}) custom-call(f32[32,256,128]{2,1,0:T(8,128)S(1)} %get-tuple-element.56.z, bf16[256,768]{1,0:T(8,128)(2,1)S(1)} %get-tuple-element.40.mix, bf16[256,256]{1,0:T(8,128)(2,1)S(1)} %get-tuple-element.41.band_cols, ...), custom_call_target="tpu_custom_call" | custom-call | flops 1000000000 | bytes 10000000 | tf_op jit(solution)/shard_map/pallas_call | solution.py:685
  42.3 0.0 collective-permute-done.5.second
  42.3 3.1 %collective-permute-done.4.first = f32[256,256]{1,0:T(8,128)S(1)} collective-permute-done((f32[256,256]{1,0:T(8,128)S(1)}, f32[256,256]{1,0:T(8,128)S(1)}, u32[]{:S(2)}, u32[]{:S(2)}) %collective-permute-start.4) | collective-permute-done | bytes 262176 | tf_op jit(solution)/shard_map/ppermute | solution.py:701
  45.4 0.8 %shard_map.110 = (f32[2,256,256]{2,1,0:T(8,128)S(1)}, f32[2,32,8,128]{3,2,1,0:T(8,128)S(1)}) custom-call(f32[256,256]{1,0:T(8,128)S(1)} %collective-permute-done.4.first, f32[256,256]{1,0:T(8,128)S(1)} %collective-permute-done.5.second, f32[2,32,8,128]{3,2,1,0:T(8,128)S(1)} %get-tuple-element.61.u_edges, bf16[4,256,256]{2,1,0:T(8,128)(2,1)S(1)} %get-tuple-element.45.mat, ...), custom_call_target="tpu_custom_call" | custom-call | flops 1000000000 | bytes 10000000 | tf_op jit(solution)/shard_map/pallas_call | solution.py:685
  46.3 0.7 collective-permute-start.7
  47.0 3.4 %collective-permute-start.6 = (f32[32,8,128]{2,1,0:T(8,128)S(1)}, f32[32,8,128]{2,1,0:T(8,128)S(1)}, u32[]{:S(2)}, u32[]{:S(2)}) collective-permute-start(f32[32,8,128]{2,1,0:T(8,128)S(1)} %get-tuple-element.78), channel_id=1, source_target_pairs={{0,4},{8,12},{16,20},{24,28},{4,0},{12,8},{20,16},{28,24},{1,5},{9... | collective-permute-start | bytes 393224 | tf_op jit(solution)/shard_map/ppermute | solution.py:701
  50.4 2.1 %shard_map.111.w = f32[32,256,128]{2,1,0:T(8,128)S(1)} custom-call(f32[32,256,128]{2,1,0:T(8,128)S(1)} %get-tuple-element.59.u, f32[2,256,256]{2,1,0:T(8,128)S(1)} %get-tuple-element.62.sides, bf16[256,768]{1,0:T(8,128)(2,1)S(1)} %get-tuple-element.46.band_rows), custom_call_target="tpu_custom_call" | custom-call | flops 1000000000 | bytes 10000000 | tf_op jit(solution)/shard_map/pallas_call | solution.py:685
  52.5 0.0 collective-permute-done.7.below
  52.5 0.0 collective-permute-done.6.above
  52.5 3.5 %shard_map.112 = (f32[32,256,128]{2,1,0:T(8,128)S(1)}, f32[32,128]{1,0:T(8,128)S(1)}) custom-call(f32[32,256,128]{2,1,0:T(8,128)S(1)} %shard_map.111.w, f32[32,8,128]{2,1,0:T(8,128)S(1)} %collective-permute-done.6.above, f32[32,8,128]{2,1,0:T(8,128)S(1)} %collective-permute-done.7.below, bf16[4,256,256]{2,1,0:T(8,128)(2,1)S(1)} %get-tuple-element.49.edge, ...), custom_call_target="tpu_custom_call" | custom-call | flops 1000000000 | bytes 10000000 | tf_op jit(solution)/shard_map/pallas_call | solution.py:685
  56.0 13.2 %all_to_all.11 = f32[32,1,128]{2,1,0:T(1,128)S(1)} all-to-all(f32[32,1,128]{2,1,0:T(1,128)S(1)} %bitcast.21), channel_id=1, replica_groups=mesh['row'=8,'col'=4] {'row','col'}, dimensions={0} | all-to-all | bytes 32768 | tf_op jit(solution)/shard_map/all_to_all | solution.py:820
  69.2 4.3 %shard_map.113 = (f32[32,256,128]{2,1,0:T(8,128)}, f32[32,256,128]{2,1,0:T(8,128)}, f32[32,1,1,1024]{3,2,1,0:T(1,128)}) custom-call(f32[32,128]{1,0:T(8,128)S(1)} %bitcast.20, f32[32,256,128]{2,1,0:T(8,128)S(1)} %get-tuple-element.50.b, f32[32,256,128]{2,1,0:T(8,128)S(1)} %get-tuple-element.64.p, f32[32,256,128]{2,1,0:T(8,128)S(1)} %get-tuple-element.67.q, ...), custom_call_target="tpu_custom_call" | custom-call | tf_op jit(solution)/shard_map/pallas_call | solution.py:821
  (4 shorter events, 0.1 us)
Async XLA Ops:
  0.6 13.9 %copy-start.1 = (f32[32,32]{1,0:T(8,128)S(1)}, f32[32,32]{1,0:T(8,128)}, u32[]{:S(2)}) copy-start(f32[32,32]{1,0:T(8,128)} %cov.1) | copy-start | bytes 12292
  7.9 10.7 %collective-permute-start.1 = (f32[256,256]{1,0:T(8,128)S(1)}, f32[256,256]{1,0:T(8,128)S(1)}, u32[]{:S(2)}, u32[]{:S(2)}) collective-permute-start(f32[256,256]{1,0:T(8,128)S(1)} %get-tuple-element.75), channel_id=1, source_target_pairs={{1,2},{2,1},{5,6},{6,5},{9,10},{10,9},{13,14},{14,13},{17,18},{18,... | collective-permute-start | bytes 786440 | tf_op jit(solution)/shard_map/ppermute | solution.py:701
  8.6 12.0 %collective-permute-start = (f32[256,256]{1,0:T(8,128)S(1)}, f32[256,256]{1,0:T(8,128)S(1)}, u32[]{:S(2)}, u32[]{:S(2)}) collective-permute-start(f32[256,256]{1,0:T(8,128)S(1)} %get-tuple-element.76), channel_id=1, source_target_pairs={{0,1},{2,3},{1,0},{3,2},{4,5},{6,7},{5,4},{7,6},{8,9},{10,11},{9,8... | collective-permute-start | bytes 786440 | tf_op jit(solution)/shard_map/ppermute | solution.py:701
  21.4 5.4 %collective-permute-start.3 = (f32[32,8,128]{2,1,0:T(8,128)S(1)}, f32[32,8,128]{2,1,0:T(8,128)S(1)}, u32[]{:S(2)}, u32[]{:S(2)}) collective-permute-start(f32[32,8,128]{2,1,0:T(8,128)S(1)} %get-tuple-element.79), channel_id=1, source_target_pairs={{4,8},{12,16},{20,24},{8,4},{16,12},{24,20},{5,9},{13,17},{21,25},... | collective-permute-start | bytes 393224 | tf_op jit(solution)/shard_map/ppermute | solution.py:701
  22.1 4.8 %collective-permute-start.2 = (f32[32,8,128]{2,1,0:T(8,128)S(1)}, f32[32,8,128]{2,1,0:T(8,128)S(1)}, u32[]{:S(2)}, u32[]{:S(2)}) collective-permute-start(f32[32,8,128]{2,1,0:T(8,128)S(1)} %get-tuple-element.80), channel_id=1, source_target_pairs={{0,4},{8,12},{16,20},{24,28},{4,0},{12,8},{20,16},{28,24},{1,5},{9... | collective-permute-start | bytes 393224 | tf_op jit(solution)/shard_map/ppermute | solution.py:701
  25.0 1.9 %copy-start = (f32[256,128]{1,0:T(8,128)S(1)}, f32[256,128]{1,0:T(8,128)}, u32[]{:S(2)}) copy-start(f32[256,128]{1,0:T(8,128)} %noise.3) | copy-start | bytes 393220
  34.3 8.0 %collective-permute-start.5 = (f32[256,256]{1,0:T(8,128)S(1)}, f32[256,256]{1,0:T(8,128)S(1)}, u32[]{:S(2)}, u32[]{:S(2)}) collective-permute-start(f32[256,256]{1,0:T(8,128)S(1)} %get-tuple-element.73), channel_id=1, source_target_pairs={{1,2},{2,1},{5,6},{6,5},{9,10},{10,9},{13,14},{14,13},{17,18},{18,... | collective-permute-start | bytes 786440 | tf_op jit(solution)/shard_map/ppermute | solution.py:701
  35.0 10.4 %collective-permute-start.4 = (f32[256,256]{1,0:T(8,128)S(1)}, f32[256,256]{1,0:T(8,128)S(1)}, u32[]{:S(2)}, u32[]{:S(2)}) collective-permute-start(f32[256,256]{1,0:T(8,128)S(1)} %get-tuple-element.74), channel_id=1, source_target_pairs={{0,1},{2,3},{1,0},{3,2},{4,5},{6,7},{5,4},{7,6},{8,9},{10,11},{9,8... | collective-permute-start | bytes 786440 | tf_op jit(solution)/shard_map/ppermute | solution.py:701
  46.3 6.2 %collective-permute-start.7 = (f32[32,8,128]{2,1,0:T(8,128)S(1)}, f32[32,8,128]{2,1,0:T(8,128)S(1)}, u32[]{:S(2)}, u32[]{:S(2)}) collective-permute-start(f32[32,8,128]{2,1,0:T(8,128)S(1)} %get-tuple-element.77), channel_id=1, source_target_pairs={{4,8},{12,16},{20,24},{8,4},{16,12},{24,20},{5,9},{13,17},{21,25},... | collective-permute-start | bytes 393224 | tf_op jit(solution)/shard_map/ppermute | solution.py:701
  47.0 5.5 %collective-permute-start.6 = (f32[32,8,128]{2,1,0:T(8,128)S(1)}, f32[32,8,128]{2,1,0:T(8,128)S(1)}, u32[]{:S(2)}, u32[]{:S(2)}) collective-permute-start(f32[32,8,128]{2,1,0:T(8,128)S(1)} %get-tuple-element.78), channel_id=1, source_target_pairs={{0,4},{8,12},{16,20},{24,28},{4,0},{12,8},{20,16},{28,24},{1,5},{9... | collective-permute-start | bytes 393224 | tf_op jit(solution)/shard_map/ppermute | solution.py:701

commit v9 on v8

--- a/solution.py
+++ b/solution.py
@@ -390,7 +390,7 @@
         unsorted[:, lanes] = out[:steps] + out[steps : 2 * steps] + out[2 * steps :]
         return carry
 
-    lax.fori_loop(0, tiles, unsort_block, 0, unroll=4)
+    lax.fori_loop(0, tiles, unsort_block, 0, unroll=8)
 
 
 def second_filter_kernel(u, sides, band_rows, w):
@@ -495,7 +495,7 @@
         return first, second, third
 
     zero = jnp.zeros((GROUP, LANES), F32)
-    carry = lax.fori_loop(0, groups, run, (zero,) * 3, unroll=8)
+    carry = lax.fori_loop(0, groups, run, (zero,) * 3, unroll=16)
 
     @pl.when(bounds[0, 2] > 1)
     def _():
@@ -583,7 +583,7 @@
         return first, second, third
 
     zero = jnp.zeros((GROUP, LANES), F32)
-    carry = lax.fori_loop(0, groups, run, (zero,) * 3, unroll=4)
+    carry = lax.fori_loop(0, groups, run, (zero,) * 3, unroll=8)
 
     first, second, third = carry
     own_shift = sums[0:1, 0:1]

time: 74 us -> 73.6 us (level)
  no operation moved by 1% of the time
where the time goes in v9:
time: 73.6 us; the launch traced here: 73.4 us
  Pallas kernels  34.6 us (47%)
  starting transfers between devices  18.4 us (25%)
  blocking collectives  13.2 us (18%)
  waiting for transfers between devices  5.42 us (7%)
  between operations  1.65 us (2%)
    pallas_call x9, Pallas kernels, call(): pl.pallas_call(kernel, out_shape=outs, in_specs=ins, out_specs=[VMEM] * l...  23.7 us
    ppermute x8, starting transfers between devices, exchange(): lax.ppermute(both[place], axis, found + [(b, a) for a, b in found])  18.4 us
    all_to_all x1, blocking collectives, body(): received = lax.all_to_all(message, ('row', 'col'), 0, 0, tiled=True)  13.2 us
    pallas_call x1, Pallas kernels, body(): pl.pallas_call(prepare_kernel, out_shape=[field, field, strips_shape, sta...  6.57 us
    ppermute x8, waiting for transfers between devices, exchange(): lax.ppermute(both[place], axis, found + [(b, a) for a, b in found])  5.42 us
    pallas_call x1, Pallas kernels, body(): pl.pallas_call(final_kernel, out_shape=[field, field, shape((steps, 1, 1,...  4.34 us
  transfers between devices with their start and end apart: 8, of which 2 were waited for; matrix products, arithmetic and copies ran while one was open for 0% of the time, Pallas kernels for 16%

profile of v9, /device:TPU:0, one launch (start us, length us, event | category | flops | bytes accessed | tf_op | source)
XLA Modules:
  0.0 73.4 jit_solution(3823659050371464756)
XLA Ops:
  0.6 0.0 copy-start.1
  1.3 6.6 %shard_map.103 = (f32[32,256,128]{2,1,0:T(8,128)S(1)}, f32[32,256,128]{2,1,0:T(8,128)S(1)}, f32[2,256,256]{2,1,0:T(8,128)S(1)}, f32[32,8,2176]{2,1,0:T(8,128)}, ...) custom-call(s32[1,1]{1,0:T(1,128)S(6)} %copy.12.count, ...), custom_call_target="tpu_custom_call" | custom-call | flops 1000000000 | bytes 10000000 | tf_op jit(solution)/shard_map/pallas_call | solution.py:726
  7.9 0.7 collective-permute-start.1
  8.6 5.9 %collective-permute-start = (f32[256,256]{1,0:T(8,128)S(1)}, f32[256,256]{1,0:T(8,128)S(1)}, u32[]{:S(2)}, u32[]{:S(2)}) collective-permute-start(f32[256,256]{1,0:T(8,128)S(1)} %get-tuple-element.76), channel_id=1, source_target_pairs={{0,1},{2,3},{1,0},{3,2},{4,5},{6,7},{5,4},{7,6},{8,9},{10,11},{9,8... | collective-permute-start | bytes 786440 | tf_op jit(solution)/shard_map/ppermute | solution.py:701
  14.5 0.0 copy-done.1
  14.5 1.0 %shard_map.104 = (bf16[256,768]{1,0:T(8,128)(2,1)S(1)}, bf16[4,256,256]{2,1,0:T(8,128)(2,1)S(1)}) custom-call(f32[32,32]{1,0:T(8,128)S(1)} %copy-done.1), custom_call_target="tpu_custom_call" | custom-call | flops 1000000000 | bytes 10000000 | tf_op jit(solution)/shard_map/pallas_call | solution.py:685
  15.5 3.0 %shard_map.105 = (f32[32,256,128]{2,1,0:T(8,128)S(1)}, f32[2,32,8,128]{3,2,1,0:T(8,128)S(1)}) custom-call(f32[32,256,128]{2,1,0:T(8,128)S(1)} %get-tuple-element.39.z.z_first, bf16[256,768]{1,0:T(8,128)(2,1)S(1)} %get-tuple-element.40.mix, bf16[256,256]{1,0:T(8,128)(2,1)S(1)} %get-tuple-element.41.band_cols), custom_call_target="tpu_custom_call" | custom-call | flops 1000000000 | bytes 10000000 | tf_op jit(solution)/shard_map/pallas_call | solution.py:685
  18.6 0.0 collective-permute-done.1.second
  18.6 2.0 %collective-permute-done.first = f32[256,256]{1,0:T(8,128)S(1)} collective-permute-done((f32[256,256]{1,0:T(8,128)S(1)}, f32[256,256]{1,0:T(8,128)S(1)}, u32[]{:S(2)}, u32[]{:S(2)}) %collective-permute-start) | collective-permute-done | bytes 262176 | tf_op jit(solution)/shard_map/ppermute | solution.py:701
  20.6 0.8 %shard_map.106 = (f32[2,256,256]{2,1,0:T(8,128)S(1)}, f32[2,32,8,128]{3,2,1,0:T(8,128)S(1)}) custom-call(f32[256,256]{1,0:T(8,128)S(1)} %collective-permute-done.first, f32[256,256]{1,0:T(8,128)S(1)} %collective-permute-done.1.second, f32[2,32,8,128]{3,2,1,0:T(8,128)S(1)} %get-tuple-element.44.u_edges, bf16[4,256,256]{2,1,0:T(8,128)(2,1)S(1)} %get-tuple-element.45.mat, ...), custom_call_target="tpu_custom_call" | custom-call | flops 1000000000 | bytes 10000000 | tf_op jit(solution)/shard_map/pallas_call | solution.py:685
  21.4 0.7 collective-permute-start.3
  22.1 2.9 %collective-permute-start.2 = (f32[32,8,128]{2,1,0:T(8,128)S(1)}, f32[32,8,128]{2,1,0:T(8,128)S(1)}, u32[]{:S(2)}, u32[]{:S(2)}) collective-permute-start(f32[32,8,128]{2,1,0:T(8,128)S(1)} %get-tuple-element.80), channel_id=1, source_target_pairs={{0,4},{8,12},{16,20},{24,28},{4,0},{12,8},{20,16},{28,24},{1,5},{9... | collective-permute-start | bytes 393224 | tf_op jit(solution)/shard_map/ppermute | solution.py:701
  25.0 0.0 copy-start
  25.0 1.8 %shard_map.107.w = f32[32,256,128]{2,1,0:T(8,128)S(1)} custom-call(f32[32,256,128]{2,1,0:T(8,128)S(1)} %get-tuple-element.42.u, f32[2,256,256]{2,1,0:T(8,128)S(1)} %get-tuple-element.47.sides, bf16[256,768]{1,0:T(8,128)(2,1)S(1)} %get-tuple-element.46.band_rows), custom_call_target="tpu_custom_call" | custom-call | flops 1000000000 | bytes 10000000 | tf_op jit(solution)/shard_map/pallas_call | solution.py:685
  26.9 0.0 collective-permute-done.3.below
  26.9 0.0 collective-permute-done.2.above
  26.9 0.0 copy-done
  26.9 7.2 %shard_map.108 = (f32[32,256,128]{2,1,0:T(8,128)S(1)}, f32[32,256,128]{2,1,0:T(8,128)S(1)}, f32[2,256,256]{2,1,0:T(8,128)S(1)}, f32[8,128]{1,0:T(8,128)S(1)}, f32[32,1024]{1,0:T(8,128)S(1)}) custom-call(s32[32,128]{1,0:T(8,128)S(1)} %get-tuple-element.38.bounds, f32[32,256,128]{2,1,0:T(8,128)S(1)} %shard_map.107.w, ...), custom_call_target="tpu_custom_call" | custom-call | flops 1000000000 | bytes 10000000 | tf_op jit(solution)/shard_map/pallas_call | solution.py:685
  34.1 0.7 collective-permute-start.5
  34.8 3.4 %collective-permute-start.4 = (f32[256,256]{1,0:T(8,128)S(1)}, f32[256,256]{1,0:T(8,128)S(1)}, u32[]{:S(2)}, u32[]{:S(2)}) collective-permute-start(f32[256,256]{1,0:T(8,128)S(1)} %get-tuple-element.74), channel_id=1, source_target_pairs={{0,1},{2,3},{1,0},{3,2},{4,5},{6,7},{5,4},{7,6},{8,9},{10,11},{9,8... | collective-permute-start | bytes 786440 | tf_op jit(solution)/shard_map/ppermute | solution.py:701
  38.2 3.5 %shard_map.109 = (f32[32,256,128]{2,1,0:T(8,128)S(1)}, f32[2,32,8,128]{3,2,1,0:T(8,128)S(1)}, f32[32,1024]{1,0:T(8,128)S(1)}) custom-call(f32[32,256,128]{2,1,0:T(8,128)S(1)} %get-tuple-element.56.z, bf16[256,768]{1,0:T(8,128)(2,1)S(1)} %get-tuple-element.40.mix, bf16[256,256]{1,0:T(8,128)(2,1)S(1)} %get-tuple-element.41.band_cols, ...), custom_call_target="tpu_custom_call" | custom-call | flops 1000000000 | bytes 10000000 | tf_op jit(solution)/shard_map/pallas_call | solution.py:685
  41.7 0.0 collective-permute-done.5.second
  41.7 3.4 %collective-permute-done.4.first = f32[256,256]{1,0:T(8,128)S(1)} collective-permute-done((f32[256,256]{1,0:T(8,128)S(1)}, f32[256,256]{1,0:T(8,128)S(1)}, u32[]{:S(2)}, u32[]{:S(2)}) %collective-permute-start.4) | collective-permute-done | bytes 262176 | tf_op jit(solution)/shard_map/ppermute | solution.py:701
  45.2 0.8 %shard_map.110 = (f32[2,256,256]{2,1,0:T(8,128)S(1)}, f32[2,32,8,128]{3,2,1,0:T(8,128)S(1)}) custom-call(f32[256,256]{1,0:T(8,128)S(1)} %collective-permute-done.4.first, f32[256,256]{1,0:T(8,128)S(1)} %collective-permute-done.5.second, f32[2,32,8,128]{3,2,1,0:T(8,128)S(1)} %get-tuple-element.61.u_edges, bf16[4,256,256]{2,1,0:T(8,128)(2,1)S(1)} %get-tuple-element.45.mat, ...), custom_call_target="tpu_custom_call" | custom-call | flops 1000000000 | bytes 10000000 | tf_op jit(solution)/shard_map/pallas_call | solution.py:685
  46.1 0.7 collective-permute-start.7
  46.7 3.4 %collective-permute-start.6 = (f32[32,8,128]{2,1,0:T(8,128)S(1)}, f32[32,8,128]{2,1,0:T(8,128)S(1)}, u32[]{:S(2)}, u32[]{:S(2)}) collective-permute-start(f32[32,8,128]{2,1,0:T(8,128)S(1)} %get-tuple-element.78), channel_id=1, source_target_pairs={{0,4},{8,12},{16,20},{24,28},{4,0},{12,8},{20,16},{28,24},{1,5},{9... | collective-permute-start | bytes 393224 | tf_op jit(solution)/shard_map/ppermute | solution.py:701
  50.2 2.1 %shard_map.111.w = f32[32,256,128]{2,1,0:T(8,128)S(1)} custom-call(f32[32,256,128]{2,1,0:T(8,128)S(1)} %get-tuple-element.59.u, f32[2,256,256]{2,1,0:T(8,128)S(1)} %get-tuple-element.62.sides, bf16[256,768]{1,0:T(8,128)(2,1)S(1)} %get-tuple-element.46.band_rows), custom_call_target="tpu_custom_call" | custom-call | flops 1000000000 | bytes 10000000 | tf_op jit(solution)/shard_map/pallas_call | solution.py:685
  52.3 0.0 collective-permute-done.7.below
  52.3 0.0 collective-permute-done.6.above
  52.3 3.4 %shard_map.112 = (f32[32,256,128]{2,1,0:T(8,128)S(1)}, f32[32,128]{1,0:T(8,128)S(1)}) custom-call(f32[32,256,128]{2,1,0:T(8,128)S(1)} %shard_map.111.w, f32[32,8,128]{2,1,0:T(8,128)S(1)} %collective-permute-done.6.above, f32[32,8,128]{2,1,0:T(8,128)S(1)} %collective-permute-done.7.below, bf16[4,256,256]{2,1,0:T(8,128)(2,1)S(1)} %get-tuple-element.49.edge, ...), custom_call_target="tpu_custom_call" | custom-call | flops 1000000000 | bytes 10000000 | tf_op jit(solution)/shard_map/pallas_call | solution.py:685
  55.7 13.2 %all_to_all.11 = f32[32,1,128]{2,1,0:T(1,128)S(1)} all-to-all(f32[32,1,128]{2,1,0:T(1,128)S(1)} %bitcast.21), channel_id=1, replica_groups=mesh['row'=8,'col'=4] {'row','col'}, dimensions={0} | all-to-all | bytes 32768 | tf_op jit(solution)/shard_map/all_to_all | solution.py:820
  68.9 4.3 %shard_map.113 = (f32[32,256,128]{2,1,0:T(8,128)}, f32[32,256,128]{2,1,0:T(8,128)}, f32[32,1,1,1024]{3,2,1,0:T(1,128)}) custom-call(f32[32,128]{1,0:T(8,128)S(1)} %bitcast.20, f32[32,256,128]{2,1,0:T(8,128)S(1)} %get-tuple-element.50.b, f32[32,256,128]{2,1,0:T(8,128)S(1)} %get-tuple-element.64.p, f32[32,256,128]{2,1,0:T(8,128)S(1)} %get-tuple-element.67.q, ...), custom_call_target="tpu_custom_call" | custom-call | tf_op jit(solution)/shard_map/pallas_call | solution.py:821
  (4 shorter events, 0.1 us)
Async XLA Ops:
  0.6 13.9 %copy-start.1 = (f32[32,32]{1,0:T(8,128)S(1)}, f32[32,32]{1,0:T(8,128)}, u32[]{:S(2)}) copy-start(f32[32,32]{1,0:T(8,128)} %cov.1) | copy-start | bytes 12292
  7.9 10.7 %collective-permute-start.1 = (f32[256,256]{1,0:T(8,128)S(1)}, f32[256,256]{1,0:T(8,128)S(1)}, u32[]{:S(2)}, u32[]{:S(2)}) collective-permute-start(f32[256,256]{1,0:T(8,128)S(1)} %get-tuple-element.75), channel_id=1, source_target_pairs={{1,2},{2,1},{5,6},{6,5},{9,10},{10,9},{13,14},{14,13},{17,18},{18,... | collective-permute-start | bytes 786440 | tf_op jit(solution)/shard_map/ppermute | solution.py:701
  8.6 12.0 %collective-permute-start = (f32[256,256]{1,0:T(8,128)S(1)}, f32[256,256]{1,0:T(8,128)S(1)}, u32[]{:S(2)}, u32[]{:S(2)}) collective-permute-start(f32[256,256]{1,0:T(8,128)S(1)} %get-tuple-element.76), channel_id=1, source_target_pairs={{0,1},{2,3},{1,0},{3,2},{4,5},{6,7},{5,4},{7,6},{8,9},{10,11},{9,8... | collective-permute-start | bytes 786440 | tf_op jit(solution)/shard_map/ppermute | solution.py:701
  21.4 5.4 %collective-permute-start.3 = (f32[32,8,128]{2,1,0:T(8,128)S(1)}, f32[32,8,128]{2,1,0:T(8,128)S(1)}, u32[]{:S(2)}, u32[]{:S(2)}) collective-permute-start(f32[32,8,128]{2,1,0:T(8,128)S(1)} %get-tuple-element.79), channel_id=1, source_target_pairs={{4,8},{12,16},{20,24},{8,4},{16,12},{24,20},{5,9},{13,17},{21,25},... | collective-permute-start | bytes 393224 | tf_op jit(solution)/shard_map/ppermute | solution.py:701
  22.1 4.8 %collective-permute-start.2 = (f32[32,8,128]{2,1,0:T(8,128)S(1)}, f32[32,8,128]{2,1,0:T(8,128)S(1)}, u32[]{:S(2)}, u32[]{:S(2)}) collective-permute-start(f32[32,8,128]{2,1,0:T(8,128)S(1)} %get-tuple-element.80), channel_id=1, source_target_pairs={{0,4},{8,12},{16,20},{24,28},{4,0},{12,8},{20,16},{28,24},{1,5},{9... | collective-permute-start | bytes 393224 | tf_op jit(solution)/shard_map/ppermute | solution.py:701
  25.0 1.9 %copy-start = (f32[256,128]{1,0:T(8,128)S(1)}, f32[256,128]{1,0:T(8,128)}, u32[]{:S(2)}) copy-start(f32[256,128]{1,0:T(8,128)} %noise.3) | copy-start | bytes 393220
  34.1 7.6 %collective-permute-start.5 = (f32[256,256]{1,0:T(8,128)S(1)}, f32[256,256]{1,0:T(8,128)S(1)}, u32[]{:S(2)}, u32[]{:S(2)}) collective-permute-start(f32[256,256]{1,0:T(8,128)S(1)} %get-tuple-element.73), channel_id=1, source_target_pairs={{1,2},{2,1},{5,6},{6,5},{9,10},{10,9},{13,14},{14,13},{17,18},{18,... | collective-permute-start | bytes 786440 | tf_op jit(solution)/shard_map/ppermute | solution.py:701
  34.8 10.4 %collective-permute-start.4 = (f32[256,256]{1,0:T(8,128)S(1)}, f32[256,256]{1,0:T(8,128)S(1)}, u32[]{:S(2)}, u32[]{:S(2)}) collective-permute-start(f32[256,256]{1,0:T(8,128)S(1)} %get-tuple-element.74), channel_id=1, source_target_pairs={{0,1},{2,3},{1,0},{3,2},{4,5},{6,7},{5,4},{7,6},{8,9},{10,11},{9,8... | collective-permute-start | bytes 786440 | tf_op jit(solution)/shard_map/ppermute | solution.py:701
  46.1 6.2 %collective-permute-start.7 = (f32[32,8,128]{2,1,0:T(8,128)S(1)}, f32[32,8,128]{2,1,0:T(8,128)S(1)}, u32[]{:S(2)}, u32[]{:S(2)}) collective-permute-start(f32[32,8,128]{2,1,0:T(8,128)S(1)} %get-tuple-element.77), channel_id=1, source_target_pairs={{4,8},{12,16},{20,24},{8,4},{16,12},{24,20},{5,9},{13,17},{21,25},... | collective-permute-start | bytes 393224 | tf_op jit(solution)/shard_map/ppermute | solution.py:701
  46.7 5.5 %collective-permute-start.6 = (f32[32,8,128]{2,1,0:T(8,128)S(1)}, f32[32,8,128]{2,1,0:T(8,128)S(1)}, u32[]{:S(2)}, u32[]{:S(2)}) collective-permute-start(f32[32,8,128]{2,1,0:T(8,128)S(1)} %get-tuple-element.78), channel_id=1, source_target_pairs={{0,4},{8,12},{16,20},{24,28},{4,0},{12,8},{20,16},{28,24},{1,5},{9... | collective-permute-start | bytes 393224 | tf_op jit(solution)/shard_map/ppermute | solution.py:701
